TPU v7x, 32 devices: a whole 2x2x4 slice. The times are simulated.
32 devices in a mesh: tile: 16 (over z, y, core), samp: 2 (over x).
Axes of the slice: x: 2, y: 2, z: 4, core: 2. Of those that a mesh axis runs over, the one named last changes fastest.
Arguments:
- bathymetry: float32 [6, 512, 512], P(None, 'tile'), may hold values from 0.5 to 2
- initial_state: float32 [16, 6, 512, 512], P(None, None, 'tile'), may hold values from -6 to 6
- patterns: bfloat16 [4, 6, 512, 512], P(None, None, 'tile'), may hold values from -6 to 6
- pattern_index: int32 [2, 16], P('samp'), may hold values from 0 to 3
- coupling: float32 [16, 16], replicated, may hold values from -1.5 to 1.5
- final_weights: float32 [2, 16, 6, 512, 512], P('samp', None, None, 'tile'), may hold values from -6 to 6
Outputs:
- gradient: float32 [6, 512, 512], P(None, 'tile')
All inputs are finite; a program needn't handle non-finite values.
Results may differ from a plain program's by a relative error of at most 0.0003.
Values sent between devices are 32-bit elements; how exact they have to be, the bound alone decides.
No kernel may reach another device: no remote copies, remote signals or barrier semaphores. Data moves between devices by JAX's collectives and lax.ppermute only.
A program may use at most 128 MiB of HBM per device.

v0:
```python
import functools

import jax
import jax.numpy as jnp
from jax import lax
from jax.experimental import pallas as pl
from jax.experimental.pallas import tpu as pltpu
from jax.sharding import PartitionSpec as P

STEP_FACTOR = 0.1
LANES = 128
CH = 40
F32 = jnp.float32


def lane_iota(shape):
    return lax.broadcasted_iota(jnp.int32, shape, len(shape) - 1)


def lane_gather(x, idx):
    return jnp.take_along_axis(x, idx, axis=1, mode="promise_in_bounds")


def mix(cat, x):
    hi = x.astype(jnp.bfloat16)
    lo = (x - hi.astype(F32)).astype(jnp.bfloat16)
    return jnp.dot(cat, jnp.concatenate([hi, hi, lo], axis=0), preferred_element_type=F32)


STRIDED = True


def layer_rows(ref, r):
    size, rows = ref.shape[0], ref.shape[2]
    if not STRIDED:
        return ref[:, 0, r, :]
    return ref.reshape(size * rows, LANES)[pl.ds(r, size, stride=rows), :]


def pack_kernel(tiles, s_ref, w_ref, pat_ref, b_ref, em_ref, lo_ref, hi_ref, mm_ref, aa_ref, aux):
    layers, rows = s_ref.shape[0], s_ref.shape[2]
    p, block, blocks = pl.program_id(0), pl.program_id(1), pl.num_programs(1)
    place = lax.axis_index("tile")
    first, final = place == 0, place == tiles - 1
    npat = pat_ref.shape[0]
    aux[...] = jnp.zeros(aux.shape, F32)
    aux[0:npat, 0] = pat_ref[:, 0].astype(F32)
    aux[npat, 0] = b_ref[0]
    groups = ((0, layers, s_ref), (layers, layers, w_ref), (2 * layers, 8, aux))

    for at, size, ref in groups:
        for c in range(2):
            lo_ref[0, c, at : at + size, :] = layer_rows(ref, c)
            hi_ref[0, c, at : at + size, :] = layer_rows(ref, rows - 2 + c)

    lane = lane_iota((CH, LANES))
    side = lane % 4

    @pl.when((p == 0) & (block == 0))
    def _():
        aa_ref[...] = jnp.zeros(aa_ref.shape, F32)

    @pl.when(block == 0)
    def _():
        em_ref[...] = jnp.zeros(em_ref.shape, F32)

    for mine, at_block in (((0, 1), blocks - 1), ((2, 3), 0)):
        @pl.when(block == at_block)
        def _(mine=mine):
            for at, size, ref in groups:
                ln = lane_iota((size, LANES))
                keep = (ln % 4 == mine[0]) | (ln % 4 == mine[1])
                out = jnp.zeros((size, LANES), F32)
                for r in range(rows):
                    turned = pltpu.roll(layer_rows(ref, r), (4 * r - 126) % LANES, 1)
                    out = jnp.where(ln // 4 == r, turned, out)
                em_ref[0, at : at + size, :] = jnp.where(keep, out, em_ref[0, at : at + size, :])

    @pl.when(block == blocks - 1)
    def _():
        @pl.when(p == 1)
        def _():
            aa_ref[tiles - 1, 0:CH, :] = em_ref[0]
            mm_ref[2] = em_ref[0]

        @pl.when(p == 2)
        def _():
            mm_ref[0] = em_ref[0]

        @pl.when(p == 3)
        def _():
            aa_ref[0, 0:CH, :] = em_ref[0]

        @pl.when((p == 3) & jnp.logical_not(first))
        def _():
            mm_ref[2] = em_ref[0]

        @pl.when(p == 4)
        def _():
            mm_ref[1] = em_ref[0]

        @pl.when(p == 5)
        def _():
            mm_ref[1] = jnp.where(side < 2, mm_ref[1], em_ref[0])

    per = LANES // rows

    def pole(ref, near, far, backward, is_five):
        x, y = ref[0, near], ref[0, far]
        turned = jnp.concatenate([x, jnp.zeros((LANES - CH, LANES), F32)], axis=0).T
        for q in range(per):
            if backward:
                t = (blocks - 1 - block) * per + q
                idx = LANES - 1 - q * rows - lane // 4
            else:
                t = block * per + q
                idx = q * rows + lane // 4
            idx = jnp.clip(idx, 0, LANES - 1)
            a, b = lane_gather(x, idx), lane_gather(y, idx)
            if is_five:
                aa_ref[t, 0:CH, :] = jnp.where(side == 1, a, jnp.where(side == 0, b, aa_ref[t, 0:CH, :]))
            else:
                aa_ref[t, 0:CH, :] = jnp.where(side == 2, a, b)
            low, high = q * rows, (q + 1) * rows - 1
            if backward:
                before, at_before = tiles - block * per - q, low
                after, at_after = tiles - 1 - block * per - (q + 1), high
            else:
                before, at_before = block * per + q + 1, high
                after, at_after = block * per + q - 1, low
            m = 0 if is_five else 1

            @pl.when(before < tiles)
            def _(before=before, at=at_before):
                aa_ref[before, CH + m : CH + m + 1, :] = turned[at : at + 1, :]

            @pl.when(after >= 0)
            def _(after=after, at=at_after):
                aa_ref[after, CH + m + 2 : CH + m + 3, :] = turned[at : at + 1, :]

    for panel in (4, 5):
        @pl.when((p == panel) & first)
        def _(panel=panel):
            pole(lo_ref, 0, 1, panel == 4, panel == 5)

        @pl.when((p == panel) & final)
        def _(panel=panel):
            pole(hi_ref, 1, 0, panel == 5, panel == 5)


def pack(tiles, s, w, pat, b):
    layers, panels, rows, n = s.shape
    npat = pat.shape[0]
    full = lambda *shape: pl.BlockSpec(shape, lambda p, c: (0,) * len(shape))
    part = lambda size: pl.BlockSpec((size, 1, rows, LANES), lambda p, c: (0, p, 0, c))
    line = pl.BlockSpec((1, 2, CH, LANES), lambda p, c: (p, 0, 0, c))
    return pl.pallas_call(
        functools.partial(pack_kernel, tiles),
        grid=(panels, n // LANES),
        in_specs=[part(layers), part(layers), part(npat), pl.BlockSpec((1, rows, LANES), lambda p, c: (p, 0, c))],
        out_specs=[
            pl.BlockSpec((1, CH, LANES), lambda p, c: (p, 0, 0)),
            line,
            line,
            full(3, CH, LANES),
            full(tiles, CH + 8, LANES),
        ],
        out_shape=[
            jax.ShapeDtypeStruct((panels, CH, LANES), F32),
            jax.ShapeDtypeStruct((panels, 2, CH, n), F32),
            jax.ShapeDtypeStruct((panels, 2, CH, n), F32),
            jax.ShapeDtypeStruct((3, CH, LANES), F32),
            jax.ShapeDtypeStruct((tiles, CH + 8, LANES), F32),
        ],
        scratch_shapes=[pltpu.VMEM((8, 1, rows, LANES), F32)],
        compiler_params=pltpu.CompilerParams(vmem_limit_bytes=48 * 1024 * 1024),
        name="pack",
    )(s, w, pat, b)


def mix_kernel(s_ref, w_ref, pat_ref, fwd_ref, bwd_ref, sel_ref, p_ref, v_ref, y_ref, pf):
    rows = s_ref.shape[2]
    npat = pat_ref.shape[0]
    pf[...] = jnp.zeros(pf.shape, F32)
    pf[0:npat, 0] = pat_ref[:, 0].astype(F32)
    fwd, bwd, sel = fwd_ref[...], bwd_ref[...], sel_ref[...]
    for r in range(rows):
        s = layer_rows(s_ref, r)
        p_ref[0, r] = mix(fwd, s)
        v_ref[0, r] = mix(bwd, layer_rows(w_ref, r))
        f = jnp.dot(sel, layer_rows(pf, r).astype(jnp.bfloat16), preferred_element_type=F32)
        y_ref[0, r] = 3.0 * s + STEP_FACTOR * f


def mix_all(s, w, pat, fwd, bwd, sel):
    layers, panels, rows, n = s.shape
    npat = pat.shape[0]
    full = lambda x: pl.BlockSpec(x.shape, lambda p, c: (0,) * x.ndim)
    part = lambda size: pl.BlockSpec((size, 1, rows, LANES), lambda p, c: (0, p, 0, c))
    out = pl.BlockSpec((1, rows, layers, LANES), lambda p, c: (p, 0, 0, c))
    size = layers * panels * rows * n * 4
    return pl.pallas_call(
        mix_kernel,
        grid=(panels, n // LANES),
        in_specs=[part(layers), part(layers), part(npat), full(fwd), full(bwd), full(sel)],
        out_specs=[out] * 3,
        out_shape=[jax.ShapeDtypeStruct((panels, rows, layers, n), F32)] * 3,
        scratch_shapes=[pltpu.VMEM((8, 1, rows, LANES), F32)],
        compiler_params=pltpu.CompilerParams(vmem_limit_bytes=48 * 1024 * 1024),
        cost_estimate=pl.CostEstimate(flops=size * 48, bytes_accessed=5 * size, transcendentals=0),
        name="mix",
    )(s, w, pat, fwd, bwd, sel)


def halo_kernel(
    tiles, layers, rows,
    west_ref, east_ref, em_ref, mm_ref, mu_ref, md_ref, aa_ref, fwd_ref, bwd_ref, sel_ref,
    hrp_ref, hrv_ref, hry_ref, hrb_ref, hlp_ref, hlv_ref, hly_ref, hlb_ref, hcp_ref, hcv_ref, hcb_ref,
    line,
):
    panels, n = west_ref.shape[0], west_ref.shape[3]
    place = lax.axis_index("tile")
    first, final = place == 0, place == tiles - 1
    fwd, bwd, sel = fwd_ref[...], bwd_ref[...], sel_ref[...]
    lane = lane_iota((CH, LANES))
    side = lane % 4
    blocks = n // LANES
    per = LANES // rows

    for p in range(panels):
        @pl.when(jnp.logical_not(first))
        def _(p=p):
            line[p, 0:2] = west_ref[p]

        @pl.when(jnp.logical_not(final))
        def _(p=p):
            line[p, 2:4] = east_ref[p]

        if p < 4:
            @pl.when(first)
            def _(p=p):
                line[p, 0:2] = west_ref[(p + 3) % 4]

            @pl.when(final)
            def _(p=p):
                line[p, 2:4] = east_ref[(p + 1) % 4]

    def collect(u_of, dest, k, backward):
        within = lane % rows
        idx = 4 * (rows - 1 - within) + k if backward else 4 * within + k
        p, at = dest
        for block in range(blocks):
            out = jnp.zeros((CH, LANES), F32)
            for q in range(per):
                u = block * per + q
                u = tiles - 1 - u if backward else u
                out = jnp.where(lane // rows == q, lane_gather(u_of(u), idx), out)
            line[p, at, :, block * LANES : (block + 1) * LANES] = out

    @pl.when(first)
    def _():
        def of(u):
            return em_ref[3] if u == 0 else mm_ref[2] if u == tiles - 1 else aa_ref[u, 0:CH, :]

        collect(of, (4, 1), 1, True)
        collect(of, (4, 0), 0, True)
        collect(of, (5, 1), 2, False)
        collect(of, (5, 0), 3, False)

    @pl.when(final)
    def _():
        def of(u):
            return mm_ref[2] if u == 0 else em_ref[1] if u == tiles - 1 else aa_ref[u, 0:CH, :]

        collect(of, (4, 2), 1, False)
        collect(of, (4, 3), 0, False)
        collect(of, (5, 2), 2, True)
        collect(of, (5, 3), 3, True)

    def force(x):
        return 3.0 * x[0:layers] + STEP_FACTOR * jnp.dot(
            sel, x[2 * layers : CH].astype(jnp.bfloat16), preferred_element_type=F32
        )

    for p in range(panels):
        for k in range(4):
            x = line[p, k]
            hrp_ref[p, k] = mix(fwd, x[0:layers])
            hrv_ref[p, k] = mix(bwd, x[layers : 2 * layers])
            hrb_ref[p, k : k + 1, :] = line[p, k, CH - 4 : CH - 3, :]
            if k in (1, 2):
                hry_ref[p, k - 1] = force(x)

    span = 4 * rows
    turn = jnp.where(lane < span, span - 1 - lane, 0)
    back0 = lane_gather(mm_ref[0], turn)
    back1 = lane_gather(mm_ref[1], turn)
    columns = (
        jnp.where(side < 2, em_ref[5], em_ref[4]),
        aa_ref[tiles - 1, 0:CH, :],
        back1,
        aa_ref[0, 0:CH, :],
        jnp.where(side < 2, em_ref[0], back0),
        jnp.where(side < 2, back0, em_ref[0]),
    )
    at_end = lane == LANES - 1
    pad = jnp.zeros((LANES - 8, LANES), F32)
    for p in range(panels):
        x = columns[p]
        hlp_ref[p] = mix(fwd, x[0:layers])
        hlv_ref[p] = mix(bwd, x[layers : 2 * layers])
        hly_ref[p] = force(x)
        depth = x[CH - 4 : CH - 3]
        hlb_ref[p] = jnp.broadcast_to(depth, (8, LANES))
        if p in (1, 3):
            turned = jnp.concatenate([aa_ref[tiles - 1 if p == 1 else 0, CH:, :], pad], axis=0).T[0:CH]
        for edge in range(2):
            at = 1 + edge
            at_cut = lambda q, block: line[q, at, :, block * LANES : (block + 1) * LANES]
            cells = (1, 2) if edge == 0 else (4 * (rows - 1) + 1, 4 * (rows - 1) + 2)
            pick = jnp.where(at_end, cells[1], cells[0])
            other = mu_ref if edge == 0 else md_ref
            if p == 0:
                inner = jnp.where(at_end, at_cut(5, blocks - 1), at_cut(4, 0))
            elif p == 2:
                inner = lane_gather(other[1], pick)
            elif p == 4:
                inner = jnp.where(at_end, at_cut(0, blocks - 1), lane_gather(other[0], pick))
            elif p == 5:
                inner = jnp.where(at_end, lane_gather(other[0], pick), at_cut(0, 0))
            else:
                inner = lane_gather(turned, jnp.where(at_end, 2 * edge, 2 * edge + 1))
            own_row = 0 if edge == 0 else rows - 1
            across = pltpu.roll(x, (126 - 4 * own_row) % LANES, 1)
            along = jnp.where(
                at_end, pltpu.roll(at_cut(p, 0), LANES - 1, 1), pltpu.roll(at_cut(p, blocks - 1), 1, 1)
            )
            corner = first if edge == 0 else final
            for version, own in ((0, across), (1, along)):
                value = jnp.where(corner, own, inner)
                slot = 2 * edge + version
                hcp_ref[p, slot] = mix(fwd, value[0:layers])
                hcv_ref[p, slot] = mix(bwd, value[layers : 2 * layers])
                hcb_ref[p, slot] = jnp.broadcast_to(value[CH - 4 : CH - 3], (8, LANES))


def halos(tiles, layers, rows, west, east, em, mm, mu, md, aa, fwd, bwd, sel):
    panels, n = west.shape[0], west.shape[3]
    shapes = [
        (panels, 4, layers, n), (panels, 4, layers, n), (panels, 2, layers, n), (panels, 8, n),
        (panels, layers, LANES), (panels, layers, LANES), (panels, layers, LANES), (panels, 8, LANES),
        (panels, 4, layers, LANES), (panels, 4, layers, LANES), (panels, 4, 8, LANES),
    ]
    return pl.pallas_call(
        functools.partial(halo_kernel, tiles, layers, rows),
        out_shape=[jax.ShapeDtypeStruct(s, F32) for s in shapes],
        scratch_shapes=[pltpu.VMEM((panels, 4, CH, n), F32)],
        compiler_params=pltpu.CompilerParams(vmem_limit_bytes=48 * 1024 * 1024),
        name="halos",
    )(west, east, em, mm, mu, md, aa, fwd, bwd, sel)


def main_kernel(
    layers, scale,
    p_ref, v_ref, y_ref, b_ref,
    hrp, hrv, hry, hrb, hlp, hlv, hly, hlb, hcp, hcv, hcb,
    g_ref,
    sp, sv, sy, sz, bi, bj, acc,
):
    rows, n = p_ref.shape[1], p_ref.shape[3]
    wide = n + LANES
    halves = layers // 8
    for src, row_src, col_src, cor_src, dst in (
        (p_ref, hrp, hlp, hcp, sp),
        (v_ref, hrv, hlv, hcv, sv),
    ):
        zero = jnp.zeros((layers, LANES), F32)
        for k, (slot, tail) in enumerate(
            ((0, zero), (1, cor_src[0, 1]), (rows + 2, cor_src[0, 3]), (rows + 3, zero))
        ):
            dst[slot, :, 0:n] = row_src[0, k]
            dst[slot, :, n:wide] = tail
        for k, slot, corner in ((1, rows + 4, 0), (2, rows + 5, 2)):
            dst[slot, :, 0:n] = row_src[0, k]
            dst[slot, :, n:wide] = cor_src[0, corner]

    def tail_of(ref, r):
        return pltpu.roll(ref[0], lax.rem(126 - 4 * r + 4 * LANES, LANES), 1)

    def fill(r, carry):
        sp[r + 2, :, 0:n] = p_ref[0, r]
        sp[r + 2, :, n:wide] = tail_of(hlp, r)
        sv[r + 2, :, 0:n] = v_ref[0, r]
        sv[r + 2, :, n:wide] = tail_of(hlv, r)
        return carry

    lax.fori_loop(0, rows, fill, 0, unroll=2)

    half_step = 0.5 * STEP_FACTOR

    def depth_row(r):
        return jnp.concatenate(
            [jnp.broadcast_to(b_ref[0, pl.ds(r, 1), :], (8, n)), tail_of(hlb, r)], axis=1
        )

    def depth_halo(k, tail):
        return jnp.concatenate([jnp.broadcast_to(hrb[0, k : k + 1, :], (8, n)), tail], axis=1)

    def shift_next(x):
        return pltpu.roll(x, wide - 1, 1)

    def shift_back(x):
        return pltpu.roll(x, 1, 1)

    zero = jnp.zeros((8, LANES), F32)
    d_m2, d_m1 = depth_halo(0, zero), depth_halo(1, hcb[0, 1])
    d_p0, d_p1 = depth_halo(2, hcb[0, 3]), depth_halo(3, zero)
    j_m1, j_p0 = depth_halo(1, hcb[0, 0]), depth_halo(2, hcb[0, 2])
    bi[0] = half_step * (d_m2 + d_m1)
    bi[1] = half_step * (d_m1 + depth_row(0))
    bi[rows + 1] = half_step * (depth_row(rows - 1) + d_p0)
    bi[rows + 2] = half_step * (d_p0 + d_p1)
    bj[0] = half_step * (j_m1 + shift_next(j_m1))
    bj[rows + 1] = half_step * (j_p0 + shift_next(j_p0))

    def fill_depth(r, here):
        bj[r + 1] = half_step * (here + shift_next(here))
        after = depth_row(jnp.minimum(r + 1, rows - 1))

        @pl.when(r + 1 < rows)
        def _():
            bi[r + 2] = half_step * (here + after)

        return after

    lax.fori_loop(0, rows, fill_depth, depth_row(0))

    def outflow(ref, h, at, flat, out):
        part = slice(8 * h, 8 * h + 8)
        here = ref[at, part]
        before = bi[out - 1 + 0] * (here - ref[at - 1, part])
        after = bi[out] * (ref[at + 1, part] - here)
        line = here if flat is None else ref[flat, part]
        along = bj[out - 1] * (shift_next(line) - line)
        return after - before + along - shift_back(along)

    def laps(at, flat, y0):
        slot = lax.rem(at, 2) if not isinstance(at, int) else at % 2
        for h in range(halves):
            part = slice(8 * h, 8 * h + 8)
            sy[slot, part] = y0(part) + outflow(sp, h, at, flat, at)
            sz[slot, part] = outflow(sv, h, at, flat, at)

    def halo_y(k):
        def get(part):
            return jnp.concatenate([hry[0, k, part, :], zero], axis=1)

        return get

    def own_y(r):
        tail = tail_of(hly, r)

        def get(part):
            return jnp.concatenate([y_ref[0, r, part, :], tail[part]], axis=1)

        return get

    def between(at):
        slot = lax.rem(at, 2) if not isinstance(at, int) else at % 2
        total = None
        for h in range(halves):
            part = slice(8 * h, 8 * h + 8)
            term = (sv[at, part, 0:n] - sv[at - 1, part, 0:n]) * (sy[slot, part, 0:n] - sy[1 - slot, part, 0:n])
            term += (sz[slot, part, 0:n] - sz[1 - slot, part, 0:n]) * (sp[at, part, 0:n] - sp[at - 1, part, 0:n])
            total = term if total is None else total + term
        return total

    def along_row(at):
        slot = lax.rem(at, 2) if not isinstance(at, int) else at % 2
        total = None
        for h in range(halves):
            part = slice(8 * h, 8 * h + 8)
            v, y, z, q = sv[at, part], sy[slot, part], sz[slot, part], sp[at, part]
            term = (shift_next(v) - v) * (shift_next(y) - y) + (shift_next(z) - z) * (shift_next(q) - q)
            total = term if total is None else total + term
        return (total + shift_back(total))[:, 0:n]

    factor = -half_step * scale

    def finish(r, total):
        g_ref[0, pl.ds(r, 1), :] = factor * jnp.sum(total, axis=0, keepdims=True)

    laps(1, rows + 4, halo_y(0))

    def step(r, carry):
        at = r + 2
        laps(at, None, own_y(r))
        edge = between(at)

        @pl.when(r > 0)
        def _():
            finish(r - 1, acc[...] + edge)

        acc[...] = edge + along_row(at)
        return carry

    lax.fori_loop(0, rows, step, 0)
    laps(rows + 2, rows + 5, halo_y(1))
    finish(rows - 1, acc[...] + between(rows + 2))


def main(scale, fields, depth, halo):
    panels, rows, layers, n = fields[0].shape
    wide = n + LANES
    block = lambda x: pl.BlockSpec((1,) + x.shape[1:], lambda p: (p,) + (0,) * (x.ndim - 1))
    operands = [*fields, depth, *halo]
    return pl.pallas_call(
        functools.partial(main_kernel, layers, scale),
        grid=(panels,),
        in_specs=[block(x) for x in operands],
        out_specs=pl.BlockSpec((1, rows, n), lambda p: (p, 0, 0)),
        out_shape=jax.ShapeDtypeStruct((panels, rows, n), F32),
        scratch_shapes=[
            pltpu.VMEM((rows + 6, layers, wide), F32),
            pltpu.VMEM((rows + 6, layers, wide), F32),
            pltpu.VMEM((2, layers, wide), F32),
            pltpu.VMEM((2, layers, wide), F32),
            pltpu.VMEM((rows + 3, 8, wide), F32),
            pltpu.VMEM((rows + 2, 8, wide), F32),
            pltpu.VMEM((8, n), F32),
        ],
        compiler_params=pltpu.CompilerParams(vmem_limit_bytes=48 * 1024 * 1024),
        name="main",
    )(*operands)


def body(bathymetry, initial_state, patterns, pattern_index, coupling, final_weights):
    tiles, samples = lax.axis_size("tile"), lax.axis_size("samp")
    layers, panels, rows, n = initial_state.shape
    weights = final_weights[0]
    mixing = jnp.eye(layers, dtype=F32) + coupling

    def cat(matrix):
        high = lax.reduce_precision(matrix, 8, 7)
        low = matrix - high
        return jnp.concatenate([high, low, high], axis=1).astype(jnp.bfloat16)

    fwd, bwd = cat(mixing), cat(mixing.T)
    sel = (pattern_index[0][:, None] == jnp.arange(8, dtype=jnp.int32)[None, :]).astype(jnp.bfloat16)

    em, low, high, mm, aa = pack(tiles, initial_state, weights, patterns, bathymetry)
    ring = [(i, (i + 1) % tiles) for i in range(tiles)]
    west = lax.ppermute(high, "tile", ring)
    east = lax.ppermute(low, "tile", [(j, i) for i, j in ring])
    mirrored = lax.ppermute(mm, "tile", [(i, tiles - 1 - i) for i in range(tiles)])
    above = lax.ppermute(mm[0:2], "tile", [(i, tiles - i) for i in range(1, tiles)])
    below = lax.ppermute(mm[0:2], "tile", [(i, tiles - 2 - i) for i in range(tiles - 1)])
    windows = lax.all_to_all(aa, "tile", 0, 0, tiled=True)
    fields = mix_all(initial_state, weights, patterns, fwd, bwd, sel)
    halo = halos(tiles, layers, rows, west, east, em, mirrored, above, below, windows, fwd, bwd, sel)
    gradient = main(1.0 / samples, fields, bathymetry, halo)
    if samples == 2:
        return gradient + lax.ppermute(gradient, "samp", [(0, 1), (1, 0)])
    return lax.psum(gradient, "samp")


def solution(mesh):
    in_specs = (
        P(None, "tile", None),
        P(None, None, "tile", None),
        P(None, None, "tile", None),
        P("samp", None),
        P(),
        P("samp", None, None, "tile", None),
    )
    return jax.shard_map(body, mesh=mesh, in_specs=in_specs, out_specs=P(None, "tile", None), check_vma=False)
```

profile of v0, /device:TPU:0, one launch (start us, length us, event | category | flops | bytes accessed | tf_op | source)
XLA Modules:
  0.0 183.8 jit_solution(4025525859432705990)
XLA Ops:
  0.0 0.0 copy-start
  0.0 1.1 copy-done
  1.1 0.0 copy-start.2
  1.1 1.0 copy-done.2
  2.1 0.0 copy-start.6
  2.1 0.0 copy-start.7
  2.1 0.0 copy-start.1
  2.1 20.5 %pack.1 = (f32[6,40,128]{2,1,0:T(8,128)S(1)}, f32[6,2,40,512]{3,2,1,0:T(8,128)}, f32[6,2,40,512]{3,2,1,0:T(8,128)}, f32[3,40,128]{2,1,0:T(8,128)}, f32[16,48,128]{2,1,0:T(8,128)}) custom-call(f32[16,6,32,512]{3,2,1,0:T(8,128)} %s_ref.3, f32[16,6,32,512]{3,2,1,0:T(8,128)} %bitcast.5, bf16[4,6,32,512]{3,2,1,0:T(8,128)(2,1)S(1)} %copy-done, ...), custom_call_target="tpu_custom_call" | custom-call | tf_op jit(solution)/shard_map/pack/pallas_call | solution.py:157
  22.7 0.0 copy-start.4
  22.7 0.6 copy-done.4
  23.3 0.0 collective-permute-start
  23.3 5.5 %collective-permute-start.1 = (f32[6,2,40,512]{3,2,1,0:T(8,128)}, f32[6,2,40,512]{3,2,1,0:T(8,128)S(1)}, u32[]{:S(2)}, u32[]{:S(2)}) collective-permute-start(f32[6,2,40,512]{3,2,1,0:T(8,128)} %get-tuple-element.28), channel_id=1, source_target_pairs={{2,0},{4,2},{6,4},{8,6},{10,8},{12,10},{14,12},{16,14},{18,16},{20... | collective-permute-start | bytes 2949128 | tf_op jit(solution)/shard_map/ppermute | solution.py:554
  28.8 1.4 slice.4
  30.2 2.8 %collective-permute-start.4 = (f32[2,40,128]{2,1,0:T(8,128)}, f32[2,40,128]{2,1,0:T(8,128)}, u32[]{:S(2)}, u32[]{:S(2)}) collective-permute-start(f32[2,40,128]{2,1,0:T(8,128)} %slice.4), channel_id=1, source_target_pairs={{0,28},{2,26},{4,24},{6,22},{8,20},{10,18},{12,16},{14,14},{16,12}... | collective-permute-start | bytes 122888 | tf_op jit(solution)/shard_map/ppermute | solution.py:557
  33.0 1.3 collective-permute-start.3
  34.2 3.4 %collective-permute-start.2 = (f32[3,40,128]{2,1,0:T(8,128)}, f32[3,40,128]{2,1,0:T(8,128)}, u32[]{:S(2)}, u32[]{:S(2)}) collective-permute-start(f32[3,40,128]{2,1,0:T(8,128)} %get-tuple-element.30), channel_id=1, source_target_pairs={{0,30},{2,28},{4,26},{6,24},{8,22},{10,20},{12,18},{14,16},{16,14}... | collective-permute-start | bytes 184328 | tf_op jit(solution)/shard_map/ppermute | solution.py:555
  37.7 6.1 %all-to-all-start = ((f32[16,48,128]{2,1,0:T(8,128)}), f32[16,48,128]{2,1,0:T(8,128)S(1)}, u32[]{:S(2)}, u32[]{:S(2)}) async-start(f32[16,48,128]{2,1,0:T(8,128)} %get-tuple-element.31), calls=%async_computation | async-start | bytes 786432 | tf_op jit(solution)/shard_map/all_to_all | solution.py:558
  43.8 0.0 copy-done.6
  43.8 0.1 copy.10
  43.8 0.1 copy.12
  43.9 0.1 copy.11
  44.0 0.0 copy-done.7
  44.0 0.1 fusion.2.sel_ref
  44.1 0.1 pad_maximum_fusion
  44.2 0.0 copy-done.1
  44.2 0.0 copy-start.3
  44.2 24.3 %mix.1 = (f32[6,32,16,512]{3,2,1,0:T(8,128)}, f32[6,32,16,512]{3,2,1,0:T(8,128)}, f32[6,32,16,512]{3,2,1,0:T(8,128)}) custom-call(f32[16,6,32,512]{3,2,1,0:T(8,128)} %s_ref.3, f32[16,6,32,512]{3,2,1,0:T(8,128)} %bitcast.6, bf16[4,6,32,512]{3,2,1,0:T(8,128)(2,1)S(1)} %copy-done.1, bf16[16,48]{1,0:T(8,128)(2,1)S(1)} %get-tuple-element.47.fwd_ref, ...), custom_call_target="tpu_custom_call" | custom-call | flops 301989888 | bytes 31457280 | tf_op jit(solution)/shard_map/mix/pallas_call | solution.py:202
  68.5 0.0 collective-permute-done.4.md_ref
  68.5 0.0 collective-permute-done.3.mu_ref
  68.5 0.0 collective-permute-done.2.mm_ref
  68.5 0.0 all-to-all-done.aa_ref
  68.5 0.0 collective-permute-done.west_ref
  68.5 0.0 collective-permute-done.1.east_ref
  68.5 0.0 copy-start.5
  68.5 0.9 copy-done.5
  69.4 2.2 %halos.1 = (f32[6,4,16,512]{3,2,1,0:T(8,128)S(1)}, f32[6,4,16,512]{3,2,1,0:T(8,128)S(1)}, f32[6,2,16,512]{3,2,1,0:T(8,128)S(1)}, f32[6,8,512]{2,1,0:T(8,128)S(1)...) custom-call(f32[6,2,40,512]{3,2,1,0:T(8,128)S(1)} %collective-permut, ...), custom_call_target="tpu_custom_call" | custom-call | tf_op jit(solution)/shard_map/halos/pallas_call | solution.py:354
  71.6 0.0 copy-done.3
  71.6 100.0 %main.1 = f32[6,32,512]{2,1,0:T(8,128)S(1)} custom-call(f32[6,32,16,512]{3,2,1,0:T(8,128)} %get-tuple-element.24.p_ref, f32[6,32,16,512]{3,2,1,0:T(8,128)} %get-tuple-element.25.v_ref, f32[6,32,16,512]{3,2,1,0:T(8,128)} %get-tuple-element.26.y_ref, f32[6,32,512]{2,1,0:T(8,128)S(1)} %copy-done.3, f32[6,4,16,512]{3,2,1,0:T(8,128)S(1)} %get-tuple-element.32.hrp, ...), custom_call_target="tpu_custom_call" | custom-call | tf_op jit(solution)/shard_map/main/pallas_call | solution.py:517
  171.7 2.0 %collective-permute-start.5 = (f32[6,32,512]{2,1,0:T(8,128)S(1)}, f32[6,32,512]{2,1,0:T(8,128)S(1)}, u32[]{:S(2)}, u32[]{:S(2)}) collective-permute-start(f32[6,32,512]{2,1,0:T(8,128)S(1)} %main.1), channel_id=1, source_target_pairs={{0,1},{1,0},{2,3},{3,2},{4,5},{5,4},{6,7},{7,6},{8,9},{9,8},{10,11... | collective-permute-start | bytes 1179656 | tf_op jit(solution)/shard_map/ppermute | solution.py:563
  173.7 9.3 %collective-permute-done.5 = f32[6,32,512]{2,1,0:T(8,128)S(1)} collective-permute-done((f32[6,32,512]{2,1,0:T(8,128)S(1)}, f32[6,32,512]{2,1,0:T(8,128)S(1)}, u32[]{:S(2)}, u32[]{:S(2)}) %collective-permute-start.5) | collective-permute-done | bytes 393248 | tf_op jit(solution)/shard_map/ppermute | solution.py:563
  183.0 0.8 add.7
  (2 shorter events, 0.0 us)
Async XLA Ops:
  0.0 1.1 copy-start
  1.1 1.0 copy-start.2
  2.1 41.6 %copy-start.6 = (f32[16,16]{1,0:T(8,128)S(1)}, f32[16,16]{1,0:T(8,128)}, u32[]{:S(2)}) copy-start(f32[16,16]{1,0:T(8,128)} %param.10) | copy-start | bytes 3076
  2.1 41.9 %copy-start.7 = (s32[1,16]{1,0:T(1,128)S(1)}, s32[1,16]{1,0:T(1,128)}, u32[]{:S(2)}) copy-start(s32[1,16]{1,0:T(1,128)} %param.9) | copy-start | bytes 196
  2.1 42.1 %copy-start.1 = (bf16[4,6,32,512]{3,2,1,0:T(8,128)(2,1)S(1)}, bf16[4,6,32,512]{3,2,1,0:T(8,128)(2,1)}, u32[]{:S(2)}) copy-start(bf16[4,6,32,512]{3,2,1,0:T(8,128)(2,1)} %pat_ref.3) | copy-start | bytes 2359300
  22.7 0.6 copy-start.4
  23.3 45.2 %collective-permute-start = (f32[6,2,40,512]{3,2,1,0:T(8,128)}, f32[6,2,40,512]{3,2,1,0:T(8,128)S(1)}, u32[]{:S(2)}, u32[]{:S(2)}) collective-permute-start(f32[6,2,40,512]{3,2,1,0:T(8,128)} %get-tuple-element.27), channel_id=1, source_target_pairs={{0,2},{2,4},{4,6},{6,8},{8,10},{10,12},{12,14},{14,16},{16,18},{18... | collective-permute-start | bytes 2949128 | tf_op jit(solution)/shard_map/ppermute | solution.py:553
  23.3 45.2 %collective-permute-start.1 = (f32[6,2,40,512]{3,2,1,0:T(8,128)}, f32[6,2,40,512]{3,2,1,0:T(8,128)S(1)}, u32[]{:S(2)}, u32[]{:S(2)}) collective-permute-start(f32[6,2,40,512]{3,2,1,0:T(8,128)} %get-tuple-element.28), channel_id=1, source_target_pairs={{2,0},{4,2},{6,4},{8,6},{10,8},{12,10},{14,12},{16,14},{18,16},{20... | collective-permute-start | bytes 2949128 | tf_op jit(solution)/shard_map/ppermute | solution.py:554
  30.2 38.3 %collective-permute-start.4 = (f32[2,40,128]{2,1,0:T(8,128)}, f32[2,40,128]{2,1,0:T(8,128)}, u32[]{:S(2)}, u32[]{:S(2)}) collective-permute-start(f32[2,40,128]{2,1,0:T(8,128)} %slice.4), channel_id=1, source_target_pairs={{0,28},{2,26},{4,24},{6,22},{8,20},{10,18},{12,16},{14,14},{16,12}... | collective-permute-start | bytes 122888 | tf_op jit(solution)/shard_map/ppermute | solution.py:557
  33.0 35.5 %collective-permute-start.3 = (f32[2,40,128]{2,1,0:T(8,128)}, f32[2,40,128]{2,1,0:T(8,128)}, u32[]{:S(2)}, u32[]{:S(2)}) collective-permute-start(f32[2,40,128]{2,1,0:T(8,128)} %slice.4), channel_id=1, source_target_pairs={{2,30},{4,28},{6,26},{8,24},{10,22},{12,20},{14,18},{16,16},{18,14... | collective-permute-start | bytes 122888 | tf_op jit(solution)/shard_map/ppermute | solution.py:556
  34.2 34.3 %collective-permute-start.2 = (f32[3,40,128]{2,1,0:T(8,128)}, f32[3,40,128]{2,1,0:T(8,128)}, u32[]{:S(2)}, u32[]{:S(2)}) collective-permute-start(f32[3,40,128]{2,1,0:T(8,128)} %get-tuple-element.30), channel_id=1, source_target_pairs={{0,30},{2,28},{4,26},{6,24},{8,22},{10,20},{12,18},{14,16},{16,14}... | collective-permute-start | bytes 184328 | tf_op jit(solution)/shard_map/ppermute | solution.py:555
  37.7 30.9 %all-to-all-start = ((f32[16,48,128]{2,1,0:T(8,128)}), f32[16,48,128]{2,1,0:T(8,128)S(1)}, u32[]{:S(2)}, u32[]{:S(2)}) async-start(f32[16,48,128]{2,1,0:T(8,128)} %get-tuple-element.31), calls=%async_computation | async-start | bytes 786432 | tf_op jit(solution)/shard_map/all_to_all | solution.py:558
  44.2 27.4 %copy-start.3 = (f32[6,32,512]{2,1,0:T(8,128)S(1)}, f32[6,32,512]{2,1,0:T(8,128)}, u32[]{:S(2)}) copy-start(f32[6,32,512]{2,1,0:T(8,128)} %b_ref.3) | copy-start | bytes 1179652
  68.5 0.9 copy-start.5
  171.7 11.3 %collective-permute-start.5 = (f32[6,32,512]{2,1,0:T(8,128)S(1)}, f32[6,32,512]{2,1,0:T(8,128)S(1)}, u32[]{:S(2)}, u32[]{:S(2)}) collective-permute-start(f32[6,32,512]{2,1,0:T(8,128)S(1)} %main.1), channel_id=1, source_target_pairs={{0,1},{1,0},{2,3},{3,2},{4,5},{5,4},{6,7},{7,6},{8,9},{9,8},{10,11... | collective-permute-start | bytes 1179656 | tf_op jit(solution)/shard_map/ppermute | solution.py:563
where the time goes:
time: 185 us; the launch traced here: 184 us
  Pallas kernels  147 us (79%)
  starting transfers between devices  21 us (11%)
  waiting for transfers between devices  9.32 us (5%)
  local copies, waits for them, and re-layouts  5.3 us (3%)
    pallas_call x1, Pallas kernels, main(): pl.pallas_call(functools.partial(main_kernel, layers, scale), grid=(panel...  100 us
    pallas_call x1, Pallas kernels, mix_all(): pl.pallas_call(mix_kernel, grid=(panels, n // LANES), in_specs=[part(laye...  24.3 us
    pallas_call x1, Pallas kernels, pack(): pl.pallas_call(functools.partial(pack_kernel, tiles), grid=(panels, n //...  20.5 us
    ppermute x1, waiting for transfers between devices, body(): return gradient + lax.ppermute(gradient, 'samp', [(0, 1), (1, 0)])  9.3 us
    all_to_all x1, starting transfers between devices, body(): windows = lax.all_to_all(aa, 'tile', 0, 0, tiled=True)  6.09 us
    ppermute x1, starting transfers between devices, body(): east = lax.ppermute(low, 'tile', [(j, i) for i, j in ring])  5.49 us
    unnamed x17, local copies, waits for them, and re-layouts  3.74 us
  transfers between devices with their start and end apart: 7, of which 1 were waited for; matrix products, arithmetic and copies ran while one was open for 1% of the time, Pallas kernels for 13%

commit v1 on v0

--- a/solution.py
+++ b/solution.py
@@ -9,6 +9,7 @@
 
 STEP_FACTOR = 0.1
 LANES = 128
+GROUP = 4
 CH = 40
 F32 = jnp.float32
 
@@ -365,7 +366,7 @@
     p_ref, v_ref, y_ref, b_ref,
     hrp, hrv, hry, hrb, hlp, hlv, hly, hlb, hcp, hcv, hcb,
     g_ref,
-    sp, sv, sy, sz, bi, bj, acc,
+    sp, sv, sy, sz, ip, iv, jp, jv, ty, bi, bj, acc,
 ):
     rows, n = p_ref.shape[1], p_ref.shape[3]
     wide = n + LANES
@@ -384,129 +385,122 @@
             dst[slot, :, 0:n] = row_src[0, k]
             dst[slot, :, n:wide] = cor_src[0, corner]
 
-    def tail_of(ref, r):
-        return pltpu.roll(ref[0], lax.rem(126 - 4 * r + 4 * LANES, LANES), 1)
-
-    def fill(r, carry):
-        sp[r + 2, :, 0:n] = p_ref[0, r]
-        sp[r + 2, :, n:wide] = tail_of(hlp, r)
-        sv[r + 2, :, 0:n] = v_ref[0, r]
-        sv[r + 2, :, n:wide] = tail_of(hlv, r)
-        return carry
-
-    lax.fori_loop(0, rows, fill, 0, unroll=2)
-
+    def tail_of(x, r):
+        return pltpu.roll(x, (126 - 4 * r) % LANES, 1)
+
+    def shift_next(x):
+        return pltpu.roll(x, wide - 1, 1)
+
+    def shift_back(x):
+        return pltpu.roll(x, 1, 1)
+
+    edges_p, edges_v, edges_y, edges_b = hlp[0], hlv[0], hly[0], hlb[0]
     half_step = 0.5 * STEP_FACTOR
-
-    def depth_row(r):
-        return jnp.concatenate(
-            [jnp.broadcast_to(b_ref[0, pl.ds(r, 1), :], (8, n)), tail_of(hlb, r)], axis=1
-        )
+    zero = jnp.zeros((8, LANES), F32)
 
     def depth_halo(k, tail):
         return jnp.concatenate([jnp.broadcast_to(hrb[0, k : k + 1, :], (8, n)), tail], axis=1)
 
-    def shift_next(x):
-        return pltpu.roll(x, wide - 1, 1)
-
-    def shift_back(x):
-        return pltpu.roll(x, 1, 1)
-
-    zero = jnp.zeros((8, LANES), F32)
     d_m2, d_m1 = depth_halo(0, zero), depth_halo(1, hcb[0, 1])
     d_p0, d_p1 = depth_halo(2, hcb[0, 3]), depth_halo(3, zero)
     j_m1, j_p0 = depth_halo(1, hcb[0, 0]), depth_halo(2, hcb[0, 2])
     bi[0] = half_step * (d_m2 + d_m1)
-    bi[1] = half_step * (d_m1 + depth_row(0))
-    bi[rows + 1] = half_step * (depth_row(rows - 1) + d_p0)
     bi[rows + 2] = half_step * (d_p0 + d_p1)
     bj[0] = half_step * (j_m1 + shift_next(j_m1))
     bj[rows + 1] = half_step * (j_p0 + shift_next(j_p0))
-
-    def fill_depth(r, here):
+    last = d_m1
+    for r in range(rows):
+        sp[r + 2, :, 0:n] = p_ref[0, r]
+        sp[r + 2, :, n:wide] = tail_of(edges_p, r)
+        sv[r + 2, :, 0:n] = v_ref[0, r]
+        sv[r + 2, :, n:wide] = tail_of(edges_v, r)
+        ty[r] = tail_of(edges_y, r)
+        here = jnp.concatenate([jnp.broadcast_to(b_ref[0, r : r + 1, :], (8, n)), tail_of(edges_b, r)], axis=1)
+        bi[r + 1] = half_step * (last + here)
         bj[r + 1] = half_step * (here + shift_next(here))
-        after = depth_row(jnp.minimum(r + 1, rows - 1))
-
-        @pl.when(r + 1 < rows)
-        def _():
-            bi[r + 2] = half_step * (here + after)
-
-        return after
-
-    lax.fori_loop(0, rows, fill_depth, depth_row(0))
-
-    def outflow(ref, h, at, flat, out):
-        part = slice(8 * h, 8 * h + 8)
-        here = ref[at, part]
-        before = bi[out - 1 + 0] * (here - ref[at - 1, part])
-        after = bi[out] * (ref[at + 1, part] - here)
-        line = here if flat is None else ref[flat, part]
-        along = bj[out - 1] * (shift_next(line) - line)
-        return after - before + along - shift_back(along)
-
-    def laps(at, flat, y0):
-        slot = lax.rem(at, 2) if not isinstance(at, int) else at % 2
+        last = here
+    bi[rows + 1] = half_step * (last + d_p0)
+
+    def lap(ref, at, flat, bases, outs, by_i, by_j, count):
         for h in range(halves):
             part = slice(8 * h, 8 * h + 8)
-            sy[slot, part] = y0(part) + outflow(sp, h, at, flat, at)
-            sz[slot, part] = outflow(sv, h, at, flat, at)
+            here = ref[at, part]
+            before = bi[at - 1] * (here - ref[at - 1, part])
+            for u in range(count):
+                after_row = ref[at + u + 1, part]
+                step_i = after_row - here
+                if by_i is not None:
+                    by_i[at + u - 1, part] = step_i[:, 0:n]
+                after = bi[at + u] * step_i
+                line = here if flat is None else ref[flat, part]
+                step_j = shift_next(line) - line
+                if by_j is not None:
+                    by_j[at + u - 2, part] = step_j
+                along = bj[at + u - 1] * step_j
+                out = after - before + along - shift_back(along)
+                if bases is not None:
+                    out = out + bases(u, part)
+                outs[at + u - 1, part] = out
+                here, before = after_row, after
 
     def halo_y(k):
-        def get(part):
-            return jnp.concatenate([hry[0, k, part, :], zero], axis=1)
-
-        return get
-
-    def own_y(r):
-        tail = tail_of(hly, r)
-
-        def get(part):
-            return jnp.concatenate([y_ref[0, r, part, :], tail[part]], axis=1)
-
-        return get
-
-    def between(at):
-        slot = lax.rem(at, 2) if not isinstance(at, int) else at % 2
+        return lambda u, part: jnp.concatenate([hry[0, k, part, :], zero], axis=1)
+
+    lap(sp, 1, rows + 4, halo_y(0), sy, ip, None, 1)
+    lap(sv, 1, rows + 4, None, sz, iv, None, 1)
+    lap(sp, rows + 2, rows + 5, halo_y(1), sy, None, None, 1)
+    lap(sv, rows + 2, rows + 5, None, sz, None, None, 1)
+
+    group = GROUP
+
+    def lap_rows(i, carry):
+        r = i * group
+
+        def own_y(u, part):
+            return jnp.concatenate([y_ref[0, r + u, part, :], ty[r + u, part]], axis=1)
+
+        lap(sp, r + 2, None, own_y, sy, ip, jp, group)
+        lap(sv, r + 2, None, None, sz, iv, jv, group)
+        return carry
+
+    lax.fori_loop(0, rows // group, lap_rows, 0)
+
+    def between(k):
         total = None
         for h in range(halves):
             part = slice(8 * h, 8 * h + 8)
-            term = (sv[at, part, 0:n] - sv[at - 1, part, 0:n]) * (sy[slot, part, 0:n] - sy[1 - slot, part, 0:n])
-            term += (sz[slot, part, 0:n] - sz[1 - slot, part, 0:n]) * (sp[at, part, 0:n] - sp[at - 1, part, 0:n])
+            term = iv[k, part] * (sy[k + 1, part, 0:n] - sy[k, part, 0:n])
+            term += ip[k, part] * (sz[k + 1, part, 0:n] - sz[k, part, 0:n])
             total = term if total is None else total + term
         return total
 
-    def along_row(at):
-        slot = lax.rem(at, 2) if not isinstance(at, int) else at % 2
+    def along_row(r):
         total = None
         for h in range(halves):
             part = slice(8 * h, 8 * h + 8)
-            v, y, z, q = sv[at, part], sy[slot, part], sz[slot, part], sp[at, part]
-            term = (shift_next(v) - v) * (shift_next(y) - y) + (shift_next(z) - z) * (shift_next(q) - q)
+            y, z = sy[r + 1, part], sz[r + 1, part]
+            term = jv[r, part] * (shift_next(y) - y) + jp[r, part] * (shift_next(z) - z)
             total = term if total is None else total + term
         return (total + shift_back(total))[:, 0:n]
 
-    factor = -half_step * scale
-
-    def finish(r, total):
-        g_ref[0, pl.ds(r, 1), :] = factor * jnp.sum(total, axis=0, keepdims=True)
-
-    laps(1, rows + 4, halo_y(0))
-
-    def step(r, carry):
-        at = r + 2
-        laps(at, None, own_y(r))
-        edge = between(at)
-
-        @pl.when(r > 0)
-        def _():
-            finish(r - 1, acc[...] + edge)
-
-        acc[...] = edge + along_row(at)
-        return carry
-
-    lax.fori_loop(0, rows, step, 0)
-    laps(rows + 2, rows + 5, halo_y(1))
-    finish(rows - 1, acc[...] + between(rows + 2))
+    def products(i, before):
+        r = i * group
+        for u in range(group):
+            after = between(r + u + 1)
+            acc[r + u] = before + after + along_row(r + u)
+            before = after
+        return before
+
+    lax.fori_loop(0, rows // group, products, between(0))
+
+    x = acc[...].reshape(8 * rows, n)
+    at_row = lax.broadcasted_iota(jnp.int32, (rows, 8 * rows), 0)
+    ones = (lax.broadcasted_iota(jnp.int32, (rows, 8 * rows), 1) // 8 == at_row).astype(F32).astype(jnp.bfloat16)
+    hi = x.astype(jnp.bfloat16)
+    rest = x - hi.astype(F32)
+    lo = rest.astype(jnp.bfloat16)
+    total = jnp.dot(ones, hi, preferred_element_type=F32) + jnp.dot(ones, lo, preferred_element_type=F32)
+    g_ref[0] = (-half_step * scale) * total
 
 
 def main(scale, fields, depth, halo):
@@ -523,11 +517,16 @@
         scratch_shapes=[
             pltpu.VMEM((rows + 6, layers, wide), F32),
             pltpu.VMEM((rows + 6, layers, wide), F32),
-            pltpu.VMEM((2, layers, wide), F32),
-            pltpu.VMEM((2, layers, wide), F32),
+            pltpu.VMEM((rows + 2, layers, wide), F32),
+            pltpu.VMEM((rows + 2, layers, wide), F32),
+            pltpu.VMEM((rows + 1, layers, n), F32),
+            pltpu.VMEM((rows + 1, layers, n), F32),
+            pltpu.VMEM((rows, layers, wide), F32),
+            pltpu.VMEM((rows, layers, wide), F32),
+            pltpu.VMEM((rows, layers, LANES), F32),
             pltpu.VMEM((rows + 3, 8, wide), F32),
             pltpu.VMEM((rows + 2, 8, wide), F32),
-            pltpu.VMEM((8, n), F32),
+            pltpu.VMEM((rows, 8, n), F32),
         ],
         compiler_params=pltpu.CompilerParams(vmem_limit_bytes=48 * 1024 * 1024),
         name="main",

time: 185 us -> 127 us (0.69)
  Pallas kernels: 147 us -> 89 us
    pallas_call x1, Pallas kernels: 100 us -> 42 us  [main(): pl.pallas_call(functools.partial(main_kernel, layers, scale), grid=(panel...]
  transfers between devices with their start and end apart: 7 -> 7, of which waited for: 1 -> 1; matrix products, arithmetic and copies ran while one was open for 1% -> 1% of each run, Pallas kernels for 13% -> 19%
where the time goes in v1:
time: 127 us; the launch traced here: 126 us
  Pallas kernels  89 us (70%)
  starting transfers between devices  21 us (17%)
  waiting for transfers between devices  9.32 us (7%)
  local copies, waits for them, and re-layouts  5.3 us (4%)
    pallas_call x1, Pallas kernels, main(): pl.pallas_call(functools.partial(main_kernel, layers, scale), grid=(panel...  42 us
    pallas_call x1, Pallas kernels, mix_all(): pl.pallas_call(mix_kernel, grid=(panels, n // LANES), in_specs=[part(laye...  24.3 us
    pallas_call x1, Pallas kernels, pack(): pl.pallas_call(functools.partial(pack_kernel, tiles), grid=(panels, n //...  20.5 us
    ppermute x1, waiting for transfers between devices, body(): return gradient + lax.ppermute(gradient, 'samp', [(0, 1), (1, 0)])  9.3 us
    all_to_all x1, starting transfers between devices, body(): windows = lax.all_to_all(aa, 'tile', 0, 0, tiled=True)  6.09 us
    ppermute x1, starting transfers between devices, body(): east = lax.ppermute(low, 'tile', [(j, i) for i, j in ring])  5.49 us
    unnamed x17, local copies, waits for them, and re-layouts  3.74 us
    ppermute x1, starting transfers between devices, body(): lax.ppermute(mm, 'tile', [(i, tiles - 1 - i) for i in range(tiles)])  3.41 us
  transfers between devices with their start and end apart: 7, of which 1 were waited for; matrix products, arithmetic and copies ran while one was open for 1% of the time, Pallas kernels for 19%

profile of v1, /device:TPU:0, one launch (start us, length us, event | category | flops | bytes accessed | tf_op | source)
XLA Modules:
  0.0 125.7 jit_solution(10730782840528022618)
XLA Ops:
  0.0 0.0 copy-start
  0.0 1.1 copy-done
  1.1 0.0 copy-start.2
  1.1 1.0 copy-done.2
  2.1 0.0 copy-start.6
  2.1 0.0 copy-start.7
  2.1 0.0 copy-start.1
  2.1 20.5 %pack.1 = (f32[6,40,128]{2,1,0:T(8,128)S(1)}, f32[6,2,40,512]{3,2,1,0:T(8,128)}, f32[6,2,40,512]{3,2,1,0:T(8,128)}, f32[3,40,128]{2,1,0:T(8,128)}, f32[16,48,128]{2,1,0:T(8,128)}) custom-call(f32[16,6,32,512]{3,2,1,0:T(8,128)} %s_ref.3, f32[16,6,32,512]{3,2,1,0:T(8,128)} %bitcast.5, bf16[4,6,32,512]{3,2,1,0:T(8,128)(2,1)S(1)} %copy-done, ...), custom_call_target="tpu_custom_call" | custom-call | tf_op jit(solution)/shard_map/pack/pallas_call | solution.py:158
  22.7 0.0 copy-start.4
  22.7 0.6 copy-done.4
  23.3 0.0 collective-permute-start
  23.3 5.5 %collective-permute-start.1 = (f32[6,2,40,512]{3,2,1,0:T(8,128)}, f32[6,2,40,512]{3,2,1,0:T(8,128)S(1)}, u32[]{:S(2)}, u32[]{:S(2)}) collective-permute-start(f32[6,2,40,512]{3,2,1,0:T(8,128)} %get-tuple-element.28), channel_id=1, source_target_pairs={{2,0},{4,2},{6,4},{8,6},{10,8},{12,10},{14,12},{16,14},{18,16},{20... | collective-permute-start | bytes 2949128 | tf_op jit(solution)/shard_map/ppermute | solution.py:553
  28.8 1.4 %slice.4 = f32[2,40,128]{2,1,0:T(8,128)} slice(f32[3,40,128]{2,1,0:T(8,128)} %get-tuple-element.30), slice={[0:2], [0:40], [0:128]} | slice | bytes 81920 | tf_op jit(solution)/shard_map/slice | solution.py:555
  30.2 2.8 %collective-permute-start.4 = (f32[2,40,128]{2,1,0:T(8,128)}, f32[2,40,128]{2,1,0:T(8,128)}, u32[]{:S(2)}, u32[]{:S(2)}) collective-permute-start(f32[2,40,128]{2,1,0:T(8,128)} %slice.4), channel_id=1, source_target_pairs={{0,28},{2,26},{4,24},{6,22},{8,20},{10,18},{12,16},{14,14},{16,12}... | collective-permute-start | bytes 122888 | tf_op jit(solution)/shard_map/ppermute | solution.py:556
  33.0 1.3 %collective-permute-start.3 = (f32[2,40,128]{2,1,0:T(8,128)}, f32[2,40,128]{2,1,0:T(8,128)}, u32[]{:S(2)}, u32[]{:S(2)}) collective-permute-start(f32[2,40,128]{2,1,0:T(8,128)} %slice.4), channel_id=1, source_target_pairs={{2,30},{4,28},{6,26},{8,24},{10,22},{12,20},{14,18},{16,16},{18,14... | collective-permute-start | bytes 122888 | tf_op jit(solution)/shard_map/ppermute | solution.py:555
  34.2 3.4 %collective-permute-start.2 = (f32[3,40,128]{2,1,0:T(8,128)}, f32[3,40,128]{2,1,0:T(8,128)}, u32[]{:S(2)}, u32[]{:S(2)}) collective-permute-start(f32[3,40,128]{2,1,0:T(8,128)} %get-tuple-element.30), channel_id=1, source_target_pairs={{0,30},{2,28},{4,26},{6,24},{8,22},{10,20},{12,18},{14,16},{16,14}... | collective-permute-start | bytes 184328 | tf_op jit(solution)/shard_map/ppermute | solution.py:554
  37.7 6.1 %all-to-all-start = ((f32[16,48,128]{2,1,0:T(8,128)}), f32[16,48,128]{2,1,0:T(8,128)S(1)}, u32[]{:S(2)}, u32[]{:S(2)}) async-start(f32[16,48,128]{2,1,0:T(8,128)} %get-tuple-element.31), calls=%async_computation | async-start | bytes 786432 | tf_op jit(solution)/shard_map/all_to_all | solution.py:557
  43.8 0.0 copy-done.6
  43.8 0.1 copy.10
  43.8 0.1 copy.12
  43.9 0.1 copy.11
  44.0 0.0 copy-done.7
  44.0 0.1 fusion.2.sel_ref
  44.1 0.1 pad_maximum_fusion
  44.2 0.0 copy-done.1
  44.2 0.0 copy-start.3
  44.2 24.3 %mix.1 = (f32[6,32,16,512]{3,2,1,0:T(8,128)}, f32[6,32,16,512]{3,2,1,0:T(8,128)}, f32[6,32,16,512]{3,2,1,0:T(8,128)}) custom-call(f32[16,6,32,512]{3,2,1,0:T(8,128)} %s_ref.3, f32[16,6,32,512]{3,2,1,0:T(8,128)} %bitcast.6, bf16[4,6,32,512]{3,2,1,0:T(8,128)(2,1)S(1)} %copy-done.1, bf16[16,48]{1,0:T(8,128)(2,1)S(1)} %get-tuple-element.47.fwd_ref, ...), custom_call_target="tpu_custom_call" | custom-call | flops 301989888 | bytes 31457280 | tf_op jit(solution)/shard_map/mix/pallas_call | solution.py:203
  68.5 0.0 collective-permute-done.4.md_ref
  68.5 0.0 collective-permute-done.3.mu_ref
  68.5 0.0 collective-permute-done.2.mm_ref
  68.5 0.0 all-to-all-done.aa_ref
  68.5 0.0 collective-permute-done.west_ref
  68.5 0.0 collective-permute-done.1.east_ref
  68.5 0.0 copy-start.5
  68.5 0.9 copy-done.5
  69.4 2.2 %halos.1 = (f32[6,4,16,512]{3,2,1,0:T(8,128)S(1)}, f32[6,4,16,512]{3,2,1,0:T(8,128)S(1)}, f32[6,2,16,512]{3,2,1,0:T(8,128)S(1)}, f32[6,8,512]{2,1,0:T(8,128)S(1)...) custom-call(f32[6,2,40,512]{3,2,1,0:T(8,128)S(1)} %collective-permut, ...), custom_call_target="tpu_custom_call" | custom-call | tf_op jit(solution)/shard_map/halos/pallas_call | solution.py:355
  71.6 0.0 copy-done.3
  71.6 42.0 %main.1 = f32[6,32,512]{2,1,0:T(8,128)S(1)} custom-call(f32[6,32,16,512]{3,2,1,0:T(8,128)} %get-tuple-element.24.p_ref, f32[6,32,16,512]{3,2,1,0:T(8,128)} %get-tuple-element.25.v_ref, f32[6,32,16,512]{3,2,1,0:T(8,128)} %get-tuple-element.26.y_ref, f32[6,32,512]{2,1,0:T(8,128)S(1)} %copy-done.3, f32[6,4,16,512]{3,2,1,0:T(8,128)S(1)} %get-tuple-element.32.hrp, ...), custom_call_target="tpu_custom_call" | custom-call | tf_op jit(solution)/shard_map/main/pallas_call | solution.py:511
  113.7 2.0 %collective-permute-start.5 = (f32[6,32,512]{2,1,0:T(8,128)S(1)}, f32[6,32,512]{2,1,0:T(8,128)S(1)}, u32[]{:S(2)}, u32[]{:S(2)}) collective-permute-start(f32[6,32,512]{2,1,0:T(8,128)S(1)} %main.1), channel_id=1, source_target_pairs={{0,1},{1,0},{2,3},{3,2},{4,5},{5,4},{6,7},{7,6},{8,9},{9,8},{10,11... | collective-permute-start | bytes 1179656 | tf_op jit(solution)/shard_map/ppermute | solution.py:562
  115.6 9.3 %collective-permute-done.5 = f32[6,32,512]{2,1,0:T(8,128)S(1)} collective-permute-done((f32[6,32,512]{2,1,0:T(8,128)S(1)}, f32[6,32,512]{2,1,0:T(8,128)S(1)}, u32[]{:S(2)}, u32[]{:S(2)}) %collective-permute-start.5) | collective-permute-done | bytes 393248 | tf_op jit(solution)/shard_map/ppermute | solution.py:562
  124.9 0.8 add.7
  (2 shorter events, 0.0 us)
Async XLA Ops:
  0.0 1.1 copy-start
  1.1 1.0 copy-start.2
  2.1 41.6 %copy-start.6 = (f32[16,16]{1,0:T(8,128)S(1)}, f32[16,16]{1,0:T(8,128)}, u32[]{:S(2)}) copy-start(f32[16,16]{1,0:T(8,128)} %param.10) | copy-start | bytes 3076
  2.1 41.9 %copy-start.7 = (s32[1,16]{1,0:T(1,128)S(1)}, s32[1,16]{1,0:T(1,128)}, u32[]{:S(2)}) copy-start(s32[1,16]{1,0:T(1,128)} %param.9) | copy-start | bytes 196
  2.1 42.1 %copy-start.1 = (bf16[4,6,32,512]{3,2,1,0:T(8,128)(2,1)S(1)}, bf16[4,6,32,512]{3,2,1,0:T(8,128)(2,1)}, u32[]{:S(2)}) copy-start(bf16[4,6,32,512]{3,2,1,0:T(8,128)(2,1)} %pat_ref.3) | copy-start | bytes 2359300
  22.7 0.6 copy-start.4
  23.3 45.2 %collective-permute-start = (f32[6,2,40,512]{3,2,1,0:T(8,128)}, f32[6,2,40,512]{3,2,1,0:T(8,128)S(1)}, u32[]{:S(2)}, u32[]{:S(2)}) collective-permute-start(f32[6,2,40,512]{3,2,1,0:T(8,128)} %get-tuple-element.27), channel_id=1, source_target_pairs={{0,2},{2,4},{4,6},{6,8},{8,10},{10,12},{12,14},{14,16},{16,18},{18... | collective-permute-start | bytes 2949128 | tf_op jit(solution)/shard_map/ppermute | solution.py:552
  23.3 45.2 %collective-permute-start.1 = (f32[6,2,40,512]{3,2,1,0:T(8,128)}, f32[6,2,40,512]{3,2,1,0:T(8,128)S(1)}, u32[]{:S(2)}, u32[]{:S(2)}) collective-permute-start(f32[6,2,40,512]{3,2,1,0:T(8,128)} %get-tuple-element.28), channel_id=1, source_target_pairs={{2,0},{4,2},{6,4},{8,6},{10,8},{12,10},{14,12},{16,14},{18,16},{20... | collective-permute-start | bytes 2949128 | tf_op jit(solution)/shard_map/ppermute | solution.py:553
  30.2 38.3 %collective-permute-start.4 = (f32[2,40,128]{2,1,0:T(8,128)}, f32[2,40,128]{2,1,0:T(8,128)}, u32[]{:S(2)}, u32[]{:S(2)}) collective-permute-start(f32[2,40,128]{2,1,0:T(8,128)} %slice.4), channel_id=1, source_target_pairs={{0,28},{2,26},{4,24},{6,22},{8,20},{10,18},{12,16},{14,14},{16,12}... | collective-permute-start | bytes 122888 | tf_op jit(solution)/shard_map/ppermute | solution.py:556
  33.0 35.5 %collective-permute-start.3 = (f32[2,40,128]{2,1,0:T(8,128)}, f32[2,40,128]{2,1,0:T(8,128)}, u32[]{:S(2)}, u32[]{:S(2)}) collective-permute-start(f32[2,40,128]{2,1,0:T(8,128)} %slice.4), channel_id=1, source_target_pairs={{2,30},{4,28},{6,26},{8,24},{10,22},{12,20},{14,18},{16,16},{18,14... | collective-permute-start | bytes 122888 | tf_op jit(solution)/shard_map/ppermute | solution.py:555
  34.2 34.3 %collective-permute-start.2 = (f32[3,40,128]{2,1,0:T(8,128)}, f32[3,40,128]{2,1,0:T(8,128)}, u32[]{:S(2)}, u32[]{:S(2)}) collective-permute-start(f32[3,40,128]{2,1,0:T(8,128)} %get-tuple-element.30), channel_id=1, source_target_pairs={{0,30},{2,28},{4,26},{6,24},{8,22},{10,20},{12,18},{14,16},{16,14}... | collective-permute-start | bytes 184328 | tf_op jit(solution)/shard_map/ppermute | solution.py:554
  37.7 30.9 %all-to-all-start = ((f32[16,48,128]{2,1,0:T(8,128)}), f32[16,48,128]{2,1,0:T(8,128)S(1)}, u32[]{:S(2)}, u32[]{:S(2)}) async-start(f32[16,48,128]{2,1,0:T(8,128)} %get-tuple-element.31), calls=%async_computation | async-start | bytes 786432 | tf_op jit(solution)/shard_map/all_to_all | solution.py:557
  44.2 27.4 %copy-start.3 = (f32[6,32,512]{2,1,0:T(8,128)S(1)}, f32[6,32,512]{2,1,0:T(8,128)}, u32[]{:S(2)}) copy-start(f32[6,32,512]{2,1,0:T(8,128)} %b_ref.3) | copy-start | bytes 1179652
  68.5 0.9 copy-start.5
  113.7 11.3 %collective-permute-start.5 = (f32[6,32,512]{2,1,0:T(8,128)S(1)}, f32[6,32,512]{2,1,0:T(8,128)S(1)}, u32[]{:S(2)}, u32[]{:S(2)}) collective-permute-start(f32[6,32,512]{2,1,0:T(8,128)S(1)} %main.1), channel_id=1, source_target_pairs={{0,1},{1,0},{2,3},{3,2},{4,5},{5,4},{6,7},{7,6},{8,9},{9,8},{10,11... | collective-permute-start | bytes 1179656 | tf_op jit(solution)/shard_map/ppermute | solution.py:562

commit v2 on v1

--- a/solution.py
+++ b/solution.py
@@ -29,6 +29,7 @@
 
 
 STRIDED = True
+VMEM = 60 * 1024 * 1024
 
 
 def layer_rows(ref, r):
@@ -38,106 +39,103 @@
     return ref.reshape(size * rows, LANES)[pl.ds(r, size, stride=rows), :]
 
 
-def pack_kernel(tiles, s_ref, w_ref, pat_ref, b_ref, em_ref, lo_ref, hi_ref, mm_ref, aa_ref, aux):
-    layers, rows = s_ref.shape[0], s_ref.shape[2]
-    p, block, blocks = pl.program_id(0), pl.program_id(1), pl.num_programs(1)
+def pack_kernel(tiles, blocks, layers, npat, *refs):
+    s_refs, w_refs, pat_refs = (refs[k * blocks : (k + 1) * blocks] for k in range(3))
+    b_ref, em_ref, lo_ref, hi_ref, mm_ref, aa_ref, aux = refs[3 * blocks :]
+    rows = b_ref.shape[1]
+    p = pl.program_id(0)
     place = lax.axis_index("tile")
     first, final = place == 0, place == tiles - 1
-    npat = pat_ref.shape[0]
     aux[...] = jnp.zeros(aux.shape, F32)
-    aux[0:npat, 0] = pat_ref[:, 0].astype(F32)
-    aux[npat, 0] = b_ref[0]
-    groups = ((0, layers, s_ref), (layers, layers, w_ref), (2 * layers, 8, aux))
-
-    for at, size, ref in groups:
-        for c in range(2):
-            lo_ref[0, c, at : at + size, :] = layer_rows(ref, c)
-            hi_ref[0, c, at : at + size, :] = layer_rows(ref, rows - 2 + c)
+    for c in range(blocks):
+        aux[c, 0:npat, 0] = pat_refs[c][:, 0].astype(F32)
+        aux[c, npat, 0] = b_ref[0, :, c * LANES : (c + 1) * LANES]
+    groups = (
+        (0, layers, s_refs),
+        (layers, layers, w_refs),
+        (2 * layers, 8, [aux.at[c] for c in range(blocks)]),
+    )
+    for at, size, parts in groups:
+        for c in range(blocks):
+            cut = slice(c * LANES, (c + 1) * LANES)
+            for k in range(2):
+                lo_ref[0, k, at : at + size, cut] = layer_rows(parts[c], k)
+                hi_ref[0, k, at : at + size, cut] = layer_rows(parts[c], rows - 2 + k)
+
+    for at, size, parts in groups:
+        shape = (8 * size, LANES)
+        ln, row = lane_iota(shape), lax.broadcasted_iota(jnp.int32, shape, 0) % 8
+        source = (ln % 4 + LANES - 2) % LANES
+        total = jnp.zeros(shape, F32)
+        for g in range(rows // 8):
+            cut = slice(8 * g, 8 * g + 8)
+            head = parts[0][:, 0, cut, :].reshape(shape)
+            tail = parts[blocks - 1][:, 0, cut, :].reshape(shape)
+            spread = lane_gather(jnp.where(ln < LANES // 2, head, tail), source)
+            total = jnp.where(ln // 4 == 8 * g + row, spread, total)
+        em_ref[0, at : at + size, :] = jnp.sum(total.reshape(size, 8, LANES), axis=1)
 
     lane = lane_iota((CH, LANES))
     side = lane % 4
-
-    @pl.when((p == 0) & (block == 0))
+    pad = jnp.zeros((LANES - CH, LANES), F32)
+
+    @pl.when(p == 0)
     def _():
         aa_ref[...] = jnp.zeros(aa_ref.shape, F32)
 
-    @pl.when(block == 0)
-    def _():
-        em_ref[...] = jnp.zeros(em_ref.shape, F32)
-
-    for mine, at_block in (((0, 1), blocks - 1), ((2, 3), 0)):
-        @pl.when(block == at_block)
-        def _(mine=mine):
-            for at, size, ref in groups:
-                ln = lane_iota((size, LANES))
-                keep = (ln % 4 == mine[0]) | (ln % 4 == mine[1])
-                out = jnp.zeros((size, LANES), F32)
-                for r in range(rows):
-                    turned = pltpu.roll(layer_rows(ref, r), (4 * r - 126) % LANES, 1)
-                    out = jnp.where(ln // 4 == r, turned, out)
-                em_ref[0, at : at + size, :] = jnp.where(keep, out, em_ref[0, at : at + size, :])
-
-    @pl.when(block == blocks - 1)
-    def _():
-        @pl.when(p == 1)
-        def _():
-            aa_ref[tiles - 1, 0:CH, :] = em_ref[0]
-            mm_ref[2] = em_ref[0]
-
-        @pl.when(p == 2)
-        def _():
-            mm_ref[0] = em_ref[0]
-
-        @pl.when(p == 3)
-        def _():
-            aa_ref[0, 0:CH, :] = em_ref[0]
-
-        @pl.when((p == 3) & jnp.logical_not(first))
-        def _():
-            mm_ref[2] = em_ref[0]
-
-        @pl.when(p == 4)
-        def _():
-            mm_ref[1] = em_ref[0]
-
-        @pl.when(p == 5)
-        def _():
-            mm_ref[1] = jnp.where(side < 2, mm_ref[1], em_ref[0])
+    @pl.when(p == 1)
+    def _():
+        aa_ref[tiles - 1, 0:CH, :] = em_ref[0]
+        mm_ref[2] = em_ref[0]
+
+    @pl.when(p == 2)
+    def _():
+        mm_ref[0] = em_ref[0]
+
+    @pl.when(p == 3)
+    def _():
+        aa_ref[0, 0:CH, :] = em_ref[0]
+
+    @pl.when((p == 3) & jnp.logical_not(first))
+    def _():
+        mm_ref[2] = em_ref[0]
+
+    @pl.when(p == 4)
+    def _():
+        mm_ref[1] = em_ref[0]
 
     per = LANES // rows
 
     def pole(ref, near, far, backward, is_five):
-        x, y = ref[0, near], ref[0, far]
-        turned = jnp.concatenate([x, jnp.zeros((LANES - CH, LANES), F32)], axis=0).T
-        for q in range(per):
-            if backward:
-                t = (blocks - 1 - block) * per + q
-                idx = LANES - 1 - q * rows - lane // 4
-            else:
-                t = block * per + q
-                idx = q * rows + lane // 4
-            idx = jnp.clip(idx, 0, LANES - 1)
-            a, b = lane_gather(x, idx), lane_gather(y, idx)
-            if is_five:
-                aa_ref[t, 0:CH, :] = jnp.where(side == 1, a, jnp.where(side == 0, b, aa_ref[t, 0:CH, :]))
-            else:
-                aa_ref[t, 0:CH, :] = jnp.where(side == 2, a, b)
-            low, high = q * rows, (q + 1) * rows - 1
-            if backward:
-                before, at_before = tiles - block * per - q, low
-                after, at_after = tiles - 1 - block * per - (q + 1), high
-            else:
-                before, at_before = block * per + q + 1, high
-                after, at_after = block * per + q - 1, low
-            m = 0 if is_five else 1
-
-            @pl.when(before < tiles)
-            def _(before=before, at=at_before):
-                aa_ref[before, CH + m : CH + m + 1, :] = turned[at : at + 1, :]
-
-            @pl.when(after >= 0)
-            def _(after=after, at=at_after):
-                aa_ref[after, CH + m + 2 : CH + m + 3, :] = turned[at : at + 1, :]
+        for block in range(blocks):
+            cut = slice(block * LANES, (block + 1) * LANES)
+            x, y = ref[0, near, :, cut], ref[0, far, :, cut]
+            turned = jnp.concatenate([x, pad], axis=0).T
+            for q in range(per):
+                if backward:
+                    t = (blocks - 1 - block) * per + q
+                    idx = LANES - 1 - q * rows - lane // 4
+                else:
+                    t = block * per + q
+                    idx = q * rows + lane // 4
+                idx = jnp.clip(idx, 0, LANES - 1)
+                a, b = lane_gather(x, idx), lane_gather(y, idx)
+                if is_five:
+                    aa_ref[t, 0:CH, :] = jnp.where(side == 1, a, jnp.where(side == 0, b, aa_ref[t, 0:CH, :]))
+                else:
+                    aa_ref[t, 0:CH, :] = jnp.where(side == 2, a, b)
+                low, high = q * rows, (q + 1) * rows - 1
+                if backward:
+                    before, at_before = tiles - block * per - q, low
+                    after, at_after = tiles - 1 - block * per - (q + 1), high
+                else:
+                    before, at_before = block * per + q + 1, high
+                    after, at_after = block * per + q - 1, low
+                m = CH if is_five else CH + 1
+                if before < tiles:
+                    aa_ref[before, m : m + 1, :] = turned[at_before : at_before + 1, :]
+                if after >= 0:
+                    aa_ref[after, m + 2 : m + 3, :] = turned[at_after : at_after + 1, :]
 
     for panel in (4, 5):
         @pl.when((p == panel) & first)
@@ -148,19 +146,36 @@
         def _(panel=panel):
             pole(hi_ref, 1, 0, panel == 5, panel == 5)
 
+    @pl.when(p == 5)
+    def _():
+        mm_ref[1] = jnp.where(side < 2, mm_ref[1], em_ref[0])
+        for k in range(2):
+            turned = jnp.concatenate([mm_ref[k], pad], axis=0).T
+            m = CH + 4 + 2 * k
+
+            @pl.when(jnp.logical_not(first))
+            def _(turned=turned, m=m):
+                aa_ref[tiles - place, m : m + 2, :] = turned[1:3, :]
+
+            @pl.when(jnp.logical_not(final))
+            def _(turned=turned, m=m):
+                at = 4 * (rows - 1) + 1
+                aa_ref[tiles - 2 - place, m : m + 2, :] = turned[at : at + 2, :]
+
 
 def pack(tiles, s, w, pat, b):
     layers, panels, rows, n = s.shape
-    npat = pat.shape[0]
-    full = lambda *shape: pl.BlockSpec(shape, lambda p, c: (0,) * len(shape))
-    part = lambda size: pl.BlockSpec((size, 1, rows, LANES), lambda p, c: (0, p, 0, c))
-    line = pl.BlockSpec((1, 2, CH, LANES), lambda p, c: (p, 0, 0, c))
+    npat, blocks = pat.shape[0], n // LANES
+    full = lambda *shape: pl.BlockSpec(shape, lambda p: (0,) * len(shape))
+    part = lambda size, c: pl.BlockSpec((size, 1, rows, LANES), lambda p: (0, p, 0, c))
+    line = pl.BlockSpec((1, 2, CH, n), lambda p: (p, 0, 0, 0))
     return pl.pallas_call(
-        functools.partial(pack_kernel, tiles),
-        grid=(panels, n // LANES),
-        in_specs=[part(layers), part(layers), part(npat), pl.BlockSpec((1, rows, LANES), lambda p, c: (p, 0, c))],
+        functools.partial(pack_kernel, tiles, blocks, layers, npat),
+        grid=(panels,),
+        in_specs=[part(size, c) for size in (layers, layers, npat) for c in range(blocks)]
+        + [pl.BlockSpec((1, rows, n), lambda p: (p, 0, 0))],
         out_specs=[
-            pl.BlockSpec((1, CH, LANES), lambda p, c: (p, 0, 0)),
+            pl.BlockSpec((1, CH, LANES), lambda p: (p, 0, 0)),
             line,
             line,
             full(3, CH, LANES),
@@ -173,41 +188,88 @@
             jax.ShapeDtypeStruct((3, CH, LANES), F32),
             jax.ShapeDtypeStruct((tiles, CH + 8, LANES), F32),
         ],
-        scratch_shapes=[pltpu.VMEM((8, 1, rows, LANES), F32)],
-        compiler_params=pltpu.CompilerParams(vmem_limit_bytes=48 * 1024 * 1024),
+        scratch_shapes=[pltpu.VMEM((blocks, 8, 1, rows, LANES), F32)],
+        compiler_params=pltpu.CompilerParams(vmem_limit_bytes=VMEM),
         name="pack",
-    )(s, w, pat, b)
-
-
-def mix_kernel(s_ref, w_ref, pat_ref, fwd_ref, bwd_ref, sel_ref, p_ref, v_ref, y_ref, pf):
-    rows = s_ref.shape[2]
-    npat = pat_ref.shape[0]
-    pf[...] = jnp.zeros(pf.shape, F32)
-    pf[0:npat, 0] = pat_ref[:, 0].astype(F32)
-    fwd, bwd, sel = fwd_ref[...], bwd_ref[...], sel_ref[...]
-    for r in range(rows):
-        s = layer_rows(s_ref, r)
-        p_ref[0, r] = mix(fwd, s)
-        v_ref[0, r] = mix(bwd, layer_rows(w_ref, r))
-        f = jnp.dot(sel, layer_rows(pf, r).astype(jnp.bfloat16), preferred_element_type=F32)
-        y_ref[0, r] = 3.0 * s + STEP_FACTOR * f
+    )(*[s] * blocks, *[w] * blocks, *[pat] * blocks, b)
+
+
+def mix_kernel(s_ref, w_ref, pat_ref, fwd_ref, bwd_ref, sel_ref, p_ref, v_ref, y_ref, left_s, left_w, pf):
+    layers, n = s_ref.shape[0], s_ref.shape[3]
+    npat, rows = pat_ref.shape[0], pat_ref.shape[2]
+    size = 8 * layers
+    p, g = pl.program_id(0), pl.program_id(1)
+
+    @pl.when((p == 0) & (g == 0))
+    def _():
+        def spread(matrix, count):
+            down = lax.broadcasted_iota(jnp.int32, (size, layers), 0) % layers
+            down = (down == lax.broadcasted_iota(jnp.int32, (size, layers), 1)).astype(F32).astype(jnp.bfloat16)
+            over = lax.broadcasted_iota(jnp.int32, (count, 8 * count), 1) // 8
+            over = (over == lax.broadcasted_iota(jnp.int32, (count, 8 * count), 0)).astype(F32).astype(jnp.bfloat16)
+            x = jnp.dot(down, matrix, preferred_element_type=F32).astype(jnp.bfloat16)
+            x = jnp.dot(x, over, preferred_element_type=F32)
+            same = lax.broadcasted_iota(jnp.int32, x.shape, 0) // layers
+            same = same == lax.broadcasted_iota(jnp.int32, x.shape, 1) % 8
+            return jnp.where(same, x, 0.0).astype(jnp.bfloat16)
+
+        def parts(ref):
+            return spread(ref[:, 0:layers], layers), spread(ref[:, layers : 2 * layers], layers)
+
+        eye = lax.broadcasted_iota(jnp.int32, (layers, layers), 0) == lax.broadcasted_iota(
+            jnp.int32, (layers, layers), 1
+        )
+        thirty = spread(jnp.where(eye, 30.0, 0.0).astype(jnp.bfloat16), layers)
+        high, low = parts(fwd_ref)
+        none = jnp.zeros((size, size), jnp.bfloat16)
+        pattern = spread(sel_ref[...], 8)
+        left_s[0:size, :] = jnp.concatenate([high, high, low, none[:, 0:64]], axis=1)
+        left_s[size:, :] = jnp.concatenate([thirty, thirty, none, pattern], axis=1)
+        high, low = parts(bwd_ref)
+        left_w[...] = jnp.concatenate([high, high, low], axis=1)
+
+    @pl.when(g == 0)
+    def _():
+        pf[...] = jnp.zeros(pf.shape, F32)
+        pf[0:npat] = pat_ref[:, 0].astype(F32)
+
+    def pieces(x):
+        hi = x.astype(jnp.bfloat16)
+        return hi, (x - hi.astype(F32)).astype(jnp.bfloat16)
+
+    step = min(n, 256)
+    for at in range(0, n, step):
+        cut = slice(at, at + step)
+        hi, lo = pieces(s_ref[:, 0, :, cut].reshape(size, step))
+        f = pf[:, pl.ds(pl.multiple_of(8 * g, 8), 8), cut].reshape(64, step).astype(jnp.bfloat16)
+        both = jnp.dot(left_s[...], jnp.concatenate([hi, lo, hi, f], axis=0), preferred_element_type=F32)
+        p_ref[0, :, :, cut] = both[0:size].reshape(8, layers, step)
+        y_ref[0, :, :, cut] = both[size:].reshape(8, layers, step)
+        hi, lo = pieces(w_ref[:, 0, :, cut].reshape(size, step))
+        v = jnp.dot(left_w[...], jnp.concatenate([hi, lo, hi], axis=0), preferred_element_type=F32)
+        v_ref[0, :, :, cut] = v.reshape(8, layers, step)
 
 
 def mix_all(s, w, pat, fwd, bwd, sel):
     layers, panels, rows, n = s.shape
     npat = pat.shape[0]
-    full = lambda x: pl.BlockSpec(x.shape, lambda p, c: (0,) * x.ndim)
-    part = lambda size: pl.BlockSpec((size, 1, rows, LANES), lambda p, c: (0, p, 0, c))
-    out = pl.BlockSpec((1, rows, layers, LANES), lambda p, c: (p, 0, 0, c))
+    full = lambda x: pl.BlockSpec(x.shape, lambda p, g: (0,) * x.ndim)
+    part = pl.BlockSpec((layers, 1, 8, n), lambda p, g: (0, p, g, 0))
+    out = pl.BlockSpec((1, 8, layers, n), lambda p, g: (p, g, 0, 0))
     size = layers * panels * rows * n * 4
+    wide = 8 * layers
     return pl.pallas_call(
         mix_kernel,
-        grid=(panels, n // LANES),
-        in_specs=[part(layers), part(layers), part(npat), full(fwd), full(bwd), full(sel)],
+        grid=(panels, rows // 8),
+        in_specs=[part, part, pl.BlockSpec((npat, 1, rows, n), lambda p, g: (0, p, 0, 0)), full(fwd), full(bwd), full(sel)],
         out_specs=[out] * 3,
         out_shape=[jax.ShapeDtypeStruct((panels, rows, layers, n), F32)] * 3,
-        scratch_shapes=[pltpu.VMEM((8, 1, rows, LANES), F32)],
-        compiler_params=pltpu.CompilerParams(vmem_limit_bytes=48 * 1024 * 1024),
+        scratch_shapes=[
+            pltpu.VMEM((2 * wide, 3 * wide + 64), jnp.bfloat16),
+            pltpu.VMEM((wide, 3 * wide), jnp.bfloat16),
+            pltpu.VMEM((8, rows, n), F32),
+        ],
+        compiler_params=pltpu.CompilerParams(vmem_limit_bytes=VMEM),
         cost_estimate=pl.CostEstimate(flops=size * 48, bytes_accessed=5 * size, transcendentals=0),
         name="mix",
     )(s, w, pat, fwd, bwd, sel)
@@ -215,7 +277,7 @@
 
 def halo_kernel(
     tiles, layers, rows,
-    west_ref, east_ref, em_ref, mm_ref, mu_ref, md_ref, aa_ref, fwd_ref, bwd_ref, sel_ref,
+    west_ref, east_ref, em_ref, mm_ref, aa_ref, fwd_ref, bwd_ref, sel_ref,
     hrp_ref, hrv_ref, hry_ref, hrb_ref, hlp_ref, hlv_ref, hly_ref, hlb_ref, hcp_ref, hcv_ref, hcb_ref,
     line,
 ):
@@ -279,7 +341,7 @@
         collect(of, (5, 3), 3, True)
 
     def force(x):
-        return 3.0 * x[0:layers] + STEP_FACTOR * jnp.dot(
+        return (3.0 / STEP_FACTOR) * x[0:layers] + jnp.dot(
             sel, x[2 * layers : CH].astype(jnp.bfloat16), preferred_element_type=F32
         )
 
@@ -306,6 +368,10 @@
     )
     at_end = lane == LANES - 1
     pad = jnp.zeros((LANES - 8, LANES), F32)
+    mirrored = [
+        jnp.concatenate([aa_ref[u, CH:, :], pad], axis=0).T[0:CH]
+        for u in (jnp.minimum(tiles - place, tiles - 1), jnp.maximum(tiles - 2 - place, 0))
+    ]
     for p in range(panels):
         x = columns[p]
         hlp_ref[p] = mix(fwd, x[0:layers])
@@ -318,17 +384,15 @@
         for edge in range(2):
             at = 1 + edge
             at_cut = lambda q, block: line[q, at, :, block * LANES : (block + 1) * LANES]
-            cells = (1, 2) if edge == 0 else (4 * (rows - 1) + 1, 4 * (rows - 1) + 2)
-            pick = jnp.where(at_end, cells[1], cells[0])
-            other = mu_ref if edge == 0 else md_ref
+            beside = lambda k: lane_gather(mirrored[edge], jnp.where(at_end, 5 + 2 * k, 4 + 2 * k))
             if p == 0:
                 inner = jnp.where(at_end, at_cut(5, blocks - 1), at_cut(4, 0))
             elif p == 2:
-                inner = lane_gather(other[1], pick)
+                inner = beside(1)
             elif p == 4:
-                inner = jnp.where(at_end, at_cut(0, blocks - 1), lane_gather(other[0], pick))
+                inner = jnp.where(at_end, at_cut(0, blocks - 1), beside(0))
             elif p == 5:
-                inner = jnp.where(at_end, lane_gather(other[0], pick), at_cut(0, 0))
+                inner = jnp.where(at_end, beside(0), at_cut(0, 0))
             else:
                 inner = lane_gather(turned, jnp.where(at_end, 2 * edge, 2 * edge + 1))
             own_row = 0 if edge == 0 else rows - 1
@@ -345,7 +409,7 @@
                 hcb_ref[p, slot] = jnp.broadcast_to(value[CH - 4 : CH - 3], (8, LANES))
 
 
-def halos(tiles, layers, rows, west, east, em, mm, mu, md, aa, fwd, bwd, sel):
+def halos(tiles, layers, rows, west, east, em, mm, aa, fwd, bwd, sel):
     panels, n = west.shape[0], west.shape[3]
     shapes = [
         (panels, 4, layers, n), (panels, 4, layers, n), (panels, 2, layers, n), (panels, 8, n),
@@ -356,9 +420,9 @@
         functools.partial(halo_kernel, tiles, layers, rows),
         out_shape=[jax.ShapeDtypeStruct(s, F32) for s in shapes],
         scratch_shapes=[pltpu.VMEM((panels, 4, CH, n), F32)],
-        compiler_params=pltpu.CompilerParams(vmem_limit_bytes=48 * 1024 * 1024),
+        compiler_params=pltpu.CompilerParams(vmem_limit_bytes=VMEM),
         name="halos",
-    )(west, east, em, mm, mu, md, aa, fwd, bwd, sel)
+    )(west, east, em, mm, aa, fwd, bwd, sel)
 
 
 def main_kernel(
@@ -395,7 +459,6 @@
         return pltpu.roll(x, 1, 1)
 
     edges_p, edges_v, edges_y, edges_b = hlp[0], hlv[0], hly[0], hlb[0]
-    half_step = 0.5 * STEP_FACTOR
     zero = jnp.zeros((8, LANES), F32)
 
     def depth_halo(k, tail):
@@ -404,10 +467,10 @@
     d_m2, d_m1 = depth_halo(0, zero), depth_halo(1, hcb[0, 1])
     d_p0, d_p1 = depth_halo(2, hcb[0, 3]), depth_halo(3, zero)
     j_m1, j_p0 = depth_halo(1, hcb[0, 0]), depth_halo(2, hcb[0, 2])
-    bi[0] = half_step * (d_m2 + d_m1)
-    bi[rows + 2] = half_step * (d_p0 + d_p1)
-    bj[0] = half_step * (j_m1 + shift_next(j_m1))
-    bj[rows + 1] = half_step * (j_p0 + shift_next(j_p0))
+    bi[0] = 0.5 * (d_m2 + d_m1)
+    bi[rows + 2] = 0.5 * (d_p0 + d_p1)
+    bj[0] = 0.5 * (j_m1 + shift_next(j_m1))
+    bj[rows + 1] = 0.5 * (j_p0 + shift_next(j_p0))
     last = d_m1
     for r in range(rows):
         sp[r + 2, :, 0:n] = p_ref[0, r]
@@ -416,10 +479,10 @@
         sv[r + 2, :, n:wide] = tail_of(edges_v, r)
         ty[r] = tail_of(edges_y, r)
         here = jnp.concatenate([jnp.broadcast_to(b_ref[0, r : r + 1, :], (8, n)), tail_of(edges_b, r)], axis=1)
-        bi[r + 1] = half_step * (last + here)
-        bj[r + 1] = half_step * (here + shift_next(here))
+        bi[r + 1] = 0.5 * (last + here)
+        bj[r + 1] = 0.5 * (here + shift_next(here))
         last = here
-    bi[rows + 1] = half_step * (last + d_p0)
+    bi[rows + 1] = 0.5 * (last + d_p0)
 
     def lap(ref, at, flat, bases, outs, by_i, by_j, count):
         for h in range(halves):
@@ -500,20 +563,20 @@
     rest = x - hi.astype(F32)
     lo = rest.astype(jnp.bfloat16)
     total = jnp.dot(ones, hi, preferred_element_type=F32) + jnp.dot(ones, lo, preferred_element_type=F32)
-    g_ref[0] = (-half_step * scale) * total
-
-
-def main(scale, fields, depth, halo):
-    panels, rows, layers, n = fields[0].shape
+    g_ref[0] = (-0.5 * STEP_FACTOR * STEP_FACTOR * scale) * total
+
+
+def main(scale, begin, count, fields, depth, halo):
+    _, rows, layers, n = fields[0].shape
     wide = n + LANES
-    block = lambda x: pl.BlockSpec((1,) + x.shape[1:], lambda p: (p,) + (0,) * (x.ndim - 1))
+    block = lambda x: pl.BlockSpec((1,) + x.shape[1:], lambda p: (p + begin,) + (0,) * (x.ndim - 1))
     operands = [*fields, depth, *halo]
     return pl.pallas_call(
         functools.partial(main_kernel, layers, scale),
-        grid=(panels,),
+        grid=(count,),
         in_specs=[block(x) for x in operands],
         out_specs=pl.BlockSpec((1, rows, n), lambda p: (p, 0, 0)),
-        out_shape=jax.ShapeDtypeStruct((panels, rows, n), F32),
+        out_shape=jax.ShapeDtypeStruct((count, rows, n), F32),
         scratch_shapes=[
             pltpu.VMEM((rows + 6, layers, wide), F32),
             pltpu.VMEM((rows + 6, layers, wide), F32),
@@ -528,7 +591,10 @@
             pltpu.VMEM((rows + 2, 8, wide), F32),
             pltpu.VMEM((rows, 8, n), F32),
         ],
-        compiler_params=pltpu.CompilerParams(vmem_limit_bytes=48 * 1024 * 1024),
+        compiler_params=pltpu.CompilerParams(vmem_limit_bytes=VMEM),
+        cost_estimate=pl.CostEstimate(
+            flops=count * rows * layers * wide * 60, bytes_accessed=count * rows * layers * n * 16, transcendentals=0
+        ),
         name="main",
     )(*operands)
 
@@ -552,15 +618,17 @@
     west = lax.ppermute(high, "tile", ring)
     east = lax.ppermute(low, "tile", [(j, i) for i, j in ring])
     mirrored = lax.ppermute(mm, "tile", [(i, tiles - 1 - i) for i in range(tiles)])
-    above = lax.ppermute(mm[0:2], "tile", [(i, tiles - i) for i in range(1, tiles)])
-    below = lax.ppermute(mm[0:2], "tile", [(i, tiles - 2 - i) for i in range(tiles - 1)])
     windows = lax.all_to_all(aa, "tile", 0, 0, tiled=True)
     fields = mix_all(initial_state, weights, patterns, fwd, bwd, sel)
-    halo = halos(tiles, layers, rows, west, east, em, mirrored, above, below, windows, fwd, bwd, sel)
-    gradient = main(1.0 / samples, fields, bathymetry, halo)
-    if samples == 2:
-        return gradient + lax.ppermute(gradient, "samp", [(0, 1), (1, 0)])
-    return lax.psum(gradient, "samp")
+    halo = halos(tiles, layers, rows, west, east, em, mirrored, windows, fwd, bwd, sel)
+    totals = []
+    for begin, end in ((0, panels // 2), (panels // 2, panels)):
+        part = main(1.0 / samples, begin, end - begin, fields, bathymetry, halo)
+        if samples == 2:
+            totals.append(part + lax.ppermute(part, "samp", [(0, 1), (1, 0)]))
+        else:
+            totals.append(lax.psum(part, "samp"))
+    return jnp.concatenate(totals, axis=0)
 
 
 def solution(mesh):

time: 127 us -> 109 us (0.86)
  Pallas kernels: 89 us -> 81.3 us
  starting transfers between devices: 21 us -> 15.6 us
  local copies, waits for them, and re-layouts: 5.3 us -> 1.65 us
  waiting for transfers between devices: 9.32 us -> 6.54 us
  other arithmetic: 0.98 us -> 3.14 us
    pallas_call x3 -> x4, Pallas kernels: 86.8 us -> 77 us  [the longest x2 45.4 us: main(): pl.pallas_call(functools.partial(main_kernel, layers, scale), grid=(count...]
    ppermute x3 -> x2, starting transfers between devices: 6.01 us -> 2.16 us  [body(): totals.append(part + lax.ppermute(part, 'samp', [(0, 1), (1, 0)]))]
    ppermute x3 -> x2, waiting for transfers between devices: 9.31 us -> 6.53 us  [body(): totals.append(part + lax.ppermute(part, 'samp', [(0, 1), (1, 0)]))]
    all_to_all x1, starting transfers between devices: 6.09 us -> 3.55 us  [body(): windows = lax.all_to_all(aa, 'tile', 0, 0, tiled=True)]
    unnamed x17 -> x15, local copies, waits for them, and re-layouts: 3.74 us -> 1.48 us
    pallas_call x1, Pallas kernels: 2.19 us -> 4.28 us  [halos(): pl.pallas_call(functools.partial(halo_kernel, tiles, layers, rows), out_s...]
    slice x1 -> x0, local copies, waits for them, and re-layouts: 1.39 us -> none  [body(): mm[0:2]]
  transfers between devices with their start and end apart: 7 -> 6, of which waited for: 1 -> 1; matrix products, arithmetic and copies ran while one was open for 1% -> 2% of each run, Pallas kernels for 19% -> 42%
where the time goes in v2:
time: 109 us; the launch traced here: 108 us
  Pallas kernels  81.3 us (75%)
  starting transfers between devices  15.6 us (14%)
  waiting for transfers between devices  6.54 us (6%)
  other arithmetic  3.14 us (3%)
  local copies, waits for them, and re-layouts  1.65 us (2%)
    pallas_call x2, Pallas kernels, main(): pl.pallas_call(functools.partial(main_kernel, layers, scale), grid=(count...  45.4 us
    pallas_call x1, Pallas kernels, mix_all(): pl.pallas_call(mix_kernel, grid=(panels, rows // 8), in_specs=[part, part...  22.4 us
    pallas_call x1, Pallas kernels, pack(): pl.pallas_call(functools.partial(pack_kernel, tiles, blocks, layers, npat...  9.16 us
    ppermute x2, waiting for transfers between devices, body(): totals.append(part + lax.ppermute(part, 'samp', [(0, 1), (1, 0)]))  6.53 us
    ppermute x1, starting transfers between devices, body(): east = lax.ppermute(low, 'tile', [(j, i) for i, j in ring])  5.53 us
    ppermute x1, starting transfers between devices, body(): lax.ppermute(mm, 'tile', [(i, tiles - 1 - i) for i in range(tiles)])  4.32 us
    pallas_call x1, Pallas kernels, halos(): pl.pallas_call(functools.partial(halo_kernel, tiles, layers, rows), out_s...  4.28 us
    all_to_all x1, starting transfers between devices, body(): windows = lax.all_to_all(aa, 'tile', 0, 0, tiled=True)  3.55 us
  transfers between devices with their start and end apart: 6, of which 1 were waited for; matrix products, arithmetic and copies ran while one was open for 2% of the time, Pallas kernels for 42%

profile of v2, /device:TPU:0, one launch (start us, length us, event | category | flops | bytes accessed | tf_op | source)
XLA Modules:
  0.0 108.3 jit_solution(16760992961074368508)
XLA Ops:
  0.0 0.0 copy-start.5
  0.0 0.0 copy-start.6
  0.0 9.2 %pack.1 = (f32[6,40,128]{2,1,0:T(8,128)}, f32[6,2,40,512]{3,2,1,0:T(8,128)}, f32[6,2,40,512]{3,2,1,0:T(8,128)}, f32[3,40,128]{2,1,0:T(8,128)}, f32[16,48,128]{2,1,0:T(8,128)}) custom-call(f32[16,6,32,512]{3,2,1,0:T(8,128)} %refs_3_.1, f32[16,6,32,512]{3,2,1,0:T(8,128)} %refs_3_.1, f32[16,6,32,512]{3,2,1,0:T(8,128)} %refs_3_.1, f32[16,6,32,512]{3,2,1,0:T(8,128)} %refs_3_.1, ...), custom_call_target="tpu_custom_call" | custom-call | tf_op jit(solution)/shard_map/pack/pallas_call | solution.py:172
  9.2 0.1 collective-permute-start
  9.2 5.5 %collective-permute-start.1 = (f32[6,2,40,512]{3,2,1,0:T(8,128)}, f32[6,2,40,512]{3,2,1,0:T(8,128)S(1)}, u32[]{:S(2)}, u32[]{:S(2)}) collective-permute-start(f32[6,2,40,512]{3,2,1,0:T(8,128)} %get-tuple-element.28), channel_id=1, source_target_pairs={{2,0},{4,2},{6,4},{8,6},{10,8},{12,10},{14,12},{16,14},{18,16},{20... | collective-permute-start | bytes 2949128 | tf_op jit(solution)/shard_map/ppermute | solution.py:619
  14.8 3.6 %all-to-all-start = ((f32[16,48,128]{2,1,0:T(8,128)}), f32[16,48,128]{2,1,0:T(8,128)S(1)}, u32[]{:S(2)}, u32[]{:S(2)}) async-start(f32[16,48,128]{2,1,0:T(8,128)} %get-tuple-element.31), calls=%async_computation | async-start | bytes 786432 | tf_op jit(solution)/shard_map/all_to_all | solution.py:621
  18.3 4.3 %collective-permute-start.2 = (f32[3,40,128]{2,1,0:T(8,128)}, f32[3,40,128]{2,1,0:T(8,128)S(1)}, u32[]{:S(2)}, u32[]{:S(2)}) collective-permute-start(f32[3,40,128]{2,1,0:T(8,128)} %get-tuple-element.30), channel_id=1, source_target_pairs={{0,30},{2,28},{4,26},{6,24},{8,22},{10,20},{12,18},{14,16},{16,14}... | collective-permute-start | bytes 184328 | tf_op jit(solution)/shard_map/ppermute | solution.py:620
  22.6 0.0 copy-done.5
  22.6 0.1 copy.10
  22.7 0.1 copy.12
  22.8 0.1 copy.11
  22.9 0.0 copy-done.6
  22.9 0.7 fusion.2.sel_ref
  23.6 0.7 pad_maximum_fusion.1
  24.3 22.4 %mix.1 = (f32[6,32,16,512]{3,2,1,0:T(8,128)}, f32[6,32,16,512]{3,2,1,0:T(8,128)}, f32[6,32,16,512]{3,2,1,0:T(8,128)}) custom-call(f32[16,6,32,512]{3,2,1,0:T(8,128)} %refs_3_.1, f32[16,6,32,512]{3,2,1,0:T(8,128)} %bitcast.9, bf16[4,6,32,512]{3,2,1,0:T(8,128)(2,1)} %refs_11_.1, bf16[16,48]{1,0:T(8,128)(2,1)} %get-tuple-element.47.fwd_ref, ...), custom_call_target="tpu_custom_call" | custom-call | flops 301989888 | bytes 31457280 | tf_op jit(solution)/shard_map/mix/pallas_call | solution.py:261
  46.7 0.0 collective-permute-done.2.mm_ref
  46.7 0.0 copy-start.4
  46.7 0.0 all-to-all-done.aa_ref
  46.7 0.0 copy-start
  46.7 0.0 collective-permute-done.west_ref
  46.7 0.0 copy-start.1
  46.7 0.0 collective-permute-done.1.east_ref
  46.8 0.0 copy-start.2
  46.8 0.5 copy-done.4
  47.3 0.2 copy-done
  47.5 0.3 copy-done.1
  47.8 0.4 copy-done.2
  48.2 4.3 %halos.1 = (f32[6,4,16,512]{3,2,1,0:T(8,128)}, f32[6,4,16,512]{3,2,1,0:T(8,128)}, f32[6,2,16,512]{3,2,1,0:T(8,128)}, f32[6,8,512]{2,1,0:T(8,128)}, f32[6,16,128]...) custom-call(f32[6,2,40,512]{3,2,1,0:T(8,128)} %copy-done.1, ...), custom_call_target="tpu_custom_call" | custom-call | tf_op jit(solution)/shard_map/halos/pallas_call | solution.py:419
  52.4 22.7 %main.2 = f32[3,32,512]{2,1,0:T(8,128)} custom-call(f32[6,32,16,512]{3,2,1,0:T(8,128)} %get-tuple-element.24.p_ref, f32[6,32,16,512]{3,2,1,0:T(8,128)} %get-tuple-element.25.v_ref, f32[6,32,16,512]{3,2,1,0:T(8,128)} %get-tuple-element.26.y_ref, f32[6,32,512]{2,1,0:T(8,128)} %b_ref.3, f32[6,4,16,512]{3,2,1,0:T(8,128)} %get-tuple-element.32.hrp, ...), custom_call_target="tpu_custom_call" | custom-call | flops 58982400 | bytes 12582912 | tf_op jit(solution)/shard_map/main/pallas_call | solution.py:574
  75.2 0.0 copy-start.3
  75.2 1.9 %collective-permute-start.3 = (f32[3,32,512]{2,1,0:T(8,128)}, f32[3,32,512]{2,1,0:T(8,128)S(1)}, u32[]{:S(2)}, u32[]{:S(2)}) collective-permute-start(f32[3,32,512]{2,1,0:T(8,128)} %main.2), channel_id=1, source_target_pairs={{0,1},{1,0},{2,3},{3,2},{4,5},{5,4},{6,7},{7,6},{8,9},{9,8},{10,11... | collective-permute-start | bytes 589832 | tf_op jit(solution)/shard_map/ppermute | solution.py:628
  77.1 22.7 %main.3 = f32[3,32,512]{2,1,0:T(8,128)} custom-call(f32[6,32,16,512]{3,2,1,0:T(8,128)} %get-tuple-element.24.p_ref, f32[6,32,16,512]{3,2,1,0:T(8,128)} %get-tuple-element.25.v_ref, f32[6,32,16,512]{3,2,1,0:T(8,128)} %get-tuple-element.26.y_ref, f32[6,32,512]{2,1,0:T(8,128)} %b_ref.3, f32[6,4,16,512]{3,2,1,0:T(8,128)} %get-tuple-element.32.hrp, ...), custom_call_target="tpu_custom_call" | custom-call | flops 58982400 | bytes 12582912 | tf_op jit(solution)/shard_map/main/pallas_call | solution.py:574
  99.8 0.2 collective-permute-start.4
  100.0 0.0 collective-permute-done.3
  100.0 0.0 copy-done.3
  100.1 6.5 %collective-permute-done.4 = f32[3,32,512]{2,1,0:T(8,128)S(1)} collective-permute-done((f32[3,32,512]{2,1,0:T(8,128)}, f32[3,32,512]{2,1,0:T(8,128)S(1)}, u32[]{:S(2)}, u32[]{:S(2)}) %collective-permute-start.4) | collective-permute-done | bytes 196640 | tf_op jit(solution)/shard_map/ppermute | solution.py:628
  106.6 1.0 add.11
  107.6 0.8 pad_maximum_fusion
  (3 shorter events, 0.0 us)
Async XLA Ops:
  0.0 22.6 %copy-start.5 = (f32[16,16]{1,0:T(8,128)S(1)}, f32[16,16]{1,0:T(8,128)}, u32[]{:S(2)}) copy-start(f32[16,16]{1,0:T(8,128)} %param.10) | copy-start | bytes 3076
  0.0 22.9 %copy-start.6 = (s32[1,16]{1,0:T(1,128)S(1)}, s32[1,16]{1,0:T(1,128)}, u32[]{:S(2)}) copy-start(s32[1,16]{1,0:T(1,128)} %param.9) | copy-start | bytes 196
  9.2 37.6 %collective-permute-start = (f32[6,2,40,512]{3,2,1,0:T(8,128)}, f32[6,2,40,512]{3,2,1,0:T(8,128)S(1)}, u32[]{:S(2)}, u32[]{:S(2)}) collective-permute-start(f32[6,2,40,512]{3,2,1,0:T(8,128)} %get-tuple-element.27), channel_id=1, source_target_pairs={{0,2},{2,4},{4,6},{6,8},{8,10},{10,12},{12,14},{14,16},{16,18},{18... | collective-permute-start | bytes 2949128 | tf_op jit(solution)/shard_map/ppermute | solution.py:618
  9.2 37.5 %collective-permute-start.1 = (f32[6,2,40,512]{3,2,1,0:T(8,128)}, f32[6,2,40,512]{3,2,1,0:T(8,128)S(1)}, u32[]{:S(2)}, u32[]{:S(2)}) collective-permute-start(f32[6,2,40,512]{3,2,1,0:T(8,128)} %get-tuple-element.28), channel_id=1, source_target_pairs={{2,0},{4,2},{6,4},{8,6},{10,8},{12,10},{14,12},{16,14},{18,16},{20... | collective-permute-start | bytes 2949128 | tf_op jit(solution)/shard_map/ppermute | solution.py:619
  14.8 31.9 %all-to-all-start = ((f32[16,48,128]{2,1,0:T(8,128)}), f32[16,48,128]{2,1,0:T(8,128)S(1)}, u32[]{:S(2)}, u32[]{:S(2)}) async-start(f32[16,48,128]{2,1,0:T(8,128)} %get-tuple-element.31), calls=%async_computation | async-start | bytes 786432 | tf_op jit(solution)/shard_map/all_to_all | solution.py:621
  18.3 28.4 %collective-permute-start.2 = (f32[3,40,128]{2,1,0:T(8,128)}, f32[3,40,128]{2,1,0:T(8,128)S(1)}, u32[]{:S(2)}, u32[]{:S(2)}) collective-permute-start(f32[3,40,128]{2,1,0:T(8,128)} %get-tuple-element.30), channel_id=1, source_target_pairs={{0,30},{2,28},{4,26},{6,24},{8,22},{10,20},{12,18},{14,16},{16,14}... | collective-permute-start | bytes 184328 | tf_op jit(solution)/shard_map/ppermute | solution.py:620
  46.7 0.6 copy-start.4
  46.7 0.8 copy-start
  46.7 1.1 copy-start.1
  46.8 1.4 %copy-start.2 = (f32[6,2,40,512]{3,2,1,0:T(8,128)}, f32[6,2,40,512]{3,2,1,0:T(8,128)S(1)}, u32[]{:S(2)}) copy-start(f32[6,2,40,512]{3,2,1,0:T(8,128)S(1)} %collective-permute-done.1.east_ref) | copy-start | bytes 2949124
  75.2 24.9 %copy-start.3 = (f32[3,32,512]{2,1,0:T(8,128)S(1)}, f32[3,32,512]{2,1,0:T(8,128)}, u32[]{:S(2)}) copy-start(f32[3,32,512]{2,1,0:T(8,128)} %main.2) | copy-start | bytes 589828
  75.2 24.9 %collective-permute-start.3 = (f32[3,32,512]{2,1,0:T(8,128)}, f32[3,32,512]{2,1,0:T(8,128)S(1)}, u32[]{:S(2)}, u32[]{:S(2)}) collective-permute-start(f32[3,32,512]{2,1,0:T(8,128)} %main.2), channel_id=1, source_target_pairs={{0,1},{1,0},{2,3},{3,2},{4,5},{5,4},{6,7},{7,6},{8,9},{9,8},{10,11... | collective-permute-start | bytes 589832 | tf_op jit(solution)/shard_map/ppermute | solution.py:628
  99.8 6.8 %collective-permute-start.4 = (f32[3,32,512]{2,1,0:T(8,128)}, f32[3,32,512]{2,1,0:T(8,128)S(1)}, u32[]{:S(2)}, u32[]{:S(2)}) collective-permute-start(f32[3,32,512]{2,1,0:T(8,128)} %main.3), channel_id=1, source_target_pairs={{0,1},{1,0},{2,3},{3,2},{4,5},{5,4},{6,7},{7,6},{8,9},{9,8},{10,11... | collective-permute-start | bytes 589832 | tf_op jit(solution)/shard_map/ppermute | solution.py:628

commit v3 on v2

--- a/solution.py
+++ b/solution.py
@@ -194,13 +194,12 @@
     )(*[s] * blocks, *[w] * blocks, *[pat] * blocks, b)
 
 
-def mix_kernel(s_ref, w_ref, pat_ref, fwd_ref, bwd_ref, sel_ref, p_ref, v_ref, y_ref, left_s, left_w, pf):
+def mix_kernel(s_ref, w_ref, pat_ref, fwd_ref, bwd_ref, sel_ref, p_ref, v_ref, y_ref, left_s, left_w, left_f, pf):
     layers, n = s_ref.shape[0], s_ref.shape[3]
     npat, rows = pat_ref.shape[0], pat_ref.shape[2]
     size = 8 * layers
-    p, g = pl.program_id(0), pl.program_id(1)
-
-    @pl.when((p == 0) & (g == 0))
+
+    @pl.when(pl.program_id(0) == 0)
     def _():
         def spread(matrix, count):
             down = lax.broadcasted_iota(jnp.int32, (size, layers), 0) % layers
@@ -221,52 +220,53 @@
         )
         thirty = spread(jnp.where(eye, 30.0, 0.0).astype(jnp.bfloat16), layers)
         high, low = parts(fwd_ref)
-        none = jnp.zeros((size, size), jnp.bfloat16)
-        pattern = spread(sel_ref[...], 8)
-        left_s[0:size, :] = jnp.concatenate([high, high, low, none[:, 0:64]], axis=1)
-        left_s[size:, :] = jnp.concatenate([thirty, thirty, none, pattern], axis=1)
-        high, low = parts(bwd_ref)
-        left_w[...] = jnp.concatenate([high, high, low], axis=1)
-
-    @pl.when(g == 0)
-    def _():
-        pf[...] = jnp.zeros(pf.shape, F32)
-        pf[0:npat] = pat_ref[:, 0].astype(F32)
+        for k, x in enumerate((high, low, thirty)):
+            left_s[k * size : (k + 1) * size, :] = jnp.concatenate([x, x], axis=1)
+        for k, x in enumerate(parts(bwd_ref)):
+            left_w[k * size : (k + 1) * size, :] = jnp.concatenate([x, x], axis=1)
+        left_f[...] = spread(sel_ref[...], 8)
+
+    pf[...] = jnp.zeros(pf.shape, F32)
+    pf[0:npat] = pat_ref[:, 0].astype(F32)
 
     def pieces(x):
         hi = x.astype(jnp.bfloat16)
-        return hi, (x - hi.astype(F32)).astype(jnp.bfloat16)
+        return jnp.concatenate([hi, (x - hi.astype(F32)).astype(jnp.bfloat16)], axis=0)
+
+    def dot(a, b):
+        return jnp.dot(a, b, preferred_element_type=F32)
 
     step = min(n, 256)
-    for at in range(0, n, step):
-        cut = slice(at, at + step)
-        hi, lo = pieces(s_ref[:, 0, :, cut].reshape(size, step))
-        f = pf[:, pl.ds(pl.multiple_of(8 * g, 8), 8), cut].reshape(64, step).astype(jnp.bfloat16)
-        both = jnp.dot(left_s[...], jnp.concatenate([hi, lo, hi, f], axis=0), preferred_element_type=F32)
-        p_ref[0, :, :, cut] = both[0:size].reshape(8, layers, step)
-        y_ref[0, :, :, cut] = both[size:].reshape(8, layers, step)
-        hi, lo = pieces(w_ref[:, 0, :, cut].reshape(size, step))
-        v = jnp.dot(left_w[...], jnp.concatenate([hi, lo, hi], axis=0), preferred_element_type=F32)
-        v_ref[0, :, :, cut] = v.reshape(8, layers, step)
+    for g in range(rows // 8):
+        own = slice(8 * g, 8 * g + 8)
+        for at in range(0, n, step):
+            cut = slice(at, at + step)
+            x = dot(left_s[...], pieces(s_ref[:, 0, own, cut].reshape(size, step)))
+            f = dot(left_f[...], pf[:, own, cut].reshape(64, step).astype(jnp.bfloat16))
+            p_ref[0, own, :, cut] = (x[0:size] + x[size : 2 * size]).reshape(8, layers, step)
+            y_ref[0, own, :, cut] = (x[2 * size :] + f).reshape(8, layers, step)
+            x = dot(left_w[...], pieces(w_ref[:, 0, own, cut].reshape(size, step)))
+            v_ref[0, own, :, cut] = (x[0:size] + x[size:]).reshape(8, layers, step)
 
 
 def mix_all(s, w, pat, fwd, bwd, sel):
     layers, panels, rows, n = s.shape
     npat = pat.shape[0]
-    full = lambda x: pl.BlockSpec(x.shape, lambda p, g: (0,) * x.ndim)
-    part = pl.BlockSpec((layers, 1, 8, n), lambda p, g: (0, p, g, 0))
-    out = pl.BlockSpec((1, 8, layers, n), lambda p, g: (p, g, 0, 0))
+    full = lambda x: pl.BlockSpec(x.shape, lambda p: (0,) * x.ndim)
+    part = lambda count: pl.BlockSpec((count, 1, rows, n), lambda p: (0, p, 0, 0))
+    out = pl.BlockSpec((1, rows, layers, n), lambda p: (p, 0, 0, 0))
     size = layers * panels * rows * n * 4
     wide = 8 * layers
     return pl.pallas_call(
         mix_kernel,
-        grid=(panels, rows // 8),
-        in_specs=[part, part, pl.BlockSpec((npat, 1, rows, n), lambda p, g: (0, p, 0, 0)), full(fwd), full(bwd), full(sel)],
+        grid=(panels,),
+        in_specs=[part(layers), part(layers), part(npat), full(fwd), full(bwd), full(sel)],
         out_specs=[out] * 3,
         out_shape=[jax.ShapeDtypeStruct((panels, rows, layers, n), F32)] * 3,
         scratch_shapes=[
-            pltpu.VMEM((2 * wide, 3 * wide + 64), jnp.bfloat16),
-            pltpu.VMEM((wide, 3 * wide), jnp.bfloat16),
+            pltpu.VMEM((3 * wide, 2 * wide), jnp.bfloat16),
+            pltpu.VMEM((2 * wide, 2 * wide), jnp.bfloat16),
+            pltpu.VMEM((wide, 64), jnp.bfloat16),
             pltpu.VMEM((8, rows, n), F32),
         ],
         compiler_params=pltpu.CompilerParams(vmem_limit_bytes=VMEM),
@@ -430,7 +430,7 @@
     p_ref, v_ref, y_ref, b_ref,
     hrp, hrv, hry, hrb, hlp, hlv, hly, hlb, hcp, hcv, hcb,
     g_ref,
-    sp, sv, sy, sz, ip, iv, jp, jv, ty, bi, bj, acc,
+    sp, sv, sy, sz, ip, iv, jp, jv, ty, depth, bi, bj, acc,
 ):
     rows, n = p_ref.shape[1], p_ref.shape[3]
     wide = n + LANES
@@ -458,48 +458,57 @@
     def shift_back(x):
         return pltpu.roll(x, 1, 1)
 
-    edges_p, edges_v, edges_y, edges_b = hlp[0], hlv[0], hly[0], hlb[0]
+    edges_p, edges_v, edges_y = hlp[0], hlv[0], hly[0]
     zero = jnp.zeros((8, LANES), F32)
-
-    def depth_halo(k, tail):
-        return jnp.concatenate([jnp.broadcast_to(hrb[0, k : k + 1, :], (8, n)), tail], axis=1)
-
-    d_m2, d_m1 = depth_halo(0, zero), depth_halo(1, hcb[0, 1])
-    d_p0, d_p1 = depth_halo(2, hcb[0, 3]), depth_halo(3, zero)
-    j_m1, j_p0 = depth_halo(1, hcb[0, 0]), depth_halo(2, hcb[0, 2])
-    bi[0] = 0.5 * (d_m2 + d_m1)
-    bi[rows + 2] = 0.5 * (d_p0 + d_p1)
-    bj[0] = 0.5 * (j_m1 + shift_next(j_m1))
-    bj[rows + 1] = 0.5 * (j_p0 + shift_next(j_p0))
-    last = d_m1
+    parts = [slice(c * LANES, (c + 1) * LANES) for c in range(wide // LANES)]
+
+    ln, row = lane_iota((rows, LANES)), lax.broadcasted_iota(jnp.int32, (rows, LANES), 0)
+    tails = lane_gather(jnp.broadcast_to(hlb[0, 0:1, :], (rows, LANES)), (ln + 4 * row + 2) % LANES)
+    depth[...] = jnp.zeros(depth.shape, F32)
+    depth[8 : 8 + rows, 0:n] = b_ref[0]
+    depth[8 : 8 + rows, n:wide] = tails
+    for at, k, corner in ((6, 0, None), (7, 1, 1), (8 + rows, 2, 3), (9 + rows, 3, None)):
+        depth[at : at + 1, 0:n] = hrb[0, k : k + 1, :]
+        if corner is not None:
+            depth[at : at + 1, n:wide] = hcb[0, corner, 0:1, :]
+    between_rows = 0.5 * (depth[0 : rows + 16, :] + depth[1 : rows + 17, :])
+    own = depth[8 : 8 + rows, :]
+    along_own = 0.5 * (own + shift_next(own))
+    for c, cut in enumerate(parts):
+        bi[c] = between_rows[:, cut]
+        bj[c, 8 : 8 + rows, :] = along_own[:, cut]
+    for at, k, corner in ((7, 1, 0), (8 + rows, 2, 2)):
+        x = jnp.concatenate([jnp.broadcast_to(hrb[0, k : k + 1, :], (8, n)), hcb[0, corner]], axis=1)
+        x = 0.5 * (x + shift_next(x))
+        for c, cut in enumerate(parts):
+            bj[c, at : at + 1, :] = x[0:1, cut]
+
+    def spread(ref, at):
+        return jnp.concatenate([ref[c, pl.ds(at, 8, stride=0), :] for c in range(len(parts))], axis=1)
+
     for r in range(rows):
         sp[r + 2, :, 0:n] = p_ref[0, r]
         sp[r + 2, :, n:wide] = tail_of(edges_p, r)
         sv[r + 2, :, 0:n] = v_ref[0, r]
         sv[r + 2, :, n:wide] = tail_of(edges_v, r)
         ty[r] = tail_of(edges_y, r)
-        here = jnp.concatenate([jnp.broadcast_to(b_ref[0, r : r + 1, :], (8, n)), tail_of(edges_b, r)], axis=1)
-        bi[r + 1] = 0.5 * (last + here)
-        bj[r + 1] = 0.5 * (here + shift_next(here))
-        last = here
-    bi[rows + 1] = 0.5 * (last + d_p0)
 
     def lap(ref, at, flat, bases, outs, by_i, by_j, count):
         for h in range(halves):
             part = slice(8 * h, 8 * h + 8)
             here = ref[at, part]
-            before = bi[at - 1] * (here - ref[at - 1, part])
+            before = spread(bi, at + 5) * (here - ref[at - 1, part])
             for u in range(count):
                 after_row = ref[at + u + 1, part]
                 step_i = after_row - here
                 if by_i is not None:
                     by_i[at + u - 1, part] = step_i[:, 0:n]
-                after = bi[at + u] * step_i
+                after = spread(bi, at + u + 6) * step_i
                 line = here if flat is None else ref[flat, part]
                 step_j = shift_next(line) - line
                 if by_j is not None:
                     by_j[at + u - 2, part] = step_j
-                along = bj[at + u - 1] * step_j
+                along = spread(bj, at + u + 6) * step_j
                 out = after - before + along - shift_back(along)
                 if bases is not None:
                     out = out + bases(u, part)
@@ -587,8 +596,9 @@
             pltpu.VMEM((rows, layers, wide), F32),
             pltpu.VMEM((rows, layers, wide), F32),
             pltpu.VMEM((rows, layers, LANES), F32),
-            pltpu.VMEM((rows + 3, 8, wide), F32),
-            pltpu.VMEM((rows + 2, 8, wide), F32),
+            pltpu.VMEM((rows + 24, wide), F32),
+            pltpu.VMEM((wide // LANES, rows + 16, LANES), F32),
+            pltpu.VMEM((wide // LANES, rows + 16, LANES), F32),
             pltpu.VMEM((rows, 8, n), F32),
         ],
         compiler_params=pltpu.CompilerParams(vmem_limit_bytes=VMEM),
@@ -622,7 +632,7 @@
     fields = mix_all(initial_state, weights, patterns, fwd, bwd, sel)
     halo = halos(tiles, layers, rows, west, east, em, mirrored, windows, fwd, bwd, sel)
     totals = []
-    for begin, end in ((0, panels // 2), (panels // 2, panels)):
+    for begin, end in ((0, panels - 1), (panels - 1, panels)):
         part = main(1.0 / samples, begin, end - begin, fields, bathymetry, halo)
         if samples == 2:
             totals.append(part + lax.ppermute(part, "samp", [(0, 1), (1, 0)]))

time: 109 us -> 99.7 us (0.915)
  Pallas kernels: 81.3 us -> 71.8 us
    pallas_call x1, Pallas kernels: 22.4 us -> 14.2 us  [mix_all(): pl.pallas_call(mix_kernel, grid=(panels,), in_specs=[part(layers), part(l...]
    all_to_all x1, waiting for transfers between devices: 0.01 us -> 3.09 us  [body(): windows = lax.all_to_all(aa, 'tile', 0, 0, tiled=True)]
    ppermute x2, waiting for transfers between devices: 6.53 us -> 3.94 us  [body(): totals.append(part + lax.ppermute(part, 'samp', [(0, 1), (1, 0)]))]
    pallas_call x2, Pallas kernels: 45.4 us -> 44.2 us  [main(): pl.pallas_call(functools.partial(main_kernel, layers, scale), grid=(count...]
  transfers between devices with their start and end apart: 6 -> 6, of which waited for: 1 -> 2; matrix products, arithmetic and copies ran while one was open for 2% -> 2% of each run, Pallas kernels for 42% -> 23%
where the time goes in v3:
time: 99.7 us; the launch traced here: 99.2 us
  Pallas kernels  71.8 us (72%)
  starting transfers between devices  15.6 us (16%)
  waiting for transfers between devices  7.05 us (7%)
  other arithmetic  3.06 us (3%)
  local copies, waits for them, and re-layouts  1.66 us (2%)
    pallas_call x2, Pallas kernels, main(): pl.pallas_call(functools.partial(main_kernel, layers, scale), grid=(count...  44.2 us
    pallas_call x1, Pallas kernels, mix_all(): pl.pallas_call(mix_kernel, grid=(panels,), in_specs=[part(layers), part(l...  14.2 us
    pallas_call x1, Pallas kernels, pack(): pl.pallas_call(functools.partial(pack_kernel, tiles, blocks, layers, npat...  9.16 us
    ppermute x1, starting transfers between devices, body(): east = lax.ppermute(low, 'tile', [(j, i) for i, j in ring])  5.53 us
    ppermute x1, starting transfers between devices, body(): lax.ppermute(mm, 'tile', [(i, tiles - 1 - i) for i in range(tiles)])  4.32 us
    pallas_call x1, Pallas kernels, halos(): pl.pallas_call(functools.partial(halo_kernel, tiles, layers, rows), out_s...  4.28 us
    ppermute x2, waiting for transfers between devices, body(): totals.append(part + lax.ppermute(part, 'samp', [(0, 1), (1, 0)]))  3.94 us
    all_to_all x1, starting transfers between devices, body(): windows = lax.all_to_all(aa, 'tile', 0, 0, tiled=True)  3.55 us
  transfers between devices with their start and end apart: 6, of which 2 were waited for; matrix products, arithmetic and copies ran while one was open for 2% of the time, Pallas kernels for 23%

profile of v3, /device:TPU:0, one launch (start us, length us, event | category | flops | bytes accessed | tf_op | source)
XLA Modules:
  0.0 99.2 jit_solution(7046439108152364321)
XLA Ops:
  0.0 0.0 copy-start.5
  0.0 0.0 copy-start.6
  0.0 9.2 %pack.1 = (f32[6,40,128]{2,1,0:T(8,128)}, f32[6,2,40,512]{3,2,1,0:T(8,128)}, f32[6,2,40,512]{3,2,1,0:T(8,128)}, f32[3,40,128]{2,1,0:T(8,128)}, f32[16,48,128]{2,1,0:T(8,128)}) custom-call(f32[16,6,32,512]{3,2,1,0:T(8,128)} %refs_3_.1, f32[16,6,32,512]{3,2,1,0:T(8,128)} %refs_3_.1, f32[16,6,32,512]{3,2,1,0:T(8,128)} %refs_3_.1, f32[16,6,32,512]{3,2,1,0:T(8,128)} %refs_3_.1, ...), custom_call_target="tpu_custom_call" | custom-call | tf_op jit(solution)/shard_map/pack/pallas_call | solution.py:172
  9.2 0.1 collective-permute-start
  9.2 5.5 %collective-permute-start.1 = (f32[6,2,40,512]{3,2,1,0:T(8,128)}, f32[6,2,40,512]{3,2,1,0:T(8,128)S(1)}, u32[]{:S(2)}, u32[]{:S(2)}) collective-permute-start(f32[6,2,40,512]{3,2,1,0:T(8,128)} %get-tuple-element.28), channel_id=1, source_target_pairs={{2,0},{4,2},{6,4},{8,6},{10,8},{12,10},{14,12},{16,14},{18,16},{20... | collective-permute-start | bytes 2949128 | tf_op jit(solution)/shard_map/ppermute | solution.py:629
  14.8 3.6 %all-to-all-start = ((f32[16,48,128]{2,1,0:T(8,128)}), f32[16,48,128]{2,1,0:T(8,128)S(1)}, u32[]{:S(2)}, u32[]{:S(2)}) async-start(f32[16,48,128]{2,1,0:T(8,128)} %get-tuple-element.31), calls=%async_computation | async-start | bytes 786432 | tf_op jit(solution)/shard_map/all_to_all | solution.py:631
  18.3 4.3 %collective-permute-start.2 = (f32[3,40,128]{2,1,0:T(8,128)}, f32[3,40,128]{2,1,0:T(8,128)S(1)}, u32[]{:S(2)}, u32[]{:S(2)}) collective-permute-start(f32[3,40,128]{2,1,0:T(8,128)} %get-tuple-element.30), channel_id=1, source_target_pairs={{0,30},{2,28},{4,26},{6,24},{8,22},{10,20},{12,18},{14,16},{16,14}... | collective-permute-start | bytes 184328 | tf_op jit(solution)/shard_map/ppermute | solution.py:630
  22.6 0.0 copy-done.5
  22.6 0.1 copy.10
  22.7 0.1 copy.12
  22.8 0.1 copy.11
  22.9 0.0 copy-done.6
  22.9 0.7 fusion.2.sel_ref
  23.6 0.7 pad_maximum_fusion.1
  24.3 14.2 %mix.1 = (f32[6,32,16,512]{3,2,1,0:T(8,128)}, f32[6,32,16,512]{3,2,1,0:T(8,128)}, f32[6,32,16,512]{3,2,1,0:T(8,128)}) custom-call(f32[16,6,32,512]{3,2,1,0:T(8,128)} %refs_3_.1, f32[16,6,32,512]{3,2,1,0:T(8,128)} %bitcast.9, bf16[4,6,32,512]{3,2,1,0:T(8,128)(2,1)} %refs_11_.1, bf16[16,48]{1,0:T(8,128)(2,1)} %get-tuple-element.47.fwd_ref, ...), custom_call_target="tpu_custom_call" | custom-call | flops 301989888 | bytes 31457280 | tf_op jit(solution)/shard_map/mix/pallas_call | solution.py:260
  38.5 0.0 collective-permute-done.2.mm_ref
  38.5 0.0 copy-start.4
  38.5 3.1 %all-to-all-done.aa_ref = f32[16,48,128]{2,1,0:T(8,128)S(1)} async-done(((f32[16,48,128]{2,1,0:T(8,128)}), f32[16,48,128]{2,1,0:T(8,128)S(1)}, u32[]{:S(2)}, u32[]{:S(2)}) %all-to-all-start) | async-done | bytes 393248 | tf_op jit(solution)/shard_map/all_to_all | solution.py:631
  41.6 0.0 copy-start
  41.6 0.0 collective-permute-done.west_ref
  41.6 0.0 copy-start.2
  41.6 0.0 collective-permute-done.1.east_ref
  41.6 0.0 copy-start.3
  41.6 0.0 copy-done.4
  41.6 0.7 copy-done
  42.3 0.3 copy-done.2
  42.7 0.4 copy-done.3
  43.0 4.3 %halos.1 = (f32[6,4,16,512]{3,2,1,0:T(8,128)}, f32[6,4,16,512]{3,2,1,0:T(8,128)}, f32[6,2,16,512]{3,2,1,0:T(8,128)}, f32[6,8,512]{2,1,0:T(8,128)}, f32[6,16,128]...) custom-call(f32[6,2,40,512]{3,2,1,0:T(8,128)} %copy-done.2, ...), custom_call_target="tpu_custom_call" | custom-call | tf_op jit(solution)/shard_map/halos/pallas_call | solution.py:419
  47.3 35.1 %main.2 = f32[5,32,512]{2,1,0:T(8,128)} custom-call(f32[6,32,16,512]{3,2,1,0:T(8,128)} %get-tuple-element.24.p_ref, f32[6,32,16,512]{3,2,1,0:T(8,128)} %get-tuple-element.25.v_ref, f32[6,32,16,512]{3,2,1,0:T(8,128)} %get-tuple-element.26.y_ref, f32[6,32,512]{2,1,0:T(8,128)} %b_ref.3, f32[6,4,16,512]{3,2,1,0:T(8,128)} %get-tuple-element.32.hrp, ...), custom_call_target="tpu_custom_call" | custom-call | flops 98304000 | bytes 20971520 | tf_op jit(solution)/shard_map/main/pallas_call | solution.py:583
  82.4 0.0 copy-start.1
  82.4 1.6 %collective-permute-start.3 = (f32[5,32,512]{2,1,0:T(8,128)}, f32[5,32,512]{2,1,0:T(8,128)S(1)}, u32[]{:S(2)}, u32[]{:S(2)}) collective-permute-start(f32[5,32,512]{2,1,0:T(8,128)} %main.2), channel_id=1, source_target_pairs={{0,1},{1,0},{2,3},{3,2},{4,5},{5,4},{6,7},{7,6},{8,9},{9,8},{10,11... | collective-permute-start | bytes 983048 | tf_op jit(solution)/shard_map/ppermute | solution.py:638
  84.0 9.1 %main.3 = f32[1,32,512]{2,1,0:T(8,128)} custom-call(f32[6,32,16,512]{3,2,1,0:T(8,128)} %get-tuple-element.24.p_ref, f32[6,32,16,512]{3,2,1,0:T(8,128)} %get-tuple-element.25.v_ref, f32[6,32,16,512]{3,2,1,0:T(8,128)} %get-tuple-element.26.y_ref, f32[6,32,512]{2,1,0:T(8,128)} %b_ref.3, f32[6,4,16,512]{3,2,1,0:T(8,128)} %get-tuple-element.32.hrp, ...), custom_call_target="tpu_custom_call" | custom-call | flops 19660800 | bytes 4194304 | tf_op jit(solution)/shard_map/main/pallas_call | solution.py:583
  93.0 0.5 collective-permute-start.4
  93.6 3.9 %collective-permute-done.4 = f32[1,32,512]{2,1,0:T(8,128)S(1)} collective-permute-done((f32[1,32,512]{2,1,0:T(8,128)}, f32[1,32,512]{2,1,0:T(8,128)S(1)}, u32[]{:S(2)}, u32[]{:S(2)}) %collective-permute-start.4) | collective-permute-done | bytes 65568 | tf_op jit(solution)/shard_map/ppermute | solution.py:638
  97.5 0.9 add.11
  98.4 0.0 collective-permute-done.3
  98.4 0.0 copy-done.1
  98.4 0.8 pad_maximum_fusion
  (3 shorter events, 0.1 us)
Async XLA Ops:
  0.0 22.6 %copy-start.5 = (f32[16,16]{1,0:T(8,128)S(1)}, f32[16,16]{1,0:T(8,128)}, u32[]{:S(2)}) copy-start(f32[16,16]{1,0:T(8,128)} %param.10) | copy-start | bytes 3076
  0.0 22.9 %copy-start.6 = (s32[1,16]{1,0:T(1,128)S(1)}, s32[1,16]{1,0:T(1,128)}, u32[]{:S(2)}) copy-start(s32[1,16]{1,0:T(1,128)} %param.9) | copy-start | bytes 196
  9.2 32.4 %collective-permute-start = (f32[6,2,40,512]{3,2,1,0:T(8,128)}, f32[6,2,40,512]{3,2,1,0:T(8,128)S(1)}, u32[]{:S(2)}, u32[]{:S(2)}) collective-permute-start(f32[6,2,40,512]{3,2,1,0:T(8,128)} %get-tuple-element.27), channel_id=1, source_target_pairs={{0,2},{2,4},{4,6},{6,8},{8,10},{10,12},{12,14},{14,16},{16,18},{18... | collective-permute-start | bytes 2949128 | tf_op jit(solution)/shard_map/ppermute | solution.py:628
  9.2 32.3 %collective-permute-start.1 = (f32[6,2,40,512]{3,2,1,0:T(8,128)}, f32[6,2,40,512]{3,2,1,0:T(8,128)S(1)}, u32[]{:S(2)}, u32[]{:S(2)}) collective-permute-start(f32[6,2,40,512]{3,2,1,0:T(8,128)} %get-tuple-element.28), channel_id=1, source_target_pairs={{2,0},{4,2},{6,4},{8,6},{10,8},{12,10},{14,12},{16,14},{18,16},{20... | collective-permute-start | bytes 2949128 | tf_op jit(solution)/shard_map/ppermute | solution.py:629
  14.8 26.8 %all-to-all-start = ((f32[16,48,128]{2,1,0:T(8,128)}), f32[16,48,128]{2,1,0:T(8,128)S(1)}, u32[]{:S(2)}, u32[]{:S(2)}) async-start(f32[16,48,128]{2,1,0:T(8,128)} %get-tuple-element.31), calls=%async_computation | async-start | bytes 786432 | tf_op jit(solution)/shard_map/all_to_all | solution.py:631
  18.3 20.1 %collective-permute-start.2 = (f32[3,40,128]{2,1,0:T(8,128)}, f32[3,40,128]{2,1,0:T(8,128)S(1)}, u32[]{:S(2)}, u32[]{:S(2)}) collective-permute-start(f32[3,40,128]{2,1,0:T(8,128)} %get-tuple-element.30), channel_id=1, source_target_pairs={{0,30},{2,28},{4,26},{6,24},{8,22},{10,20},{12,18},{14,16},{16,14}... | collective-permute-start | bytes 184328 | tf_op jit(solution)/shard_map/ppermute | solution.py:630
  38.5 3.1 %copy-start.4 = (f32[3,40,128]{2,1,0:T(8,128)}, f32[3,40,128]{2,1,0:T(8,128)S(1)}, u32[]{:S(2)}) copy-start(f32[3,40,128]{2,1,0:T(8,128)S(1)} %collective-permute-done.2.mm_ref) | copy-start | bytes 184324
  41.6 0.7 copy-start
  41.6 1.1 %copy-start.2 = (f32[6,2,40,512]{3,2,1,0:T(8,128)}, f32[6,2,40,512]{3,2,1,0:T(8,128)S(1)}, u32[]{:S(2)}) copy-start(f32[6,2,40,512]{3,2,1,0:T(8,128)S(1)} %collective-permute-done.west_ref) | copy-start | bytes 2949124
  41.6 1.4 %copy-start.3 = (f32[6,2,40,512]{3,2,1,0:T(8,128)}, f32[6,2,40,512]{3,2,1,0:T(8,128)S(1)}, u32[]{:S(2)}) copy-start(f32[6,2,40,512]{3,2,1,0:T(8,128)S(1)} %collective-permute-done.1.east_ref) | copy-start | bytes 2949124
  82.4 16.0 %copy-start.1 = (f32[5,32,512]{2,1,0:T(8,128)S(1)}, f32[5,32,512]{2,1,0:T(8,128)}, u32[]{:S(2)}) copy-start(f32[5,32,512]{2,1,0:T(8,128)} %main.2) | copy-start | bytes 983044
  82.4 16.0 %collective-permute-start.3 = (f32[5,32,512]{2,1,0:T(8,128)}, f32[5,32,512]{2,1,0:T(8,128)S(1)}, u32[]{:S(2)}, u32[]{:S(2)}) collective-permute-start(f32[5,32,512]{2,1,0:T(8,128)} %main.2), channel_id=1, source_target_pairs={{0,1},{1,0},{2,3},{3,2},{4,5},{5,4},{6,7},{7,6},{8,9},{9,8},{10,11... | collective-permute-start | bytes 983048 | tf_op jit(solution)/shard_map/ppermute | solution.py:638
  93.0 4.5 %collective-permute-start.4 = (f32[1,32,512]{2,1,0:T(8,128)}, f32[1,32,512]{2,1,0:T(8,128)S(1)}, u32[]{:S(2)}, u32[]{:S(2)}) collective-permute-start(f32[1,32,512]{2,1,0:T(8,128)} %main.3), channel_id=1, source_target_pairs={{0,1},{1,0},{2,3},{3,2},{4,5},{5,4},{6,7},{7,6},{8,9},{9,8},{10,11... | collective-permute-start | bytes 196616 | tf_op jit(solution)/shard_map/ppermute | solution.py:638

commit v4 on v3

--- a/solution.py
+++ b/solution.py
@@ -278,7 +278,7 @@
 def halo_kernel(
     tiles, layers, rows,
     west_ref, east_ref, em_ref, mm_ref, aa_ref, fwd_ref, bwd_ref, sel_ref,
-    hrp_ref, hrv_ref, hry_ref, hrb_ref, hlp_ref, hlv_ref, hly_ref, hlb_ref, hcp_ref, hcv_ref, hcb_ref,
+    hrp_ref, hrv_ref, hry_ref, hrb_ref, fix_ref,
     line,
 ):
     panels, n = west_ref.shape[0], west_ref.shape[3]
@@ -372,15 +372,28 @@
         jnp.concatenate([aa_ref[u, CH:, :], pad], axis=0).T[0:CH]
         for u in (jnp.minimum(tiles - place, tiles - 1), jnp.maximum(tiles - 2 - place, 0))
     ]
+    ln = lane_iota((layers, LANES))
+    k_of, r_of = ln % 4, ln // 4
+    end = ln == LANES - 1
+    depth_at = CH - 4
+
+    def mixed(x):
+        depth = jnp.broadcast_to(x[depth_at : depth_at + 1], (layers, LANES))
+        return mix(fwd, x[0:layers]), mix(bwd, x[layers : 2 * layers]), depth
+
+    def turn(x, by):
+        return pltpu.roll(x, by % LANES, 1)
+
+    def fold(x):
+        return jnp.sum(x, axis=0, keepdims=True)
+
     for p in range(panels):
-        x = columns[p]
-        hlp_ref[p] = mix(fwd, x[0:layers])
-        hlv_ref[p] = mix(bwd, x[layers : 2 * layers])
-        hly_ref[p] = force(x)
-        depth = x[CH - 4 : CH - 3]
-        hlb_ref[p] = jnp.broadcast_to(depth, (8, LANES))
+        raw = columns[p]
         if p in (1, 3):
             turned = jnp.concatenate([aa_ref[tiles - 1 if p == 1 else 0, CH:, :], pad], axis=0).T[0:CH]
+        outer, inner_own = mixed(raw), mixed(em_ref[p])
+        force_outer, force_own = force(raw), force(em_ref[p])
+        beyond = []
         for edge in range(2):
             at = 1 + edge
             at_cut = lambda q, block: line[q, at, :, block * LANES : (block + 1) * LANES]
@@ -396,25 +409,74 @@
             else:
                 inner = lane_gather(turned, jnp.where(at_end, 2 * edge, 2 * edge + 1))
             own_row = 0 if edge == 0 else rows - 1
-            across = pltpu.roll(x, (126 - 4 * own_row) % LANES, 1)
-            along = jnp.where(
-                at_end, pltpu.roll(at_cut(p, 0), LANES - 1, 1), pltpu.roll(at_cut(p, blocks - 1), 1, 1)
-            )
+            across = turn(raw, 126 - 4 * own_row)
+            along = jnp.where(at_end, turn(at_cut(p, 0), LANES - 1), turn(at_cut(p, blocks - 1), 1))
             corner = first if edge == 0 else final
-            for version, own in ((0, across), (1, along)):
-                value = jnp.where(corner, own, inner)
-                slot = 2 * edge + version
-                hcp_ref[p, slot] = mix(fwd, value[0:layers])
-                hcv_ref[p, slot] = mix(bwd, value[layers : 2 * layers])
-                hcb_ref[p, slot] = jnp.broadcast_to(value[CH - 4 : CH - 3], (8, LANES))
+            sideways = mixed(jnp.where(corner, across, inner))
+            onward = mixed(jnp.where(corner, along, inner))
+            head, tail = mixed(at_cut(p, 0)), mixed(at_cut(p, blocks - 1))
+            base = 4 * own_row
+            here = [
+                [turn(jnp.where(end, o, h), base + 2) for o, h in zip(onward, head)],
+                [turn(jnp.where(end, t, o), base + 2) for o, t in zip(onward, tail)],
+            ]
+            lateral = [[turn(x, base + 3) for x in sideways], [turn(x, base + 1) for x in sideways]]
+            beyond.append((here, lateral))
+        total = None
+        for right in range(2):
+            own_k = 1 if right else 2
+            halves = (inner_own, outer) if right else (outer, inner_own)
+            q, v, b = (jnp.where(k_of < 2, x, y) for x, y in zip(*halves))
+            y0 = jnp.where(k_of < 2, *((force_own, force_outer) if right else (force_outer, force_own)))
+            (here_m, lat_m), (here_p, lat_p) = [(h[right], t[right]) for h, t in beyond]
+            at_first, at_last, is_own = r_of == 0, r_of == rows - 1, k_of == own_k
+            bj = 0.5 * (b + turn(b, -1))
+            bi = 0.5 * (b + jnp.where(at_last, here_p[2], turn(b, -4)))
+            bi_m = 0.5 * (b + here_m[2])
+            laps, di, dj, extra, extra_m, extra_p, di_m = [], [], [], [], [], [], []
+            for f, x in enumerate((q, v)):
+                step_i = jnp.where(at_last, here_p[f], turn(x, -4)) - x
+                step_m = x - here_m[f]
+                step_j = turn(x, -1) - x
+                flow_i, flow_j = bi * step_i, bj * step_j
+                before = jnp.where(at_first, bi_m * step_m, turn(flow_i, 4))
+                laps.append(flow_i - before + flow_j - turn(flow_j, 1))
+                cross = flow_j if right else -turn(flow_j, 1)
+                extra.append(jnp.where(is_own, cross, 0.0))
+                extra_m.append(0.5 * (here_m[2] + lat_m[2]) * (lat_m[f] - here_m[f]))
+                extra_p.append(0.5 * (here_p[2] + lat_p[2]) * (lat_p[f] - here_p[f]))
+                di.append(step_i)
+                di_m.append(step_m)
+                dj.append(step_j)
+            y, z = y0 + laps[0], laps[1]
+            cross_edge = fold(dj[1] * (turn(y, -1) - y) + (turn(z, -1) - z) * dj[0])
+            after = [jnp.where(at_last, e, turn(x, -4)) for x, e in zip(extra, extra_p)]
+            along_i = fold(di[1] * (after[0] - extra[0]) + di[0] * (after[1] - extra[1]))
+            along_m = fold(di_m[1] * (extra[0] - extra_m[0]) + di_m[0] * (extra[1] - extra_m[1]))
+            if right:
+                inside = fold(dj[1] * turn(extra[0], -1) + dj[0] * turn(extra[1], -1))
+            else:
+                inside = -fold(dj[1] * extra[0] + dj[0] * extra[1])
+            k1, r1 = k_of[0:1], r_of[0:1]
+            whole = along_i + jnp.where(r1 == 0, along_m, turn(along_i, 4))
+            if right:
+                whole = whole + cross_edge + turn(inside, 1)
+                result = jnp.where(k1 == 1, whole, inside)
+            else:
+                whole = whole + turn(cross_edge, 1) + inside
+                result = jnp.where(k1 == 2, whole, turn(inside, 1))
+            if right:
+                total = jnp.where(k1 < 2, result, total)
+            else:
+                total = result
+        fix_ref[p] = jnp.broadcast_to(total, (8, LANES))
 
 
 def halos(tiles, layers, rows, west, east, em, mm, aa, fwd, bwd, sel):
     panels, n = west.shape[0], west.shape[3]
     shapes = [
         (panels, 4, layers, n), (panels, 4, layers, n), (panels, 2, layers, n), (panels, 8, n),
-        (panels, layers, LANES), (panels, layers, LANES), (panels, layers, LANES), (panels, 8, LANES),
-        (panels, 4, layers, LANES), (panels, 4, layers, LANES), (panels, 4, 8, LANES),
+        (panels, 8, LANES),
     ]
     return pl.pallas_call(
         functools.partial(halo_kernel, tiles, layers, rows),
@@ -428,72 +490,43 @@
 def main_kernel(
     layers, scale,
     p_ref, v_ref, y_ref, b_ref,
-    hrp, hrv, hry, hrb, hlp, hlv, hly, hlb, hcp, hcv, hcb,
+    hrp, hrv, hry, hrb, fix,
     g_ref,
-    sp, sv, sy, sz, ip, iv, jp, jv, ty, depth, bi, bj, acc,
+    sp, sv, sy, sz, ip, iv, jp, jv, depth, bi, bj, acc,
 ):
     rows, n = p_ref.shape[1], p_ref.shape[3]
-    wide = n + LANES
     halves = layers // 8
-    for src, row_src, col_src, cor_src, dst in (
-        (p_ref, hrp, hlp, hcp, sp),
-        (v_ref, hrv, hlv, hcv, sv),
-    ):
-        zero = jnp.zeros((layers, LANES), F32)
-        for k, (slot, tail) in enumerate(
-            ((0, zero), (1, cor_src[0, 1]), (rows + 2, cor_src[0, 3]), (rows + 3, zero))
-        ):
-            dst[slot, :, 0:n] = row_src[0, k]
-            dst[slot, :, n:wide] = tail
-        for k, slot, corner in ((1, rows + 4, 0), (2, rows + 5, 2)):
-            dst[slot, :, 0:n] = row_src[0, k]
-            dst[slot, :, n:wide] = cor_src[0, corner]
-
-    def tail_of(x, r):
-        return pltpu.roll(x, (126 - 4 * r) % LANES, 1)
 
     def shift_next(x):
-        return pltpu.roll(x, wide - 1, 1)
+        return pltpu.roll(x, n - 1, 1)
 
     def shift_back(x):
         return pltpu.roll(x, 1, 1)
 
-    edges_p, edges_v, edges_y = hlp[0], hlv[0], hly[0]
-    zero = jnp.zeros((8, LANES), F32)
-    parts = [slice(c * LANES, (c + 1) * LANES) for c in range(wide // LANES)]
-
-    ln, row = lane_iota((rows, LANES)), lax.broadcasted_iota(jnp.int32, (rows, LANES), 0)
-    tails = lane_gather(jnp.broadcast_to(hlb[0, 0:1, :], (rows, LANES)), (ln + 4 * row + 2) % LANES)
+    parts = [slice(c * LANES, (c + 1) * LANES) for c in range(n // LANES)]
+
     depth[...] = jnp.zeros(depth.shape, F32)
-    depth[8 : 8 + rows, 0:n] = b_ref[0]
-    depth[8 : 8 + rows, n:wide] = tails
-    for at, k, corner in ((6, 0, None), (7, 1, 1), (8 + rows, 2, 3), (9 + rows, 3, None)):
-        depth[at : at + 1, 0:n] = hrb[0, k : k + 1, :]
-        if corner is not None:
-            depth[at : at + 1, n:wide] = hcb[0, corner, 0:1, :]
-    between_rows = 0.5 * (depth[0 : rows + 16, :] + depth[1 : rows + 17, :])
-    own = depth[8 : 8 + rows, :]
-    along_own = 0.5 * (own + shift_next(own))
+    depth[8 : 8 + rows, :] = b_ref[0]
+    depth[6:8, :] = hrb[0, 0:2, :]
+    depth[8 + rows : 10 + rows, :] = hrb[0, 2:4, :]
+    all_rows = depth[0 : rows + 16, :]
+    between_rows = 0.5 * (all_rows + depth[1 : rows + 17, :])
+    along_rows = 0.5 * (all_rows + shift_next(all_rows))
+    along_rows = jnp.where(lane_iota(along_rows.shape) == n - 1, 0.0, along_rows)
     for c, cut in enumerate(parts):
         bi[c] = between_rows[:, cut]
-        bj[c, 8 : 8 + rows, :] = along_own[:, cut]
-    for at, k, corner in ((7, 1, 0), (8 + rows, 2, 2)):
-        x = jnp.concatenate([jnp.broadcast_to(hrb[0, k : k + 1, :], (8, n)), hcb[0, corner]], axis=1)
-        x = 0.5 * (x + shift_next(x))
-        for c, cut in enumerate(parts):
-            bj[c, at : at + 1, :] = x[0:1, cut]
+        bj[c] = along_rows[:, cut]
 
     def spread(ref, at):
         return jnp.concatenate([ref[c, pl.ds(at, 8, stride=0), :] for c in range(len(parts))], axis=1)
 
-    for r in range(rows):
-        sp[r + 2, :, 0:n] = p_ref[0, r]
-        sp[r + 2, :, n:wide] = tail_of(edges_p, r)
-        sv[r + 2, :, 0:n] = v_ref[0, r]
-        sv[r + 2, :, n:wide] = tail_of(edges_v, r)
-        ty[r] = tail_of(edges_y, r)
-
-    def lap(ref, at, flat, bases, outs, by_i, by_j, count):
+    for src, row_src, dst in ((p_ref, hrp, sp), (v_ref, hrv, sv)):
+        for k, slot in enumerate((0, 1, rows + 2, rows + 3)):
+            dst[slot] = row_src[0, k]
+        for r in range(rows):
+            dst[r + 2] = src[0, r]
+
+    def lap(ref, at, bases, outs, by_i, by_j, count):
         for h in range(halves):
             part = slice(8 * h, 8 * h + 8)
             here = ref[at, part]
@@ -502,10 +535,9 @@
                 after_row = ref[at + u + 1, part]
                 step_i = after_row - here
                 if by_i is not None:
-                    by_i[at + u - 1, part] = step_i[:, 0:n]
+                    by_i[at + u - 1, part] = step_i
                 after = spread(bi, at + u + 6) * step_i
-                line = here if flat is None else ref[flat, part]
-                step_j = shift_next(line) - line
+                step_j = shift_next(here) - here
                 if by_j is not None:
                     by_j[at + u - 2, part] = step_j
                 along = spread(bj, at + u + 6) * step_j
@@ -516,12 +548,12 @@
                 here, before = after_row, after
 
     def halo_y(k):
-        return lambda u, part: jnp.concatenate([hry[0, k, part, :], zero], axis=1)
-
-    lap(sp, 1, rows + 4, halo_y(0), sy, ip, None, 1)
-    lap(sv, 1, rows + 4, None, sz, iv, None, 1)
-    lap(sp, rows + 2, rows + 5, halo_y(1), sy, None, None, 1)
-    lap(sv, rows + 2, rows + 5, None, sz, None, None, 1)
+        return lambda u, part: hry[0, k, part, :]
+
+    lap(sp, 1, halo_y(0), sy, ip, None, 1)
+    lap(sv, 1, None, sz, iv, None, 1)
+    lap(sp, rows + 2, halo_y(1), sy, None, None, 1)
+    lap(sv, rows + 2, None, sz, None, None, 1)
 
     group = GROUP
 
@@ -529,10 +561,10 @@
         r = i * group
 
         def own_y(u, part):
-            return jnp.concatenate([y_ref[0, r + u, part, :], ty[r + u, part]], axis=1)
-
-        lap(sp, r + 2, None, own_y, sy, ip, jp, group)
-        lap(sv, r + 2, None, None, sz, iv, jv, group)
+            return y_ref[0, r + u, part, :]
+
+        lap(sp, r + 2, own_y, sy, ip, jp, group)
+        lap(sv, r + 2, None, sz, iv, jv, group)
         return carry
 
     lax.fori_loop(0, rows // group, lap_rows, 0)
@@ -541,8 +573,8 @@
         total = None
         for h in range(halves):
             part = slice(8 * h, 8 * h + 8)
-            term = iv[k, part] * (sy[k + 1, part, 0:n] - sy[k, part, 0:n])
-            term += ip[k, part] * (sz[k + 1, part, 0:n] - sz[k, part, 0:n])
+            term = iv[k, part] * (sy[k + 1, part] - sy[k, part])
+            term += ip[k, part] * (sz[k + 1, part] - sz[k, part])
             total = term if total is None else total + term
         return total
 
@@ -553,7 +585,8 @@
             y, z = sy[r + 1, part], sz[r + 1, part]
             term = jv[r, part] * (shift_next(y) - y) + jp[r, part] * (shift_next(z) - z)
             total = term if total is None else total + term
-        return (total + shift_back(total))[:, 0:n]
+        total = jnp.where(lane_iota(total.shape) == n - 1, 0.0, total)
+        return total + shift_back(total)
 
     def products(i, before):
         r = i * group
@@ -572,12 +605,20 @@
     rest = x - hi.astype(F32)
     lo = rest.astype(jnp.bfloat16)
     total = jnp.dot(ones, hi, preferred_element_type=F32) + jnp.dot(ones, lo, preferred_element_type=F32)
+    ln, row = lane_iota((rows, LANES)), lax.broadcasted_iota(jnp.int32, (rows, LANES), 0)
+    edges = lane_gather(jnp.broadcast_to(fix[0, 0:1, :], (rows, LANES)), (ln + 4 * row + 2) % LANES)
+    left = jnp.where(ln < 2, edges, 0.0)
+    right = jnp.where(ln >= LANES - 2, edges, 0.0)
+    columns = [total[:, cut] for cut in parts]
+    columns[0] = columns[0] + left
+    columns[-1] = columns[-1] + right
+    total = jnp.concatenate(columns, axis=1)
     g_ref[0] = (-0.5 * STEP_FACTOR * STEP_FACTOR * scale) * total
 
 
 def main(scale, begin, count, fields, depth, halo):
     _, rows, layers, n = fields[0].shape
-    wide = n + LANES
+    wide = n
     block = lambda x: pl.BlockSpec((1,) + x.shape[1:], lambda p: (p + begin,) + (0,) * (x.ndim - 1))
     operands = [*fields, depth, *halo]
     return pl.pallas_call(
@@ -587,15 +628,14 @@
         out_specs=pl.BlockSpec((1, rows, n), lambda p: (p, 0, 0)),
         out_shape=jax.ShapeDtypeStruct((count, rows, n), F32),
         scratch_shapes=[
-            pltpu.VMEM((rows + 6, layers, wide), F32),
-            pltpu.VMEM((rows + 6, layers, wide), F32),
+            pltpu.VMEM((rows + 4, layers, wide), F32),
+            pltpu.VMEM((rows + 4, layers, wide), F32),
             pltpu.VMEM((rows + 2, layers, wide), F32),
             pltpu.VMEM((rows + 2, layers, wide), F32),
             pltpu.VMEM((rows + 1, layers, n), F32),
             pltpu.VMEM((rows + 1, layers, n), F32),
             pltpu.VMEM((rows, layers, wide), F32),
             pltpu.VMEM((rows, layers, wide), F32),
-            pltpu.VMEM((rows, layers, LANES), F32),
             pltpu.VMEM((rows + 24, wide), F32),
             pltpu.VMEM((wide // LANES, rows + 16, LANES), F32),
             pltpu.VMEM((wide // LANES, rows + 16, LANES), F32),

time: 99.7 us -> 88.6 us (0.89)
  Pallas kernels: 71.8 us -> 60.8 us
    pallas_call x2, Pallas kernels: 44.2 us -> 32.1 us  [main(): pl.pallas_call(functools.partial(main_kernel, layers, scale), grid=(count...]
    pallas_call x1, Pallas kernels: 4.28 us -> 5.33 us  [halos(): pl.pallas_call(functools.partial(halo_kernel, tiles, layers, rows), out_s...]
  transfers between devices with their start and end apart: 6 -> 6, of which waited for: 2 -> 2; matrix products, arithmetic and copies ran while one was open for 2% -> 3% of each run, Pallas kernels for 23% -> 24%
where the time goes in v4:
time: 88.6 us; the launch traced here: 88.2 us
  Pallas kernels  60.8 us (69%)
  starting transfers between devices  15.6 us (18%)
  waiting for transfers between devices  7.05 us (8%)
  other arithmetic  3.05 us (3%)
  local copies, waits for them, and re-layouts  1.66 us (2%)
    pallas_call x2, Pallas kernels, main(): pl.pallas_call(functools.partial(main_kernel, layers, scale), grid=(count...  32.1 us
    pallas_call x1, Pallas kernels, mix_all(): pl.pallas_call(mix_kernel, grid=(panels,), in_specs=[part(layers), part(l...  14.2 us
    pallas_call x1, Pallas kernels, pack(): pl.pallas_call(functools.partial(pack_kernel, tiles, blocks, layers, npat...  9.16 us
    ppermute x1, starting transfers between devices, body(): east = lax.ppermute(low, 'tile', [(j, i) for i, j in ring])  5.53 us
    pallas_call x1, Pallas kernels, halos(): pl.pallas_call(functools.partial(halo_kernel, tiles, layers, rows), out_s...  5.33 us
    ppermute x1, starting transfers between devices, body(): lax.ppermute(mm, 'tile', [(i, tiles - 1 - i) for i in range(tiles)])  4.32 us
    ppermute x2, waiting for transfers between devices, body(): totals.append(part + lax.ppermute(part, 'samp', [(0, 1), (1, 0)]))  3.94 us
    all_to_all x1, starting transfers between devices, body(): windows = lax.all_to_all(aa, 'tile', 0, 0, tiled=True)  3.55 us
  transfers between devices with their start and end apart: 6, of which 2 were waited for; matrix products, arithmetic and copies ran while one was open for 3% of the time, Pallas kernels for 24%

profile of v4, /device:TPU:0, one launch (start us, length us, event | category | flops | bytes accessed | tf_op | source)
XLA Modules:
  0.0 88.2 jit_solution(11798610341765174043)
XLA Ops:
  0.0 0.0 copy-start.5
  0.0 0.0 copy-start.6
  0.0 9.2 %pack.1 = (f32[6,40,128]{2,1,0:T(8,128)}, f32[6,2,40,512]{3,2,1,0:T(8,128)}, f32[6,2,40,512]{3,2,1,0:T(8,128)}, f32[3,40,128]{2,1,0:T(8,128)}, f32[16,48,128]{2,1,0:T(8,128)}) custom-call(f32[16,6,32,512]{3,2,1,0:T(8,128)} %refs_3_.1, f32[16,6,32,512]{3,2,1,0:T(8,128)} %refs_3_.1, f32[16,6,32,512]{3,2,1,0:T(8,128)} %refs_3_.1, f32[16,6,32,512]{3,2,1,0:T(8,128)} %refs_3_.1, ...), custom_call_target="tpu_custom_call" | custom-call | tf_op jit(solution)/shard_map/pack/pallas_call | solution.py:172
  9.2 0.1 collective-permute-start
  9.2 5.5 %collective-permute-start.1 = (f32[6,2,40,512]{3,2,1,0:T(8,128)}, f32[6,2,40,512]{3,2,1,0:T(8,128)S(1)}, u32[]{:S(2)}, u32[]{:S(2)}) collective-permute-start(f32[6,2,40,512]{3,2,1,0:T(8,128)} %get-tuple-element.22), channel_id=1, source_target_pairs={{2,0},{4,2},{6,4},{8,6},{10,8},{12,10},{14,12},{16,14},{18,16},{20... | collective-permute-start | bytes 2949128 | tf_op jit(solution)/shard_map/ppermute | solution.py:669
  14.8 3.6 %all-to-all-start = ((f32[16,48,128]{2,1,0:T(8,128)}), f32[16,48,128]{2,1,0:T(8,128)S(1)}, u32[]{:S(2)}, u32[]{:S(2)}) async-start(f32[16,48,128]{2,1,0:T(8,128)} %get-tuple-element.25), calls=%async_computation | async-start | bytes 786432 | tf_op jit(solution)/shard_map/all_to_all | solution.py:671
  18.3 4.3 %collective-permute-start.2 = (f32[3,40,128]{2,1,0:T(8,128)}, f32[3,40,128]{2,1,0:T(8,128)S(1)}, u32[]{:S(2)}, u32[]{:S(2)}) collective-permute-start(f32[3,40,128]{2,1,0:T(8,128)} %get-tuple-element.24), channel_id=1, source_target_pairs={{0,30},{2,28},{4,26},{6,24},{8,22},{10,20},{12,18},{14,16},{16,14}... | collective-permute-start | bytes 184328 | tf_op jit(solution)/shard_map/ppermute | solution.py:670
  22.6 0.0 copy-done.5
  22.6 0.1 copy.10
  22.7 0.1 copy.12
  22.8 0.1 copy.11
  22.9 0.0 copy-done.6
  22.9 0.7 fusion.2.sel_ref
  23.6 0.7 pad_maximum_fusion.1
  24.3 14.2 %mix.1 = (f32[6,32,16,512]{3,2,1,0:T(8,128)}, f32[6,32,16,512]{3,2,1,0:T(8,128)}, f32[6,32,16,512]{3,2,1,0:T(8,128)}) custom-call(f32[16,6,32,512]{3,2,1,0:T(8,128)} %refs_3_.1, f32[16,6,32,512]{3,2,1,0:T(8,128)} %bitcast.9, bf16[4,6,32,512]{3,2,1,0:T(8,128)(2,1)} %refs_11_.1, bf16[16,48]{1,0:T(8,128)(2,1)} %get-tuple-element.35.fwd_ref, ...), custom_call_target="tpu_custom_call" | custom-call | flops 301989888 | bytes 31457280 | tf_op jit(solution)/shard_map/mix/pallas_call | solution.py:260
  38.5 0.0 collective-permute-done.2.mm_ref
  38.5 0.0 copy-start.4
  38.5 3.1 %all-to-all-done.aa_ref = f32[16,48,128]{2,1,0:T(8,128)S(1)} async-done(((f32[16,48,128]{2,1,0:T(8,128)}), f32[16,48,128]{2,1,0:T(8,128)S(1)}, u32[]{:S(2)}, u32[]{:S(2)}) %all-to-all-start) | async-done | bytes 393248 | tf_op jit(solution)/shard_map/all_to_all | solution.py:671
  41.6 0.0 copy-start
  41.6 0.0 collective-permute-done.west_ref
  41.6 0.0 copy-start.2
  41.6 0.0 collective-permute-done.1.east_ref
  41.6 0.0 copy-start.3
  41.6 0.0 copy-done.4
  41.6 0.7 copy-done
  42.3 0.3 copy-done.2
  42.7 0.4 copy-done.3
  43.0 5.3 %halos.1 = (f32[6,4,16,512]{3,2,1,0:T(8,128)}, f32[6,4,16,512]{3,2,1,0:T(8,128)}, f32[6,2,16,512]{3,2,1,0:T(8,128)}, f32[6,8,512]{2,1,0:T(8,128)}, f32[6,8,128]{2,1,0:T(8,128)}) custom-call(f32[6,2,40,512]{3,2,1,0:T(8,128)} %copy-done.2, f32[6,2,40,512]{3,2,1,0:T(8,128)} %copy-done.3, f32[6,40,128]{2,1,0:T(8,128)} %get-tuple-element.23.em_ref, ...), custom_call_target="tpu_custom_call" | custom-call | tf_op jit(solution)/shard_map/halos/pallas_call | solution.py:481
  48.3 25.1 %main.2 = f32[5,32,512]{2,1,0:T(8,128)} custom-call(f32[6,32,16,512]{3,2,1,0:T(8,128)} %get-tuple-element.18.p_ref, f32[6,32,16,512]{3,2,1,0:T(8,128)} %get-tuple-element.19.v_ref, f32[6,32,16,512]{3,2,1,0:T(8,128)} %get-tuple-element.20.y_ref, f32[6,32,512]{2,1,0:T(8,128)} %b_ref.3, f32[6,4,16,512]{3,2,1,0:T(8,128)} %get-tuple-element.26.hrp, ...), custom_call_target="tpu_custom_call" | custom-call | flops 78643200 | bytes 20971520 | tf_op jit(solution)/shard_map/main/pallas_call | solution.py:624
  73.4 0.0 copy-start.1
  73.4 1.6 %collective-permute-start.3 = (f32[5,32,512]{2,1,0:T(8,128)}, f32[5,32,512]{2,1,0:T(8,128)S(1)}, u32[]{:S(2)}, u32[]{:S(2)}) collective-permute-start(f32[5,32,512]{2,1,0:T(8,128)} %main.2), channel_id=1, source_target_pairs={{0,1},{1,0},{2,3},{3,2},{4,5},{5,4},{6,7},{7,6},{8,9},{9,8},{10,11... | collective-permute-start | bytes 983048 | tf_op jit(solution)/shard_map/ppermute | solution.py:678
  75.0 7.0 %main.3 = f32[1,32,512]{2,1,0:T(8,128)} custom-call(f32[6,32,16,512]{3,2,1,0:T(8,128)} %get-tuple-element.18.p_ref, f32[6,32,16,512]{3,2,1,0:T(8,128)} %get-tuple-element.19.v_ref, f32[6,32,16,512]{3,2,1,0:T(8,128)} %get-tuple-element.20.y_ref, f32[6,32,512]{2,1,0:T(8,128)} %b_ref.3, f32[6,4,16,512]{3,2,1,0:T(8,128)} %get-tuple-element.26.hrp, ...), custom_call_target="tpu_custom_call" | custom-call | flops 15728640 | bytes 4194304 | tf_op jit(solution)/shard_map/main/pallas_call | solution.py:624
  82.0 0.5 collective-permute-start.4
  82.5 3.9 %collective-permute-done.4 = f32[1,32,512]{2,1,0:T(8,128)S(1)} collective-permute-done((f32[1,32,512]{2,1,0:T(8,128)}, f32[1,32,512]{2,1,0:T(8,128)S(1)}, u32[]{:S(2)}, u32[]{:S(2)}) %collective-permute-start.4) | collective-permute-done | bytes 65568 | tf_op jit(solution)/shard_map/ppermute | solution.py:678
  86.5 0.9 add.11
  87.3 0.0 collective-permute-done.3
  87.3 0.0 copy-done.1
  87.4 0.8 pad_maximum_fusion
  (3 shorter events, 0.1 us)
Async XLA Ops:
  0.0 22.6 %copy-start.5 = (f32[16,16]{1,0:T(8,128)S(1)}, f32[16,16]{1,0:T(8,128)}, u32[]{:S(2)}) copy-start(f32[16,16]{1,0:T(8,128)} %param.10) | copy-start | bytes 3076
  0.0 22.9 %copy-start.6 = (s32[1,16]{1,0:T(1,128)S(1)}, s32[1,16]{1,0:T(1,128)}, u32[]{:S(2)}) copy-start(s32[1,16]{1,0:T(1,128)} %param.9) | copy-start | bytes 196
  9.2 32.4 %collective-permute-start = (f32[6,2,40,512]{3,2,1,0:T(8,128)}, f32[6,2,40,512]{3,2,1,0:T(8,128)S(1)}, u32[]{:S(2)}, u32[]{:S(2)}) collective-permute-start(f32[6,2,40,512]{3,2,1,0:T(8,128)} %get-tuple-element.21), channel_id=1, source_target_pairs={{0,2},{2,4},{4,6},{6,8},{8,10},{10,12},{12,14},{14,16},{16,18},{18... | collective-permute-start | bytes 2949128 | tf_op jit(solution)/shard_map/ppermute | solution.py:668
  9.2 32.3 %collective-permute-start.1 = (f32[6,2,40,512]{3,2,1,0:T(8,128)}, f32[6,2,40,512]{3,2,1,0:T(8,128)S(1)}, u32[]{:S(2)}, u32[]{:S(2)}) collective-permute-start(f32[6,2,40,512]{3,2,1,0:T(8,128)} %get-tuple-element.22), channel_id=1, source_target_pairs={{2,0},{4,2},{6,4},{8,6},{10,8},{12,10},{14,12},{16,14},{18,16},{20... | collective-permute-start | bytes 2949128 | tf_op jit(solution)/shard_map/ppermute | solution.py:669
  14.8 26.8 %all-to-all-start = ((f32[16,48,128]{2,1,0:T(8,128)}), f32[16,48,128]{2,1,0:T(8,128)S(1)}, u32[]{:S(2)}, u32[]{:S(2)}) async-start(f32[16,48,128]{2,1,0:T(8,128)} %get-tuple-element.25), calls=%async_computation | async-start | bytes 786432 | tf_op jit(solution)/shard_map/all_to_all | solution.py:671
  18.3 20.1 %collective-permute-start.2 = (f32[3,40,128]{2,1,0:T(8,128)}, f32[3,40,128]{2,1,0:T(8,128)S(1)}, u32[]{:S(2)}, u32[]{:S(2)}) collective-permute-start(f32[3,40,128]{2,1,0:T(8,128)} %get-tuple-element.24), channel_id=1, source_target_pairs={{0,30},{2,28},{4,26},{6,24},{8,22},{10,20},{12,18},{14,16},{16,14}... | collective-permute-start | bytes 184328 | tf_op jit(solution)/shard_map/ppermute | solution.py:670
  38.5 3.1 %copy-start.4 = (f32[3,40,128]{2,1,0:T(8,128)}, f32[3,40,128]{2,1,0:T(8,128)S(1)}, u32[]{:S(2)}) copy-start(f32[3,40,128]{2,1,0:T(8,128)S(1)} %collective-permute-done.2.mm_ref) | copy-start | bytes 184324
  41.6 0.7 copy-start
  41.6 1.1 %copy-start.2 = (f32[6,2,40,512]{3,2,1,0:T(8,128)}, f32[6,2,40,512]{3,2,1,0:T(8,128)S(1)}, u32[]{:S(2)}) copy-start(f32[6,2,40,512]{3,2,1,0:T(8,128)S(1)} %collective-permute-done.west_ref) | copy-start | bytes 2949124
  41.6 1.4 %copy-start.3 = (f32[6,2,40,512]{3,2,1,0:T(8,128)}, f32[6,2,40,512]{3,2,1,0:T(8,128)S(1)}, u32[]{:S(2)}) copy-start(f32[6,2,40,512]{3,2,1,0:T(8,128)S(1)} %collective-permute-done.1.east_ref) | copy-start | bytes 2949124
  73.4 13.9 %copy-start.1 = (f32[5,32,512]{2,1,0:T(8,128)S(1)}, f32[5,32,512]{2,1,0:T(8,128)}, u32[]{:S(2)}) copy-start(f32[5,32,512]{2,1,0:T(8,128)} %main.2) | copy-start | bytes 983044
  73.4 13.9 %collective-permute-start.3 = (f32[5,32,512]{2,1,0:T(8,128)}, f32[5,32,512]{2,1,0:T(8,128)S(1)}, u32[]{:S(2)}, u32[]{:S(2)}) collective-permute-start(f32[5,32,512]{2,1,0:T(8,128)} %main.2), channel_id=1, source_target_pairs={{0,1},{1,0},{2,3},{3,2},{4,5},{5,4},{6,7},{7,6},{8,9},{9,8},{10,11... | collective-permute-start | bytes 983048 | tf_op jit(solution)/shard_map/ppermute | solution.py:678
  82.0 4.5 %collective-permute-start.4 = (f32[1,32,512]{2,1,0:T(8,128)}, f32[1,32,512]{2,1,0:T(8,128)S(1)}, u32[]{:S(2)}, u32[]{:S(2)}) collective-permute-start(f32[1,32,512]{2,1,0:T(8,128)} %main.3), channel_id=1, source_target_pairs={{0,1},{1,0},{2,3},{3,2},{4,5},{5,4},{6,7},{7,6},{8,9},{9,8},{10,11... | collective-permute-start | bytes 196616 | tf_op jit(solution)/shard_map/ppermute | solution.py:678

commit v5 on v4

--- a/solution.py
+++ b/solution.py
@@ -6,6 +6,7 @@
 from jax.experimental import pallas as pl
 from jax.experimental.pallas import tpu as pltpu
 from jax.sharding import PartitionSpec as P
+
 
 STEP_FACTOR = 0.1
 LANES = 128
@@ -194,37 +195,56 @@
     )(*[s] * blocks, *[w] * blocks, *[pat] * blocks, b)
 
 
-def mix_kernel(s_ref, w_ref, pat_ref, fwd_ref, bwd_ref, sel_ref, p_ref, v_ref, y_ref, left_s, left_w, left_f, pf):
+def mix_kernel(
+    s_ref, w_ref, pat_ref, mat_ref, index_ref,
+    p_ref, v_ref, y_ref, fwd_ref, bwd_ref, sel_ref,
+    left_s, left_w, left_f, pf,
+):
     layers, n = s_ref.shape[0], s_ref.shape[3]
     npat, rows = pat_ref.shape[0], pat_ref.shape[2]
     size = 8 * layers
-
-    @pl.when(pl.program_id(0) == 0)
-    def _():
-        def spread(matrix, count):
-            down = lax.broadcasted_iota(jnp.int32, (size, layers), 0) % layers
-            down = (down == lax.broadcasted_iota(jnp.int32, (size, layers), 1)).astype(F32).astype(jnp.bfloat16)
-            over = lax.broadcasted_iota(jnp.int32, (count, 8 * count), 1) // 8
-            over = (over == lax.broadcasted_iota(jnp.int32, (count, 8 * count), 0)).astype(F32).astype(jnp.bfloat16)
-            x = jnp.dot(down, matrix, preferred_element_type=F32).astype(jnp.bfloat16)
-            x = jnp.dot(x, over, preferred_element_type=F32)
-            same = lax.broadcasted_iota(jnp.int32, x.shape, 0) // layers
-            same = same == lax.broadcasted_iota(jnp.int32, x.shape, 1) % 8
-            return jnp.where(same, x, 0.0).astype(jnp.bfloat16)
-
-        def parts(ref):
-            return spread(ref[:, 0:layers], layers), spread(ref[:, layers : 2 * layers], layers)
-
-        eye = lax.broadcasted_iota(jnp.int32, (layers, layers), 0) == lax.broadcasted_iota(
-            jnp.int32, (layers, layers), 1
-        )
-        thirty = spread(jnp.where(eye, 30.0, 0.0).astype(jnp.bfloat16), layers)
-        high, low = parts(fwd_ref)
-        for k, x in enumerate((high, low, thirty)):
+    half = jnp.bfloat16
+
+    def matrices(_, carry):
+        def iotas(shape):
+            return (lax.broadcasted_iota(jnp.int32, shape, d) for d in range(2))
+
+        def one(cond):
+            return cond.astype(F32).astype(half)
+
+        def product(a, b, flipped=False):
+            dims = (((1,), (1 if flipped else 0,)), ((), ()))
+            return lax.dot_general(a, b, dims, preferred_element_type=F32).astype(half)
+
+        def spread(matrix, flipped=False):
+            i, j = iotas((size, layers))
+            x = product(one(i % layers == j), matrix, flipped)
+            i, j = iotas((x.shape[1], 8 * x.shape[1]))
+            x = jnp.dot(x, one(j // 8 == i), preferred_element_type=F32)
+            i, j = iotas(x.shape)
+            return jnp.where(i // layers == j % 8, x, 0.0).astype(half)
+
+        i, j = iotas((layers, layers))
+        eye = one(i == j)
+        mixing = mat_ref[...] + eye.astype(F32)
+        high = mixing.astype(half)
+        low = (mixing - high.astype(F32)).astype(half)
+        q = lax.broadcasted_iota(jnp.int32, (8, layers), 0)
+        chosen = one(jnp.broadcast_to(index_ref[...], (8, layers)) == q)
+        for k, x in enumerate((spread(high), spread(low), spread((30.0 * eye.astype(F32)).astype(half)))):
             left_s[k * size : (k + 1) * size, :] = jnp.concatenate([x, x], axis=1)
-        for k, x in enumerate(parts(bwd_ref)):
+        for k, x in enumerate((spread(high, True), spread(low, True))):
             left_w[k * size : (k + 1) * size, :] = jnp.concatenate([x, x], axis=1)
-        left_f[...] = spread(sel_ref[...], 8)
+        left_f[...] = spread(chosen, True)
+        high_t, low_t = product(eye, high, True), product(eye, low, True)
+        for k, (x, y) in enumerate(((high, high_t), (low, low_t), (high, high_t))):
+            fwd_ref[:, k * layers : (k + 1) * layers] = x
+            bwd_ref[:, k * layers : (k + 1) * layers] = y
+        sel_ref[...] = product(eye, chosen, True)
+        return carry
+
+    start = (pl.program_id(0) == 0) & (pl.program_id(1) == 0)
+    lax.fori_loop(0, jnp.where(start, 1, 0), matrices, 0)
 
     pf[...] = jnp.zeros(pf.shape, F32)
     pf[0:npat] = pat_ref[:, 0].astype(F32)
@@ -249,37 +269,40 @@
             v_ref[0, own, :, cut] = (x[0:size] + x[size:]).reshape(8, layers, step)
 
 
-def mix_all(s, w, pat, fwd, bwd, sel):
+def mix_all(s, w, pat, matrix, index):
     layers, panels, rows, n = s.shape
-    npat = pat.shape[0]
-    full = lambda x: pl.BlockSpec(x.shape, lambda p: (0,) * x.ndim)
-    part = lambda count: pl.BlockSpec((count, 1, rows, n), lambda p: (0, p, 0, 0))
-    out = pl.BlockSpec((1, rows, layers, n), lambda p: (p, 0, 0, 0))
+    npat, each = pat.shape[0], rows
+    full = lambda *shape: pl.BlockSpec(shape, lambda p, g: (0, 0))
+    part = lambda count: pl.BlockSpec((count, 1, each, n), lambda p, g: (0, p, g, 0))
+    out = pl.BlockSpec((1, each, layers, n), lambda p, g: (p, g, 0, 0))
     size = layers * panels * rows * n * 4
     wide = 8 * layers
-    return pl.pallas_call(
+    small = [(layers, 3 * layers), (layers, 3 * layers), (layers, 8)]
+    *fields, fwd, bwd, sel = pl.pallas_call(
         mix_kernel,
-        grid=(panels,),
-        in_specs=[part(layers), part(layers), part(npat), full(fwd), full(bwd), full(sel)],
-        out_specs=[out] * 3,
-        out_shape=[jax.ShapeDtypeStruct((panels, rows, layers, n), F32)] * 3,
+        grid=(panels, rows // each),
+        in_specs=[part(layers), part(layers), part(npat), full(layers, layers), full(1, layers)],
+        out_specs=[out] * 3 + [full(*x) for x in small],
+        out_shape=[jax.ShapeDtypeStruct((panels, rows, layers, n), F32)] * 3
+        + [jax.ShapeDtypeStruct(x, jnp.bfloat16) for x in small],
         scratch_shapes=[
             pltpu.VMEM((3 * wide, 2 * wide), jnp.bfloat16),
             pltpu.VMEM((2 * wide, 2 * wide), jnp.bfloat16),
             pltpu.VMEM((wide, 64), jnp.bfloat16),
-            pltpu.VMEM((8, rows, n), F32),
+            pltpu.VMEM((8, each, n), F32),
         ],
         compiler_params=pltpu.CompilerParams(vmem_limit_bytes=VMEM),
         cost_estimate=pl.CostEstimate(flops=size * 48, bytes_accessed=5 * size, transcendentals=0),
         name="mix",
-    )(s, w, pat, fwd, bwd, sel)
+    )(s, w, pat, matrix, index)
+    return fields, fwd, bwd, sel
 
 
 def halo_kernel(
     tiles, layers, rows,
-    west_ref, east_ref, em_ref, mm_ref, aa_ref, fwd_ref, bwd_ref, sel_ref,
-    hrp_ref, hrv_ref, hry_ref, hrb_ref, fix_ref,
-    line,
+    west_ref, east_ref, low_ref, high_ref, em_ref, mm_ref, aa_ref, fwd_ref, bwd_ref, sel_ref,
+    fix_ref,
+    line, hrp_ref, hrv_ref, hrb_ref,
 ):
     panels, n = west_ref.shape[0], west_ref.shape[3]
     place = lax.axis_index("tile")
@@ -345,14 +368,63 @@
             sel, x[2 * layers : CH].astype(jnp.bfloat16), preferred_element_type=F32
         )
 
-    for p in range(panels):
-        for k in range(4):
-            x = line[p, k]
-            hrp_ref[p, k] = mix(fwd, x[0:layers])
-            hrv_ref[p, k] = mix(bwd, x[layers : 2 * layers])
-            hrb_ref[p, k : k + 1, :] = line[p, k, CH - 4 : CH - 3, :]
-            if k in (1, 2):
-                hry_ref[p, k - 1] = force(x)
+    def fold(x):
+        return sum(x[k : k + 8] for k in range(0, layers, 8))
+
+    def shift_next(x):
+        return pltpu.roll(x, n - 1, 1)
+
+    def shift_back(x):
+        return pltpu.roll(x, 1, 1)
+
+    last_lane = lane_iota((1, n)) == n - 1
+
+    def row_edges(p, carry):
+        fix_ref[p] = jnp.zeros((8, n), F32)
+        for bottom in range(2):
+            own = 1 if bottom else 2
+            far = 2 if bottom else 1
+            lines = (high_ref, line) if bottom else (line, low_ref)
+            raw = [lines[0].at[p, 0], lines[0].at[p, 1]]
+            raw += [line.at[p, 2], line.at[p, 3]] if bottom else [low_ref.at[p, 0], low_ref.at[p, 1]]
+            fields = (
+                [mix(fwd, x[0:layers, :]) for x in raw],
+                [mix(bwd, x[layers : 2 * layers, :]) for x in raw],
+            )
+            bases = {k: force(raw[k][...]) for k in (1, 2)}
+            depth = [x[CH - 4 : CH - 3, :] for x in raw]
+            hrp_ref[p, bottom], hrv_ref[p, bottom] = fields[0][far], fields[1][far]
+            hrb_ref[p, bottom : bottom + 1, :] = depth[far]
+            wi = [0.5 * (depth[k] + depth[k + 1]) for k in range(3)]
+            wj = {k: jnp.where(last_lane, 0.0, 0.5 * (depth[k] + shift_next(depth[k]))) for k in (1, 2)}
+            steps, sides, flows, laps = [], [], [], []
+            for x in fields:
+                step = [x[k + 1] - x[k] for k in range(3)]
+                flow = [w * d for w, d in zip(wi, step)]
+                side = {k: shift_next(x[k]) - x[k] for k in (1, 2)}
+                out = {}
+                for k in (1, 2):
+                    along = wj[k] * side[k]
+                    out[k] = flow[k] - flow[k - 1] + along - shift_back(along)
+                steps.append(step)
+                sides.append(side[own])
+                flows.append(flow[1] if bottom else -flow[1])
+                laps.append(out)
+            y = {k: bases[k] + laps[0][k] for k in (1, 2)}
+            cross = fold(steps[1][1] * (y[2] - y[1]) + steps[0][1] * (laps[1][2] - laps[1][1]))
+            at = 0 if bottom else 2
+            inside = fold(steps[1][at] * flows[0] + steps[0][at] * flows[1])
+            inside = inside if bottom else -inside
+            beside = fold(sides[1] * (shift_next(flows[0]) - flows[0]) + sides[0] * (shift_next(flows[1]) - flows[1]))
+            beside = jnp.where(last_lane, 0.0, beside)
+            whole = jnp.sum(cross + inside + beside + shift_back(beside), axis=0, keepdims=True)
+            inside = jnp.sum(inside, axis=0, keepdims=True)
+            slots = (2, 3) if bottom else (1, 0)
+            fix_ref[p, slots[0] : slots[0] + 1, :] = inside
+            fix_ref[p, slots[1] : slots[1] + 1, :] = whole
+        return carry
+
+    lax.fori_loop(0, panels, row_edges, 0)
 
     span = 4 * rows
     turn = jnp.where(lane < span, span - 1 - lane, 0)
@@ -383,9 +455,6 @@
 
     def turn(x, by):
         return pltpu.roll(x, by % LANES, 1)
-
-    def fold(x):
-        return jnp.sum(x, axis=0, keepdims=True)
 
     for p in range(panels):
         raw = columns[p]
@@ -414,7 +483,10 @@
             corner = first if edge == 0 else final
             sideways = mixed(jnp.where(corner, across, inner))
             onward = mixed(jnp.where(corner, along, inner))
-            head, tail = mixed(at_cut(p, 0)), mixed(at_cut(p, blocks - 1))
+            head, tail = (
+                (hrp_ref[p, edge, :, cut], hrv_ref[p, edge, :, cut], jnp.broadcast_to(hrb_ref[p, edge : edge + 1, cut], (layers, LANES)))
+                for cut in (slice(0, LANES), slice(n - LANES, n))
+            )
             base = 4 * own_row
             here = [
                 [turn(jnp.where(end, o, h), base + 2) for o, h in zip(onward, head)],
@@ -457,7 +529,7 @@
                 inside = fold(dj[1] * turn(extra[0], -1) + dj[0] * turn(extra[1], -1))
             else:
                 inside = -fold(dj[1] * extra[0] + dj[0] * extra[1])
-            k1, r1 = k_of[0:1], r_of[0:1]
+            k1, r1 = k_of[0:8], r_of[0:8]
             whole = along_i + jnp.where(r1 == 0, along_m, turn(along_i, 4))
             if right:
                 whole = whole + cross_edge + turn(inside, 1)
@@ -469,28 +541,29 @@
                 total = jnp.where(k1 < 2, result, total)
             else:
                 total = result
-        fix_ref[p] = jnp.broadcast_to(total, (8, LANES))
-
-
-def halos(tiles, layers, rows, west, east, em, mm, aa, fwd, bwd, sel):
+        fix_ref[p, 4:5, 0:LANES] = jnp.sum(total, axis=0, keepdims=True)
+
+
+def halos(tiles, layers, rows, west, east, *others):
     panels, n = west.shape[0], west.shape[3]
-    shapes = [
-        (panels, 4, layers, n), (panels, 4, layers, n), (panels, 2, layers, n), (panels, 8, n),
-        (panels, 8, LANES),
-    ]
     return pl.pallas_call(
         functools.partial(halo_kernel, tiles, layers, rows),
-        out_shape=[jax.ShapeDtypeStruct(s, F32) for s in shapes],
-        scratch_shapes=[pltpu.VMEM((panels, 4, CH, n), F32)],
+        out_shape=jax.ShapeDtypeStruct((panels, 8, n), F32),
+        scratch_shapes=[
+            pltpu.VMEM((panels, 4, CH, n), F32),
+            pltpu.VMEM((panels, 2, layers, n), F32),
+            pltpu.VMEM((panels, 2, layers, n), F32),
+            pltpu.VMEM((panels, 8, n), F32),
+        ],
         compiler_params=pltpu.CompilerParams(vmem_limit_bytes=VMEM),
+        cost_estimate=pl.CostEstimate(flops=100 * panels * n * layers, bytes_accessed=4 * panels * n * CH * 8, transcendentals=0),
         name="halos",
-    )(west, east, em, mm, aa, fwd, bwd, sel)
+    )(west, east, *others)
 
 
 def main_kernel(
     layers, scale,
     p_ref, v_ref, y_ref, b_ref,
-    hrp, hrv, hry, hrb, fix,
     g_ref,
     sp, sv, sy, sz, ip, iv, jp, jv, depth, bi, bj, acc,
 ):
@@ -507,10 +580,10 @@
 
     depth[...] = jnp.zeros(depth.shape, F32)
     depth[8 : 8 + rows, :] = b_ref[0]
-    depth[6:8, :] = hrb[0, 0:2, :]
-    depth[8 + rows : 10 + rows, :] = hrb[0, 2:4, :]
     all_rows = depth[0 : rows + 16, :]
     between_rows = 0.5 * (all_rows + depth[1 : rows + 17, :])
+    at = lax.broadcasted_iota(jnp.int32, between_rows.shape, 0)
+    between_rows = jnp.where((at >= 8) & (at < 7 + rows), between_rows, 0.0)
     along_rows = 0.5 * (all_rows + shift_next(all_rows))
     along_rows = jnp.where(lane_iota(along_rows.shape) == n - 1, 0.0, along_rows)
     for c, cut in enumerate(parts):
@@ -520,9 +593,9 @@
     def spread(ref, at):
         return jnp.concatenate([ref[c, pl.ds(at, 8, stride=0), :] for c in range(len(parts))], axis=1)
 
-    for src, row_src, dst in ((p_ref, hrp, sp), (v_ref, hrv, sv)):
-        for k, slot in enumerate((0, 1, rows + 2, rows + 3)):
-            dst[slot] = row_src[0, k]
+    for src, dst in ((p_ref, sp), (v_ref, sv)):
+        for slot in (1, rows + 2):
+            dst[slot] = jnp.zeros((layers, n), F32)
         for r in range(rows):
             dst[r + 2] = src[0, r]
 
@@ -547,14 +620,6 @@
                 outs[at + u - 1, part] = out
                 here, before = after_row, after
 
-    def halo_y(k):
-        return lambda u, part: hry[0, k, part, :]
-
-    lap(sp, 1, halo_y(0), sy, ip, None, 1)
-    lap(sv, 1, None, sz, iv, None, 1)
-    lap(sp, rows + 2, halo_y(1), sy, None, None, 1)
-    lap(sv, rows + 2, None, sz, None, None, 1)
-
     group = GROUP
 
     def lap_rows(i, carry):
@@ -568,6 +633,8 @@
         return carry
 
     lax.fori_loop(0, rows // group, lap_rows, 0)
+    none = jnp.zeros((layers, n), F32)
+    sy[rows + 1], sz[rows + 1], ip[rows], iv[rows] = none, none, none, none
 
     def between(k):
         total = None
@@ -596,7 +663,7 @@
             before = after
         return before
 
-    lax.fori_loop(0, rows // group, products, between(0))
+    lax.fori_loop(0, rows // group, products, jnp.zeros((8, n), F32))
 
     x = acc[...].reshape(8 * rows, n)
     at_row = lax.broadcasted_iota(jnp.int32, (rows, 8 * rows), 0)
@@ -605,22 +672,14 @@
     rest = x - hi.astype(F32)
     lo = rest.astype(jnp.bfloat16)
     total = jnp.dot(ones, hi, preferred_element_type=F32) + jnp.dot(ones, lo, preferred_element_type=F32)
-    ln, row = lane_iota((rows, LANES)), lax.broadcasted_iota(jnp.int32, (rows, LANES), 0)
-    edges = lane_gather(jnp.broadcast_to(fix[0, 0:1, :], (rows, LANES)), (ln + 4 * row + 2) % LANES)
-    left = jnp.where(ln < 2, edges, 0.0)
-    right = jnp.where(ln >= LANES - 2, edges, 0.0)
-    columns = [total[:, cut] for cut in parts]
-    columns[0] = columns[0] + left
-    columns[-1] = columns[-1] + right
-    total = jnp.concatenate(columns, axis=1)
     g_ref[0] = (-0.5 * STEP_FACTOR * STEP_FACTOR * scale) * total
 
 
-def main(scale, begin, count, fields, depth, halo):
-    _, rows, layers, n = fields[0].shape
+def main(scale, fields, depth):
+    count, rows, layers, n = fields[0].shape
     wide = n
-    block = lambda x: pl.BlockSpec((1,) + x.shape[1:], lambda p: (p + begin,) + (0,) * (x.ndim - 1))
-    operands = [*fields, depth, *halo]
+    block = lambda x: pl.BlockSpec((1,) + x.shape[1:], lambda p: (p,) + (0,) * (x.ndim - 1))
+    operands = [*fields, depth]
     return pl.pallas_call(
         functools.partial(main_kernel, layers, scale),
         grid=(count,),
@@ -649,36 +708,49 @@
     )(*operands)
 
 
+def finish_kernel(scale, *refs):
+    *ins, out_ref = refs
+    half = len(ins) // 2
+    panels, rows, n = out_ref.shape
+    ln, row = lane_iota((rows, LANES)), lax.broadcasted_iota(jnp.int32, (rows, LANES), 0)
+    for p in range(panels):
+        fix = (-0.5 * STEP_FACTOR * STEP_FACTOR * scale) * sum(x[p] for x in ins[half:])
+        out_ref[p] = sum(x[p] for x in ins[:half])
+        edges = lane_gather(jnp.broadcast_to(fix[4:5, 0:LANES], (rows, LANES)), (ln + 4 * row + 2) % LANES)
+        out_ref[p, :, 0:LANES] += jnp.where(ln < 2, edges, 0.0)
+        out_ref[p, :, n - LANES : n] += jnp.where(ln >= LANES - 2, edges, 0.0)
+        out_ref[p, 0:2, :] += fix[0:2]
+        out_ref[p, rows - 2 : rows, :] += fix[2:4]
+
+
+def finish(scale, totals, fixes):
+    return pl.pallas_call(
+        functools.partial(finish_kernel, scale),
+        out_shape=jax.ShapeDtypeStruct(totals[0].shape, F32),
+        name="finish",
+    )(*totals, *fixes)
+
+
 def body(bathymetry, initial_state, patterns, pattern_index, coupling, final_weights):
     tiles, samples = lax.axis_size("tile"), lax.axis_size("samp")
-    layers, panels, rows, n = initial_state.shape
+    layers, _, rows, _ = initial_state.shape
     weights = final_weights[0]
-    mixing = jnp.eye(layers, dtype=F32) + coupling
-
-    def cat(matrix):
-        high = lax.reduce_precision(matrix, 8, 7)
-        low = matrix - high
-        return jnp.concatenate([high, low, high], axis=1).astype(jnp.bfloat16)
-
-    fwd, bwd = cat(mixing), cat(mixing.T)
-    sel = (pattern_index[0][:, None] == jnp.arange(8, dtype=jnp.int32)[None, :]).astype(jnp.bfloat16)
-
     em, low, high, mm, aa = pack(tiles, initial_state, weights, patterns, bathymetry)
     ring = [(i, (i + 1) % tiles) for i in range(tiles)]
     west = lax.ppermute(high, "tile", ring)
     east = lax.ppermute(low, "tile", [(j, i) for i, j in ring])
     mirrored = lax.ppermute(mm, "tile", [(i, tiles - 1 - i) for i in range(tiles)])
     windows = lax.all_to_all(aa, "tile", 0, 0, tiled=True)
-    fields = mix_all(initial_state, weights, patterns, fwd, bwd, sel)
-    halo = halos(tiles, layers, rows, west, east, em, mirrored, windows, fwd, bwd, sel)
-    totals = []
-    for begin, end in ((0, panels - 1), (panels - 1, panels)):
-        part = main(1.0 / samples, begin, end - begin, fields, bathymetry, halo)
-        if samples == 2:
-            totals.append(part + lax.ppermute(part, "samp", [(0, 1), (1, 0)]))
-        else:
-            totals.append(lax.psum(part, "samp"))
-    return jnp.concatenate(totals, axis=0)
+    fields, fwd, bwd, sel = mix_all(initial_state, weights, patterns, coupling, pattern_index)
+    total = main(1.0 / samples, fields, bathymetry)
+    fix = halos(tiles, layers, rows, west, east, low, high, em, mirrored, windows, fwd, bwd, sel)
+    if samples == 2:
+        swap = [(0, 1), (1, 0)]
+        totals = (total, lax.ppermute(total, "samp", swap))
+        fixes = (fix, lax.ppermute(fix, "samp", swap))
+    else:
+        totals, fixes = (lax.psum(total, "samp"),), (lax.psum(fix, "samp"),)
+    return finish(1.0 / samples, totals, fixes)
 
 
 def solution(mesh):

time: 88.6 us -> 89.3 us (level)
  Pallas kernels: 60.8 us -> 64.2 us
  other arithmetic: 3.05 us -> 0 us
    pallas_call x1, Pallas kernels: 5.33 us -> 10.3 us  [halos(): pl.pallas_call(functools.partial(halo_kernel, tiles, layers, rows), out_s...]
    pallas_call x2 -> x1, Pallas kernels: 32.1 us -> 28.4 us  [main(): pl.pallas_call(functools.partial(main_kernel, layers, scale), grid=(count...]
    all_to_all x1, waiting for transfers between devices: 3.1 us -> 0.01 us  [body(): windows = lax.all_to_all(aa, 'tile', 0, 0, tiled=True)]
    ppermute x1, waiting for transfers between devices: 0.01 us -> 2.64 us  [body(): lax.ppermute(mm, 'tile', [(i, tiles - 1 - i) for i in range(tiles)])]
    pallas_call x1 -> x2, Pallas kernels: 14.2 us -> 16.3 us  [the longest x1 14.2 us: mix_all(): pl.pallas_call(mix_kernel, grid=(panels, rows // each), in_specs=[part(la...]
    concatenate x2 -> x0, other arithmetic: 1.46 us -> none  [the longest x1 0.77 us: body(): return jnp.concatenate(totals, axis=0)]
    add x2 -> x0, other arithmetic: 0.9 us -> none  [body(): totals.append(part + lax.ppermute(part, 'samp', [(0, 1), (1, 0)]))]
    unnamed x15 -> x14, local copies, waits for them, and re-layouts: 1.49 us -> 2.08 us
  transfers between devices with their start and end apart: 6 -> 6, of which waited for: 2 -> 2; matrix products, arithmetic and copies ran while one was open for 3% -> 0% of each run, Pallas kernels for 24% -> 60%
where the time goes in v5:
time: 89.3 us; the launch traced here: 88.8 us
  Pallas kernels  64.2 us (72%)
  starting transfers between devices  15.2 us (17%)
  waiting for transfers between devices  7.32 us (8%)
  local copies, waits for them, and re-layouts  2.08 us (2%)
    pallas_call x1, Pallas kernels, main(): pl.pallas_call(functools.partial(main_kernel, layers, scale), grid=(count...  28.4 us
    pallas_call x1, Pallas kernels, mix_all(): pl.pallas_call(mix_kernel, grid=(panels, rows // each), in_specs=[part(la...  14.2 us
    pallas_call x1, Pallas kernels, halos(): pl.pallas_call(functools.partial(halo_kernel, tiles, layers, rows), out_s...  10.3 us
    pallas_call x1, Pallas kernels, pack(): pl.pallas_call(functools.partial(pack_kernel, tiles, blocks, layers, npat...  9.15 us
    ppermute x1, starting transfers between devices, body(): east = lax.ppermute(low, 'tile', [(j, i) for i, j in ring])  5.53 us
    ppermute x1, waiting for transfers between devices, body(): fixes = (fix, lax.ppermute(fix, 'samp', swap))  4.67 us
    ppermute x1, starting transfers between devices, body(): lax.ppermute(mm, 'tile', [(i, tiles - 1 - i) for i in range(tiles)])  4.02 us
    all_to_all x1, starting transfers between devices, body(): windows = lax.all_to_all(aa, 'tile', 0, 0, tiled=True)  3.55 us
  transfers between devices with their start and end apart: 6, of which 2 were waited for; matrix products, arithmetic and copies ran while one was open for 0% of the time, Pallas kernels for 60%

profile of v5, /device:TPU:0, one launch (start us, length us, event | category | flops | bytes accessed | tf_op | source)
XLA Modules:
  0.0 88.8 jit_solution(16115740084656789364)
XLA Ops:
  0.0 9.2 %pack.1 = (f32[6,40,128]{2,1,0:T(8,128)}, f32[6,2,40,512]{3,2,1,0:T(8,128)}, f32[6,2,40,512]{3,2,1,0:T(8,128)}, f32[3,40,128]{2,1,0:T(8,128)}, f32[16,48,128]{2,1,0:T(8,128)}) custom-call(f32[16,6,32,512]{3,2,1,0:T(8,128)} %refs_3_.1, f32[16,6,32,512]{3,2,1,0:T(8,128)} %refs_3_.1, f32[16,6,32,512]{3,2,1,0:T(8,128)} %refs_3_.1, f32[16,6,32,512]{3,2,1,0:T(8,128)} %refs_3_.1, ...), custom_call_target="tpu_custom_call" | custom-call | tf_op jit(solution)/shard_map/pack/pallas_call | solution.py:173
  9.2 0.1 collective-permute-start.1
  9.2 5.5 %collective-permute-start.2 = (f32[6,2,40,512]{3,2,1,0:T(8,128)}, f32[6,2,40,512]{3,2,1,0:T(8,128)S(1)}, u32[]{:S(2)}, u32[]{:S(2)}) collective-permute-start(f32[6,2,40,512]{3,2,1,0:T(8,128)} %get-tuple-element.20.low_ref), channel_id=1, source_target_pairs={{2,0},{4,2},{6,4},{8,6},{10,8},{12,10},{14,12},{16,14},{18,16},{20... | collective-permute-start | bytes 2949128 | tf_op jit(solution)/shard_map/ppermute | solution.py:741
  14.8 3.6 %all-to-all-start = ((f32[16,48,128]{2,1,0:T(8,128)}), f32[16,48,128]{2,1,0:T(8,128)S(1)}, u32[]{:S(2)}, u32[]{:S(2)}) async-start(f32[16,48,128]{2,1,0:T(8,128)} %get-tuple-element.23), calls=%async_computation | async-start | bytes 786432 | tf_op jit(solution)/shard_map/all_to_all | solution.py:743
  18.3 14.2 %mix.1 = (f32[6,32,16,512]{3,2,1,0:T(8,128)}, f32[6,32,16,512]{3,2,1,0:T(8,128)}, f32[6,32,16,512]{3,2,1,0:T(8,128)}, bf16[16,48]{1,0:T(8,128)(2,1)}, bf16[16,48]{1,0:T(8,128)(2,1)}, /*index=5*/bf16[16,8]{1,0:T(8,128)(2,1)}) custom-call(f32[16,6,32,512]{3,2,1,0:T(8,128)} %refs_3_.1, f32[16,6,32,512]{3,2,1,0:T(8,128)} %bitcast.5, ...), custom_call_target="tpu_custom_call" | custom-call | flops 301989888 | bytes 31457280 | tf_op jit(solution)/shard_map/mix/pallas_call | solution.py:281
  32.6 0.0 copy-start.6
  32.6 28.4 %main.1.refs_0_ = f32[6,32,512]{2,1,0:T(8,128)} custom-call(f32[6,32,16,512]{3,2,1,0:T(8,128)} %get-tuple-element.16.p_ref, f32[6,32,16,512]{3,2,1,0:T(8,128)} %get-tuple-element.17.v_ref, f32[6,32,16,512]{3,2,1,0:T(8,128)} %get-tuple-element.18.y_ref, f32[6,32,512]{2,1,0:T(8,128)} %refs_12_.1), custom_call_target="tpu_custom_call" | custom-call | flops 94371840 | bytes 25165824 | tf_op jit(solution)/shard_map/main/pallas_call | solution.py:683
  61.0 1.9 %collective-permute-start = (f32[6,32,512]{2,1,0:T(8,128)}, f32[6,32,512]{2,1,0:T(8,128)S(1)}, u32[]{:S(2)}, u32[]{:S(2)}) collective-permute-start(f32[6,32,512]{2,1,0:T(8,128)} %main.1.refs_0_), channel_id=1, source_target_pairs={{0,1},{1,0},{2,3},{3,2},{4,5},{5,4},{6,7},{7,6},{8,9},{9,8},{10,11... | collective-permute-start | bytes 1179656 | tf_op jit(solution)/shard_map/ppermute | solution.py:749
  62.9 0.0 copy-done.6
  62.9 4.0 %collective-permute-start.3 = (f32[3,40,128]{2,1,0:T(8,128)S(1)}, f32[3,40,128]{2,1,0:T(8,128)S(1)}, u32[]{:S(2)}, u32[]{:S(2)}) collective-permute-start(f32[3,40,128]{2,1,0:T(8,128)S(1)} %copy-done.6), channel_id=1, source_target_pairs={{0,30},{2,28},{4,26},{6,24},{8,22},{10,20},{12,18},{14,16},{16,14}... | collective-permute-start | bytes 184328 | tf_op jit(solution)/shard_map/ppermute | solution.py:742
  66.9 2.6 %collective-permute-done.3.mm_ref = f32[3,40,128]{2,1,0:T(8,128)S(1)} collective-permute-done((f32[3,40,128]{2,1,0:T(8,128)S(1)}, f32[3,40,128]{2,1,0:T(8,128)S(1)}, u32[]{:S(2)}, u32[]{:S(2)}) %collective-permute-start.3) | collective-permute-done | bytes 61472 | tf_op jit(solution)/shard_map/ppermute | solution.py:742
  69.5 0.0 copy-start.5
  69.5 0.0 all-to-all-done.aa_ref
  69.5 0.0 copy-start
  69.5 0.0 collective-permute-done.1.west_ref
  69.6 0.0 copy-start.1
  69.6 0.0 collective-permute-done.2.east_ref
  69.6 0.0 copy-start.2
  69.6 0.6 copy-done.5
  70.2 0.1 copy-done
  70.3 0.3 copy-done.1
  70.6 0.4 copy-done.2
  71.0 10.3 %halos.1.refs_2_ = f32[6,8,512]{2,1,0:T(8,128)} custom-call(f32[6,2,40,512]{3,2,1,0:T(8,128)} %copy-done.1, f32[6,2,40,512]{3,2,1,0:T(8,128)} %copy-done.2, f32[6,2,40,512]{3,2,1,0:T(8,128)} %get-tuple-element.20.low_ref, f32[6,2,40,512]{3,2,1,0:T(8,128)} %get-tuple-element.19.high_ref, f32[6,40,128]{2,1,0:T(8,128)} %get-tuple-element.21.em_ref, ...), custom_call_target="tpu_custom_call" | custom-call | flops 4915200 | bytes 3932160 | tf_op jit(solution)/shard_map/halos/pallas_call | solution.py:549
  81.3 0.2 collective-permute-start.4
  81.5 0.0 collective-permute-done.refs_1_
  81.5 0.0 copy-start.3
  81.5 4.7 %collective-permute-done.4.refs_3_ = f32[6,8,512]{2,1,0:T(8,128)S(1)} collective-permute-done((f32[6,8,512]{2,1,0:T(8,128)}, f32[6,8,512]{2,1,0:T(8,128)S(1)}, u32[]{:S(2)}, u32[]{:S(2)}) %collective-permute-start.4) | collective-permute-done | bytes 98336 | tf_op jit(solution)/shard_map/ppermute | solution.py:750
  86.2 0.0 copy-done.3
  86.2 0.0 copy-start.4
  86.2 0.6 copy-done.4
  86.8 2.0 %finish.1 = f32[6,32,512]{2,1,0:T(8,128)} custom-call(f32[6,32,512]{2,1,0:T(8,128)} %main.1.refs_0_, f32[6,32,512]{2,1,0:T(8,128)} %copy-done.3, f32[6,8,512]{2,1,0:T(8,128)} %halos.1.refs_2_, f32[6,8,512]{2,1,0:T(8,128)} %copy-done.4), custom_call_target="tpu_custom_call" | custom-call | tf_op jit(solution)/shard_map/finish/pallas_call | solution.py:727
Async XLA Ops:
  9.2 60.4 %collective-permute-start.1 = (f32[6,2,40,512]{3,2,1,0:T(8,128)}, f32[6,2,40,512]{3,2,1,0:T(8,128)S(1)}, u32[]{:S(2)}, u32[]{:S(2)}) collective-permute-start(f32[6,2,40,512]{3,2,1,0:T(8,128)} %get-tuple-element.19.high_ref), channel_id=1, source_target_pairs={{0,2},{2,4},{4,6},{6,8},{8,10},{10,12},{12,14},{14,16},{16,18},{18... | collective-permute-start | bytes 2949128 | tf_op jit(solution)/shard_map/ppermute | solution.py:740
  9.2 60.3 %collective-permute-start.2 = (f32[6,2,40,512]{3,2,1,0:T(8,128)}, f32[6,2,40,512]{3,2,1,0:T(8,128)S(1)}, u32[]{:S(2)}, u32[]{:S(2)}) collective-permute-start(f32[6,2,40,512]{3,2,1,0:T(8,128)} %get-tuple-element.20.low_ref), channel_id=1, source_target_pairs={{2,0},{4,2},{6,4},{8,6},{10,8},{12,10},{14,12},{16,14},{18,16},{20... | collective-permute-start | bytes 2949128 | tf_op jit(solution)/shard_map/ppermute | solution.py:741
  14.8 54.8 %all-to-all-start = ((f32[16,48,128]{2,1,0:T(8,128)}), f32[16,48,128]{2,1,0:T(8,128)S(1)}, u32[]{:S(2)}, u32[]{:S(2)}) async-start(f32[16,48,128]{2,1,0:T(8,128)} %get-tuple-element.23), calls=%async_computation | async-start | bytes 786432 | tf_op jit(solution)/shard_map/all_to_all | solution.py:743
  32.6 30.3 %copy-start.6 = (f32[3,40,128]{2,1,0:T(8,128)S(1)}, f32[3,40,128]{2,1,0:T(8,128)}, u32[]{:S(2)}) copy-start(f32[3,40,128]{2,1,0:T(8,128)} %get-tuple-element.22) | copy-start | bytes 184324
  61.0 20.5 %collective-permute-start = (f32[6,32,512]{2,1,0:T(8,128)}, f32[6,32,512]{2,1,0:T(8,128)S(1)}, u32[]{:S(2)}, u32[]{:S(2)}) collective-permute-start(f32[6,32,512]{2,1,0:T(8,128)} %main.1.refs_0_), channel_id=1, source_target_pairs={{0,1},{1,0},{2,3},{3,2},{4,5},{5,4},{6,7},{7,6},{8,9},{9,8},{10,11... | collective-permute-start | bytes 1179656 | tf_op jit(solution)/shard_map/ppermute | solution.py:749
  62.9 6.7 %collective-permute-start.3 = (f32[3,40,128]{2,1,0:T(8,128)S(1)}, f32[3,40,128]{2,1,0:T(8,128)S(1)}, u32[]{:S(2)}, u32[]{:S(2)}) collective-permute-start(f32[3,40,128]{2,1,0:T(8,128)S(1)} %copy-done.6), channel_id=1, source_target_pairs={{0,30},{2,28},{4,26},{6,24},{8,22},{10,20},{12,18},{14,16},{16,14}... | collective-permute-start | bytes 184328 | tf_op jit(solution)/shard_map/ppermute | solution.py:742
  69.5 0.6 copy-start.5
  69.5 0.8 copy-start
  69.6 1.1 %copy-start.1 = (f32[6,2,40,512]{3,2,1,0:T(8,128)}, f32[6,2,40,512]{3,2,1,0:T(8,128)S(1)}, u32[]{:S(2)}) copy-start(f32[6,2,40,512]{3,2,1,0:T(8,128)S(1)} %collective-permute-done.1.west_ref) | copy-start | bytes 2949124
  69.6 1.4 %copy-start.2 = (f32[6,2,40,512]{3,2,1,0:T(8,128)}, f32[6,2,40,512]{3,2,1,0:T(8,128)S(1)}, u32[]{:S(2)}) copy-start(f32[6,2,40,512]{3,2,1,0:T(8,128)S(1)} %collective-permute-done.2.east_ref) | copy-start | bytes 2949124
  81.3 4.8 %collective-permute-start.4 = (f32[6,8,512]{2,1,0:T(8,128)}, f32[6,8,512]{2,1,0:T(8,128)S(1)}, u32[]{:S(2)}, u32[]{:S(2)}) collective-permute-start(f32[6,8,512]{2,1,0:T(8,128)} %halos.1.refs_2_), channel_id=1, source_target_pairs={{0,1},{1,0},{2,3},{3,2},{4,5},{5,4},{6,7},{7,6},{8,9},{9,8},{10,11... | collective-permute-start | bytes 294920 | tf_op jit(solution)/shard_map/ppermute | solution.py:750
  81.5 4.7 %copy-start.3 = (f32[6,32,512]{2,1,0:T(8,128)}, f32[6,32,512]{2,1,0:T(8,128)S(1)}, u32[]{:S(2)}) copy-start(f32[6,32,512]{2,1,0:T(8,128)S(1)} %collective-permute-done.refs_1_) | copy-start | bytes 1179652
  86.2 0.6 copy-start.4

commit v6 on v5

--- a/solution.py
+++ b/solution.py
@@ -195,9 +195,9 @@
     )(*[s] * blocks, *[w] * blocks, *[pat] * blocks, b)
 
 
-def mix_kernel(
+def mix_panel(
     s_ref, w_ref, pat_ref, mat_ref, index_ref,
-    p_ref, v_ref, y_ref, fwd_ref, bwd_ref, sel_ref,
+    sp, sv, ty, fwd_ref, bwd_ref, sel_ref,
     left_s, left_w, left_f, pf,
 ):
     layers, n = s_ref.shape[0], s_ref.shape[3]
@@ -243,8 +243,7 @@
         sel_ref[...] = product(eye, chosen, True)
         return carry
 
-    start = (pl.program_id(0) == 0) & (pl.program_id(1) == 0)
-    lax.fori_loop(0, jnp.where(start, 1, 0), matrices, 0)
+    lax.fori_loop(0, jnp.where(pl.program_id(0) == 0, 1, 0), matrices, 0)
 
     pf[...] = jnp.zeros(pf.shape, F32)
     pf[0:npat] = pat_ref[:, 0].astype(F32)
@@ -263,39 +262,10 @@
             cut = slice(at, at + step)
             x = dot(left_s[...], pieces(s_ref[:, 0, own, cut].reshape(size, step)))
             f = dot(left_f[...], pf[:, own, cut].reshape(64, step).astype(jnp.bfloat16))
-            p_ref[0, own, :, cut] = (x[0:size] + x[size : 2 * size]).reshape(8, layers, step)
-            y_ref[0, own, :, cut] = (x[2 * size :] + f).reshape(8, layers, step)
+            sp[2 + 8 * g : 10 + 8 * g, :, cut] = (x[0:size] + x[size : 2 * size]).reshape(8, layers, step)
+            ty[own, :, cut] = (x[2 * size :] + f).reshape(8, layers, step)
             x = dot(left_w[...], pieces(w_ref[:, 0, own, cut].reshape(size, step)))
-            v_ref[0, own, :, cut] = (x[0:size] + x[size:]).reshape(8, layers, step)
-
-
-def mix_all(s, w, pat, matrix, index):
-    layers, panels, rows, n = s.shape
-    npat, each = pat.shape[0], rows
-    full = lambda *shape: pl.BlockSpec(shape, lambda p, g: (0, 0))
-    part = lambda count: pl.BlockSpec((count, 1, each, n), lambda p, g: (0, p, g, 0))
-    out = pl.BlockSpec((1, each, layers, n), lambda p, g: (p, g, 0, 0))
-    size = layers * panels * rows * n * 4
-    wide = 8 * layers
-    small = [(layers, 3 * layers), (layers, 3 * layers), (layers, 8)]
-    *fields, fwd, bwd, sel = pl.pallas_call(
-        mix_kernel,
-        grid=(panels, rows // each),
-        in_specs=[part(layers), part(layers), part(npat), full(layers, layers), full(1, layers)],
-        out_specs=[out] * 3 + [full(*x) for x in small],
-        out_shape=[jax.ShapeDtypeStruct((panels, rows, layers, n), F32)] * 3
-        + [jax.ShapeDtypeStruct(x, jnp.bfloat16) for x in small],
-        scratch_shapes=[
-            pltpu.VMEM((3 * wide, 2 * wide), jnp.bfloat16),
-            pltpu.VMEM((2 * wide, 2 * wide), jnp.bfloat16),
-            pltpu.VMEM((wide, 64), jnp.bfloat16),
-            pltpu.VMEM((8, each, n), F32),
-        ],
-        compiler_params=pltpu.CompilerParams(vmem_limit_bytes=VMEM),
-        cost_estimate=pl.CostEstimate(flops=size * 48, bytes_accessed=5 * size, transcendentals=0),
-        name="mix",
-    )(s, w, pat, matrix, index)
-    return fields, fwd, bwd, sel
+            sv[2 + 8 * g : 10 + 8 * g, :, cut] = (x[0:size] + x[size:]).reshape(8, layers, step)
 
 
 def halo_kernel(
@@ -562,12 +532,15 @@
 
 
 def main_kernel(
-    layers, scale,
-    p_ref, v_ref, y_ref, b_ref,
-    g_ref,
-    sp, sv, sy, sz, ip, iv, jp, jv, depth, bi, bj, acc,
+    scale,
+    s_ref, w_ref, pat_ref, mat_ref, index_ref, b_ref,
+    g_ref, fwd_ref, bwd_ref, sel_ref,
+    left_s, left_w, left_f, pf, ty, sp, sv, sy, sz, ip, iv, jp, jv, depth, bi, bj, acc,
 ):
-    rows, n = p_ref.shape[1], p_ref.shape[3]
+    layers, rows, n = s_ref.shape[0], s_ref.shape[2], s_ref.shape[3]
+    mix_panel(
+        s_ref, w_ref, pat_ref, mat_ref, index_ref, sp, sv, ty, fwd_ref, bwd_ref, sel_ref, left_s, left_w, left_f, pf
+    )
     halves = layers // 8
 
     def shift_next(x):
@@ -593,11 +566,9 @@
     def spread(ref, at):
         return jnp.concatenate([ref[c, pl.ds(at, 8, stride=0), :] for c in range(len(parts))], axis=1)
 
-    for src, dst in ((p_ref, sp), (v_ref, sv)):
+    for dst in (sp, sv):
         for slot in (1, rows + 2):
             dst[slot] = jnp.zeros((layers, n), F32)
-        for r in range(rows):
-            dst[r + 2] = src[0, r]
 
     def lap(ref, at, bases, outs, by_i, by_j, count):
         for h in range(halves):
@@ -626,7 +597,7 @@
         r = i * group
 
         def own_y(u, part):
-            return y_ref[0, r + u, part, :]
+            return ty[r + u, part]
 
         lap(sp, r + 2, own_y, sy, ip, jp, group)
         lap(sv, r + 2, None, sz, iv, jv, group)
@@ -675,37 +646,42 @@
     g_ref[0] = (-0.5 * STEP_FACTOR * STEP_FACTOR * scale) * total
 
 
-def main(scale, fields, depth):
-    count, rows, layers, n = fields[0].shape
-    wide = n
-    block = lambda x: pl.BlockSpec((1,) + x.shape[1:], lambda p: (p,) + (0,) * (x.ndim - 1))
-    operands = [*fields, depth]
+def main(scale, s, w, pat, matrix, index, depth):
+    layers, panels, rows, n = s.shape
+    npat, size = pat.shape[0], 8 * layers
+    part = lambda count: pl.BlockSpec((count, 1, rows, n), lambda p: (0, p, 0, 0))
+    full = lambda *shape: pl.BlockSpec(shape, lambda p: (0, 0))
+    plane = pl.BlockSpec((1, rows, n), lambda p: (p, 0, 0))
+    small = [(layers, 3 * layers), (layers, 3 * layers), (layers, 8)]
+    field = lambda count: pltpu.VMEM((count, layers, n), F32)
     return pl.pallas_call(
-        functools.partial(main_kernel, layers, scale),
-        grid=(count,),
-        in_specs=[block(x) for x in operands],
-        out_specs=pl.BlockSpec((1, rows, n), lambda p: (p, 0, 0)),
-        out_shape=jax.ShapeDtypeStruct((count, rows, n), F32),
+        functools.partial(main_kernel, scale),
+        grid=(panels,),
+        in_specs=[part(layers), part(layers), part(npat), full(layers, layers), full(1, layers), plane],
+        out_specs=[plane] + [full(*x) for x in small],
+        out_shape=[jax.ShapeDtypeStruct((panels, rows, n), F32)]
+        + [jax.ShapeDtypeStruct(x, jnp.bfloat16) for x in small],
         scratch_shapes=[
-            pltpu.VMEM((rows + 4, layers, wide), F32),
-            pltpu.VMEM((rows + 4, layers, wide), F32),
-            pltpu.VMEM((rows + 2, layers, wide), F32),
-            pltpu.VMEM((rows + 2, layers, wide), F32),
-            pltpu.VMEM((rows + 1, layers, n), F32),
-            pltpu.VMEM((rows + 1, layers, n), F32),
-            pltpu.VMEM((rows, layers, wide), F32),
-            pltpu.VMEM((rows, layers, wide), F32),
-            pltpu.VMEM((rows + 24, wide), F32),
-            pltpu.VMEM((wide // LANES, rows + 16, LANES), F32),
-            pltpu.VMEM((wide // LANES, rows + 16, LANES), F32),
+            pltpu.VMEM((3 * size, 2 * size), jnp.bfloat16),
+            pltpu.VMEM((2 * size, 2 * size), jnp.bfloat16),
+            pltpu.VMEM((size, 64), jnp.bfloat16),
+            pltpu.VMEM((8, rows, n), F32),
+            field(rows),
+            field(rows + 4), field(rows + 4),
+            field(rows + 2), field(rows + 2),
+            field(rows + 1), field(rows + 1),
+            field(rows), field(rows),
+            pltpu.VMEM((rows + 24, n), F32),
+            pltpu.VMEM((n // LANES, rows + 16, LANES), F32),
+            pltpu.VMEM((n // LANES, rows + 16, LANES), F32),
             pltpu.VMEM((rows, 8, n), F32),
         ],
         compiler_params=pltpu.CompilerParams(vmem_limit_bytes=VMEM),
         cost_estimate=pl.CostEstimate(
-            flops=count * rows * layers * wide * 60, bytes_accessed=count * rows * layers * n * 16, transcendentals=0
+            flops=panels * rows * layers * n * 120, bytes_accessed=panels * rows * layers * n * 10, transcendentals=0
         ),
         name="main",
-    )(*operands)
+    )(s, w, pat, matrix, index, depth)
 
 
 def finish_kernel(scale, *refs):
@@ -741,8 +717,7 @@
     east = lax.ppermute(low, "tile", [(j, i) for i, j in ring])
     mirrored = lax.ppermute(mm, "tile", [(i, tiles - 1 - i) for i in range(tiles)])
     windows = lax.all_to_all(aa, "tile", 0, 0, tiled=True)
-    fields, fwd, bwd, sel = mix_all(initial_state, weights, patterns, coupling, pattern_index)
-    total = main(1.0 / samples, fields, bathymetry)
+    total, fwd, bwd, sel = main(1.0 / samples, initial_state, weights, patterns, coupling, pattern_index, bathymetry)
     fix = halos(tiles, layers, rows, west, east, low, high, em, mirrored, windows, fwd, bwd, sel)
     if samples == 2:
         swap = [(0, 1), (1, 0)]

time: 89.3 us -> 79.7 us (0.89)
  Pallas kernels: 64.2 us -> 54.8 us
    pallas_call x2 -> x1, Pallas kernels: 42.7 us -> 33.2 us  [main(): pl.pallas_call(functools.partial(main_kernel, scale), grid=(panels,), in_...]
  transfers between devices with their start and end apart: 6 -> 6, of which waited for: 2 -> 2; matrix products, arithmetic and copies ran while one was open for 0% -> 0% of each run, Pallas kernels for 60% -> 55%
where the time goes in v6:
time: 79.7 us; the launch traced here: 79.4 us
  Pallas kernels  54.8 us (69%)
  starting transfers between devices  15.2 us (19%)
  waiting for transfers between devices  7.31 us (9%)
  local copies, waits for them, and re-layouts  2.04 us (3%)
    pallas_call x1, Pallas kernels, main(): pl.pallas_call(functools.partial(main_kernel, scale), grid=(panels,), in_...  33.2 us
    pallas_call x1, Pallas kernels, halos(): pl.pallas_call(functools.partial(halo_kernel, tiles, layers, rows), out_s...  10.3 us
    pallas_call x1, Pallas kernels, pack(): pl.pallas_call(functools.partial(pack_kernel, tiles, blocks, layers, npat...  9.15 us
    ppermute x1, starting transfers between devices, body(): east = lax.ppermute(low, 'tile', [(j, i) for i, j in ring])  5.53 us
    ppermute x1, waiting for transfers between devices, body(): fixes = (fix, lax.ppermute(fix, 'samp', swap))  4.67 us
    ppermute x1, starting transfers between devices, body(): lax.ppermute(mm, 'tile', [(i, tiles - 1 - i) for i in range(tiles)])  4.03 us
    all_to_all x1, starting transfers between devices, body(): windows = lax.all_to_all(aa, 'tile', 0, 0, tiled=True)  3.55 us
    ppermute x1, waiting for transfers between devices, body(): lax.ppermute(mm, 'tile', [(i, tiles - 1 - i) for i in range(tiles)])  2.62 us
  transfers between devices with their start and end apart: 6, of which 2 were waited for; matrix products, arithmetic and copies ran while one was open for 0% of the time, Pallas kernels for 55%

profile of v6, /device:TPU:0, one launch (start us, length us, event | category | flops | bytes accessed | tf_op | source)
XLA Modules:
  0.0 79.4 jit_solution(1823562937977279110)
XLA Ops:
  0.0 9.2 %pack.1 = (f32[6,40,128]{2,1,0:T(8,128)}, f32[6,2,40,512]{3,2,1,0:T(8,128)}, f32[6,2,40,512]{3,2,1,0:T(8,128)}, f32[3,40,128]{2,1,0:T(8,128)}, f32[16,48,128]{2,1,0:T(8,128)}) custom-call(f32[16,6,32,512]{3,2,1,0:T(8,128)} %refs_3_.1, f32[16,6,32,512]{3,2,1,0:T(8,128)} %refs_3_.1, f32[16,6,32,512]{3,2,1,0:T(8,128)} %refs_3_.1, f32[16,6,32,512]{3,2,1,0:T(8,128)} %refs_3_.1, ...), custom_call_target="tpu_custom_call" | custom-call | tf_op jit(solution)/shard_map/pack/pallas_call | solution.py:173
  9.2 0.1 collective-permute-start.1
  9.2 5.5 %collective-permute-start.2 = (f32[6,2,40,512]{3,2,1,0:T(8,128)}, f32[6,2,40,512]{3,2,1,0:T(8,128)S(1)}, u32[]{:S(2)}, u32[]{:S(2)}) collective-permute-start(f32[6,2,40,512]{3,2,1,0:T(8,128)} %get-tuple-element.16.low_ref), channel_id=1, source_target_pairs={{2,0},{4,2},{6,4},{8,6},{10,8},{12,10},{14,12},{16,14},{18,16},{20... | collective-permute-start | bytes 2949128 | tf_op jit(solution)/shard_map/ppermute | solution.py:717
  14.8 3.6 %all-to-all-start = ((f32[16,48,128]{2,1,0:T(8,128)}), f32[16,48,128]{2,1,0:T(8,128)S(1)}, u32[]{:S(2)}, u32[]{:S(2)}) async-start(f32[16,48,128]{2,1,0:T(8,128)} %get-tuple-element.19), calls=%async_computation | async-start | bytes 786432 | tf_op jit(solution)/shard_map/all_to_all | solution.py:719
  18.3 0.0 copy-start.6
  18.3 33.2 %main.1 = (f32[6,32,512]{2,1,0:T(8,128)}, bf16[16,48]{1,0:T(8,128)(2,1)}, bf16[16,48]{1,0:T(8,128)(2,1)}, bf16[16,8]{1,0:T(8,128)(2,1)}) custom-call(f32[16,6,32,512]{3,2,1,0:T(8,128)} %refs_3_.1, f32[16,6,32,512]{3,2,1,0:T(8,128)} %bitcast.5, bf16[4,6,32,512]{3,2,1,0:T(8,128)(2,1)} %refs_11_.1, f32[16,16]{1,0:T(8,128)} %mat_ref.1, s32[1,16]{1,0:T(1,128)} %index_ref.1, ...), custom_call_target="tpu_custom_call" | custom-call | flops 188743680 | bytes 15728640 | tf_op jit(solution)/shard_map/main/pallas_call | solution.py:657
  51.6 1.9 %collective-permute-start = (f32[6,32,512]{2,1,0:T(8,128)}, f32[6,32,512]{2,1,0:T(8,128)S(1)}, u32[]{:S(2)}, u32[]{:S(2)}) collective-permute-start(f32[6,32,512]{2,1,0:T(8,128)} %get-tuple-element.14.refs_0_), channel_id=1, source_target_pairs={{0,1},{1,0},{2,3},{3,2},{4,5},{5,4},{6,7},{7,6},{8,9},{9,8},{10,11... | collective-permute-start | bytes 1179656 | tf_op jit(solution)/shard_map/ppermute | solution.py:724
  53.4 0.0 copy-done.6
  53.4 4.0 %collective-permute-start.3 = (f32[3,40,128]{2,1,0:T(8,128)S(1)}, f32[3,40,128]{2,1,0:T(8,128)S(1)}, u32[]{:S(2)}, u32[]{:S(2)}) collective-permute-start(f32[3,40,128]{2,1,0:T(8,128)S(1)} %copy-done.6), channel_id=1, source_target_pairs={{0,30},{2,28},{4,26},{6,24},{8,22},{10,20},{12,18},{14,16},{16,14}... | collective-permute-start | bytes 184328 | tf_op jit(solution)/shard_map/ppermute | solution.py:718
  57.5 2.6 %collective-permute-done.3.mm_ref = f32[3,40,128]{2,1,0:T(8,128)S(1)} collective-permute-done((f32[3,40,128]{2,1,0:T(8,128)S(1)}, f32[3,40,128]{2,1,0:T(8,128)S(1)}, u32[]{:S(2)}, u32[]{:S(2)}) %collective-permute-start.3) | collective-permute-done | bytes 61472 | tf_op jit(solution)/shard_map/ppermute | solution.py:718
  60.1 0.0 copy-start.5
  60.1 0.0 all-to-all-done.aa_ref
  60.1 0.0 copy-start
  60.1 0.0 collective-permute-done.1.west_ref
  60.1 0.0 copy-start.1
  60.1 0.0 collective-permute-done.2.east_ref
  60.1 0.0 copy-start.2
  60.1 0.6 copy-done.5
  60.7 0.1 copy-done
  60.9 0.4 copy-done.1
  61.2 0.3 copy-done.2
  61.5 10.3 %halos.1.refs_2_ = f32[6,8,512]{2,1,0:T(8,128)} custom-call(f32[6,2,40,512]{3,2,1,0:T(8,128)} %copy-done.1, f32[6,2,40,512]{3,2,1,0:T(8,128)} %copy-done.2, f32[6,2,40,512]{3,2,1,0:T(8,128)} %get-tuple-element.16.low_ref, f32[6,2,40,512]{3,2,1,0:T(8,128)} %get-tuple-element.15.high_ref, f32[6,40,128]{2,1,0:T(8,128)} %get-tuple-element.17.em_ref, ...), custom_call_target="tpu_custom_call" | custom-call | flops 4915200 | bytes 3932160 | tf_op jit(solution)/shard_map/halos/pallas_call | solution.py:519
  71.9 0.1 collective-permute-start.4
  72.0 0.0 collective-permute-done.refs_1_
  72.0 0.0 copy-start.3
  72.0 4.7 %collective-permute-done.4.refs_3_ = f32[6,8,512]{2,1,0:T(8,128)S(1)} collective-permute-done((f32[6,8,512]{2,1,0:T(8,128)}, f32[6,8,512]{2,1,0:T(8,128)S(1)}, u32[]{:S(2)}, u32[]{:S(2)}) %collective-permute-start.4) | collective-permute-done | bytes 98336 | tf_op jit(solution)/shard_map/ppermute | solution.py:725
  76.7 0.0 copy-done.3
  76.7 0.0 copy-start.4
  76.7 0.6 copy-done.4
  77.3 2.0 %finish.1 = f32[6,32,512]{2,1,0:T(8,128)} custom-call(f32[6,32,512]{2,1,0:T(8,128)} %get-tuple-element.14.refs_0_, f32[6,32,512]{2,1,0:T(8,128)} %copy-done.3, f32[6,8,512]{2,1,0:T(8,128)} %halos.1.refs_2_, f32[6,8,512]{2,1,0:T(8,128)} %copy-done.4), custom_call_target="tpu_custom_call" | custom-call | tf_op jit(solution)/shard_map/finish/pallas_call | solution.py:703
Async XLA Ops:
  9.2 51.0 %collective-permute-start.1 = (f32[6,2,40,512]{3,2,1,0:T(8,128)}, f32[6,2,40,512]{3,2,1,0:T(8,128)S(1)}, u32[]{:S(2)}, u32[]{:S(2)}) collective-permute-start(f32[6,2,40,512]{3,2,1,0:T(8,128)} %get-tuple-element.15.high_ref), channel_id=1, source_target_pairs={{0,2},{2,4},{4,6},{6,8},{8,10},{10,12},{12,14},{14,16},{16,18},{18... | collective-permute-start | bytes 2949128 | tf_op jit(solution)/shard_map/ppermute | solution.py:716
  9.2 50.9 %collective-permute-start.2 = (f32[6,2,40,512]{3,2,1,0:T(8,128)}, f32[6,2,40,512]{3,2,1,0:T(8,128)S(1)}, u32[]{:S(2)}, u32[]{:S(2)}) collective-permute-start(f32[6,2,40,512]{3,2,1,0:T(8,128)} %get-tuple-element.16.low_ref), channel_id=1, source_target_pairs={{2,0},{4,2},{6,4},{8,6},{10,8},{12,10},{14,12},{16,14},{18,16},{20... | collective-permute-start | bytes 2949128 | tf_op jit(solution)/shard_map/ppermute | solution.py:717
  14.8 45.4 %all-to-all-start = ((f32[16,48,128]{2,1,0:T(8,128)}), f32[16,48,128]{2,1,0:T(8,128)S(1)}, u32[]{:S(2)}, u32[]{:S(2)}) async-start(f32[16,48,128]{2,1,0:T(8,128)} %get-tuple-element.19), calls=%async_computation | async-start | bytes 786432 | tf_op jit(solution)/shard_map/all_to_all | solution.py:719
  18.3 35.1 %copy-start.6 = (f32[3,40,128]{2,1,0:T(8,128)S(1)}, f32[3,40,128]{2,1,0:T(8,128)}, u32[]{:S(2)}) copy-start(f32[3,40,128]{2,1,0:T(8,128)} %get-tuple-element.18) | copy-start | bytes 184324
  51.6 20.4 %collective-permute-start = (f32[6,32,512]{2,1,0:T(8,128)}, f32[6,32,512]{2,1,0:T(8,128)S(1)}, u32[]{:S(2)}, u32[]{:S(2)}) collective-permute-start(f32[6,32,512]{2,1,0:T(8,128)} %get-tuple-element.14.refs_0_), channel_id=1, source_target_pairs={{0,1},{1,0},{2,3},{3,2},{4,5},{5,4},{6,7},{7,6},{8,9},{9,8},{10,11... | collective-permute-start | bytes 1179656 | tf_op jit(solution)/shard_map/ppermute | solution.py:724
  53.4 6.7 %collective-permute-start.3 = (f32[3,40,128]{2,1,0:T(8,128)S(1)}, f32[3,40,128]{2,1,0:T(8,128)S(1)}, u32[]{:S(2)}, u32[]{:S(2)}) collective-permute-start(f32[3,40,128]{2,1,0:T(8,128)S(1)} %copy-done.6), channel_id=1, source_target_pairs={{0,30},{2,28},{4,26},{6,24},{8,22},{10,20},{12,18},{14,16},{16,14}... | collective-permute-start | bytes 184328 | tf_op jit(solution)/shard_map/ppermute | solution.py:718
  60.1 0.6 copy-start.5
  60.1 0.8 copy-start
  60.1 1.1 %copy-start.1 = (f32[6,2,40,512]{3,2,1,0:T(8,128)}, f32[6,2,40,512]{3,2,1,0:T(8,128)S(1)}, u32[]{:S(2)}) copy-start(f32[6,2,40,512]{3,2,1,0:T(8,128)S(1)} %collective-permute-done.1.west_ref) | copy-start | bytes 2949124
  60.1 1.4 %copy-start.2 = (f32[6,2,40,512]{3,2,1,0:T(8,128)}, f32[6,2,40,512]{3,2,1,0:T(8,128)S(1)}, u32[]{:S(2)}) copy-start(f32[6,2,40,512]{3,2,1,0:T(8,128)S(1)} %collective-permute-done.2.east_ref) | copy-start | bytes 2949124
  71.9 4.8 %collective-permute-start.4 = (f32[6,8,512]{2,1,0:T(8,128)}, f32[6,8,512]{2,1,0:T(8,128)S(1)}, u32[]{:S(2)}, u32[]{:S(2)}) collective-permute-start(f32[6,8,512]{2,1,0:T(8,128)} %halos.1.refs_2_), channel_id=1, source_target_pairs={{0,1},{1,0},{2,3},{3,2},{4,5},{5,4},{6,7},{7,6},{8,9},{9,8},{10,11... | collective-permute-start | bytes 294920 | tf_op jit(solution)/shard_map/ppermute | solution.py:725
  72.0 4.7 %copy-start.3 = (f32[6,32,512]{2,1,0:T(8,128)}, f32[6,32,512]{2,1,0:T(8,128)S(1)}, u32[]{:S(2)}) copy-start(f32[6,32,512]{2,1,0:T(8,128)S(1)} %collective-permute-done.refs_1_) | copy-start | bytes 1179652
  76.7 0.6 copy-start.4
